TPU v7x, 32 devices: a whole 2x2x4 slice. The times are simulated.
32 devices in a mesh: au: 4 (over x, core), row: 8 (over z, y).
Axes of the slice: x: 2, y: 2, z: 4, core: 2. Of those that a mesh axis runs over, the one named last changes fastest.
Arguments:
- tokens: bfloat16 [4096, 768], P(('au', 'row')), may hold values from -6 to 6
- cotangent: bfloat16 [4096, 768], P(('au', 'row')), may hold values from -6 to 6
- doc_lengths: int32 [16], replicated, may hold values from 1 to 2048, 4096 in all
- query_weight: float32 [768, 768], P(('au', 'row')), may hold values from -0.21875 to 0.21875
- query_bias: float32 [768], P(('au', 'row')), may hold values from -3 to 3
- key_weight: float32 [768, 768], P(('au', 'row')), may hold values from -0.21875 to 0.21875
- value_weight: float32 [768, 768], P(('au', 'row')), may hold values from -0.21875 to 0.21875
- value_bias: float32 [768], P(('au', 'row')), may hold values from -0.3125 to 0.3125
- mix_weight: float32 [768, 768], P(('au', 'row')), may hold values from -1.75 to 1.75
- mix_bias: float32 [768], P(('au', 'row')), may hold values from -1.5 to 1.5
- early_gain: float32 [768], P(('au', 'row')), may hold values from 0.5 to 1.5
- early_shift: float32 [768], P(('au', 'row')), may hold values from -1.5 to 1.5
- inner_weight: float32 [768, 3072], P(('au', 'row')), may hold values from -0.21875 to 0.21875
- inner_bias: float32 [3072], P(('au', 'row')), may hold values from -1.5 to 1.5
- outer_weight: float32 [3072, 768], P(('au', 'row')), may hold values from -0.109375 to 0.109375
- outer_bias: float32 [768], P(('au', 'row')), may hold values from -1.5 to 1.5
- final_gain: float32 [768], P(('au', 'row')), may hold values from 0.5 to 1.5
- final_shift: float32 [768], P(('au', 'row')), may hold values from -1.5 to 1.5
Outputs:
- output: bfloat16 [4096, 768], P(('au', 'row'))
- input_grad: bfloat16 [4096, 768], P(('au', 'row'))
- query_weight_grad: float32 [768, 768], P(('au', 'row'))
- query_bias_grad: float32 [768], P(('au', 'row'))
- key_weight_grad: float32 [768, 768], P(('au', 'row'))
- value_weight_grad: float32 [768, 768], P(('au', 'row'))
- value_bias_grad: float32 [768], P(('au', 'row'))
- mix_weight_grad: float32 [768, 768], P(('au', 'row'))
- mix_bias_grad: float32 [768], P(('au', 'row'))
- early_gain_grad: float32 [768], P(('au', 'row'))
- early_shift_grad: float32 [768], P(('au', 'row'))
- inner_weight_grad: float32 [768, 3072], P(('au', 'row'))
- inner_bias_grad: float32 [3072], P(('au', 'row'))
- outer_weight_grad: float32 [3072, 768], P(('au', 'row'))
- outer_bias_grad: float32 [768], P(('au', 'row'))
- final_gain_grad: float32 [768], P(('au', 'row'))
- final_shift_grad: float32 [768], P(('au', 'row'))
Inputs may be any that keep to these rules, and one draw needn't show every extreme that they name: `doc_lengths`: the documents lie one after another and fill the sequence: the lengths add up to 4096, and the longest is exactly 2048.
All inputs are finite; a program needn't handle non-finite values.
Results may differ from a plain program's by a relative error of at most 0.017.
Values may be sent and summed in bfloat16 or wider, within the bound.
A program may use at most 192 MiB of HBM per device.

v0:
```python
import jax
import jax.numpy as jnp
from jax import lax
from jax.sharding import PartitionSpec as P

HEADS = 12
HEAD = 64


eps_norm = 1e-06
mask_fill = -1000000000.0
lowest_start = -1e30


def layer_norm(hidden, gain, shift):
    mean = jnp.mean(hidden, axis=-1, keepdims=True)
    centered = hidden - mean
    spread = jnp.mean(centered * centered, axis=-1, keepdims=True)
    return centered * lax.rsqrt(spread + eps_norm) * gain + shift


def gelu_exact(values):
    return jax.nn.gelu(values, approximate=False)


def block_size():
    return 512


def over_blocks(carry, pieces, step):
    count = pieces[0].shape[0]
    size = block_size()

    def advance(state, turn):
        begin = turn * size
        sliced = tuple((lax.dynamic_slice_in_dim(piece, begin, size, 0) for piece in pieces))
        return (step(state, sliced, begin), None)

    result, unused = lax.scan(advance, carry, jnp.arange(count // size, dtype=jnp.int32))
    return result


def token_places(first, count, local_rows, cycle, rows):
    index = first + jnp.arange(count, dtype=jnp.int32)
    owner = index // local_rows
    within = index % local_rows
    return within // rows * (cycle * rows) + owner * rows + within % rows


def segment_of(places, starts):
    return jnp.sum((starts[None, :] <= places[:, None]).astype(jnp.int32), axis=1) - 1


def on_device(
    tokens,
    cotangent,
    doc_lengths,
    query_weight,
    query_bias,
    key_weight,
    value_weight,
    value_bias,
    mix_weight,
    mix_bias,
    early_gain,
    early_shift,
    inner_weight,
    inner_bias,
    outer_weight,
    outer_bias,
    final_gain,
    final_shift,
):
    low_type = jnp.bfloat16
    wide = jnp.float32
    full = (
        lax.all_gather(query_weight.astype(low_type), ("au", "row"), axis=0, tiled=True),
        lax.all_gather(query_bias.astype(low_type), ("au", "row"), axis=0, tiled=True),
        lax.all_gather(key_weight.astype(low_type), ("au", "row"), axis=0, tiled=True),
        lax.all_gather(value_weight.astype(low_type), ("au", "row"), axis=0, tiled=True),
        lax.all_gather(value_bias.astype(low_type), ("au", "row"), axis=0, tiled=True),
        lax.all_gather(mix_weight.astype(low_type), ("au", "row"), axis=0, tiled=True),
        lax.all_gather(mix_bias.astype(low_type), ("au", "row"), axis=0, tiled=True),
        lax.all_gather(early_gain.astype(low_type), ("au", "row"), axis=0, tiled=True),
        lax.all_gather(early_shift.astype(low_type), ("au", "row"), axis=0, tiled=True),
        lax.all_gather(inner_weight.astype(low_type), ("au", "row"), axis=0, tiled=True),
        lax.all_gather(inner_bias.astype(low_type), ("au", "row"), axis=0, tiled=True),
        lax.all_gather(outer_weight.astype(low_type), ("au", "row"), axis=0, tiled=True),
        lax.all_gather(outer_bias.astype(low_type), ("au", "row"), axis=0, tiled=True),
        lax.all_gather(final_gain.astype(low_type), ("au", "row"), axis=0, tiled=True),
        lax.all_gather(final_shift.astype(low_type), ("au", "row"), axis=0, tiled=True),
    )
    rows = tokens.shape[0]
    groups = lax.axis_size("au")
    cycle = lax.axis_size("row")
    local_heads = HEADS // groups
    local_rows = groups * rows
    width = local_heads * HEAD
    scale = HEAD ** (-0.5)
    starts = jnp.cumsum(doc_lengths) - doc_lengths
    queries_tok = (
        jnp.dot(tokens, full[0], preferred_element_type=wide) + full[1].astype(wide)
    ).astype(low_type)
    keys_tok = jnp.dot(tokens, full[2], preferred_element_type=wide).astype(low_type)
    values_tok = (
        jnp.dot(tokens, full[3], preferred_element_type=wide) + full[4].astype(wide)
    ).astype(low_type)
    queries, keys, values = (
        lax.all_to_all(queries_tok, "au", split_axis=1, concat_axis=0, tiled=True),
        lax.all_to_all(keys_tok, "au", split_axis=1, concat_axis=0, tiled=True),
        lax.all_to_all(values_tok, "au", split_axis=1, concat_axis=0, tiled=True),
    )
    queries = queries.reshape(local_rows, local_heads, HEAD)
    keys = keys.reshape(local_rows, local_heads, HEAD)
    values = values.reshape(local_rows, local_heads, HEAD)
    own_first = lax.axis_index("row") * local_rows
    own_segment = segment_of(token_places(own_first, local_rows, local_rows, cycle, rows), starts)

    def forward_step(carry, pieces, first):
        top, total, weighted = carry
        key_piece, value_piece = pieces
        count = key_piece.shape[0]
        piece_segment = segment_of(token_places(first, count, local_rows, cycle, rows), starts)
        scores = jnp.einsum("qhd,khd->qhk", queries, key_piece, preferred_element_type=wide) * scale
        same = own_segment[:, None] == piece_segment[None, :]
        scores = jnp.where(same[:, None, :], scores, mask_fill)
        new_top = jnp.maximum(top, jnp.max(scores, axis=-1))
        factor = jnp.exp(top - new_top)
        powers = jnp.exp(scores - new_top[:, :, None])
        total = total * factor + jnp.sum(powers, axis=-1)
        weighted = weighted * factor[:, :, None] + jnp.einsum(
            "qhk,khd->qhd", powers.astype(low_type), value_piece, preferred_element_type=wide
        )
        return (new_top, total, weighted)

    start_state = (
        jnp.full((local_rows, local_heads), lowest_start, wide),
        jnp.zeros((local_rows, local_heads), wide),
        jnp.zeros((local_rows, local_heads, HEAD), wide),
    )
    top, total, weighted = over_blocks(
        start_state,
        (
            lax.all_gather(keys, "row", axis=0, tiled=True),
            lax.all_gather(values, "row", axis=0, tiled=True),
        ),
        forward_step,
    )
    mixed = weighted / total[:, :, None]
    log_total = top + jnp.log(total)
    mixed_heads = mixed.astype(low_type).reshape(local_rows, width)
    mixed_tok = lax.all_to_all(mixed_heads, "au", split_axis=0, concat_axis=1, tiled=True)
    attn = jnp.dot(mixed_tok, full[5], preferred_element_type=wide) + full[6].astype(wide)
    early, early_pull = jax.vjp(
        layer_norm, tokens.astype(wide) + attn, full[7].astype(wide), full[8].astype(wide)
    )
    early_low = early.astype(low_type)
    inner = jnp.dot(early_low, full[9], preferred_element_type=wide) + full[10].astype(wide)
    act, gelu_pull = jax.vjp(gelu_exact, inner)
    act_low = act.astype(low_type)
    branch = jnp.dot(act_low, full[11], preferred_element_type=wide) + full[12].astype(wide)
    result, final_pull = jax.vjp(
        layer_norm, early + branch, full[13].astype(wide), full[14].astype(wide)
    )
    output = result.astype(low_type)
    final_grads = final_pull(cotangent.astype(wide))
    branch_grad = final_grads[0].astype(low_type)
    outer_grad = jnp.einsum("tf,td->fd", act_low, branch_grad, preferred_element_type=wide)
    outer_bias_grad = jnp.sum(branch_grad.astype(wide), axis=0)
    act_grad = jnp.einsum("td,fd->tf", branch_grad, full[11], preferred_element_type=wide)
    inner_grad = gelu_pull(act_grad)[0].astype(low_type)
    inner_grad_weight = jnp.einsum("td,tf->df", early_low, inner_grad, preferred_element_type=wide)
    inner_bias_grad = jnp.sum(inner_grad.astype(wide), axis=0)
    early_grad = final_grads[0] + jnp.einsum(
        "tf,df->td", inner_grad, full[9], preferred_element_type=wide
    )
    early_grads = early_pull(early_grad)
    attn_grad = early_grads[0].astype(low_type)
    mix_grad = jnp.einsum("tc,td->cd", mixed_tok, attn_grad, preferred_element_type=wide)
    mix_bias_grad = jnp.sum(attn_grad.astype(wide), axis=0)
    mixed_grad = jnp.einsum("td,cd->tc", attn_grad, full[5], preferred_element_type=wide).astype(
        low_type
    )
    grad_heads = lax.all_to_all(mixed_grad, "au", split_axis=1, concat_axis=0, tiled=True).reshape(
        local_rows, local_heads, HEAD
    )
    delta = jnp.sum(grad_heads.astype(wide) * mixed, axis=-1)
    empty_heads = jnp.zeros((local_rows, local_heads, HEAD), wide)

    def query_step(carry, pieces, first):
        key_piece, value_piece = pieces
        count = key_piece.shape[0]
        piece_segment = segment_of(token_places(first, count, local_rows, cycle, rows), starts)
        scores = jnp.einsum("qhd,khd->qhk", queries, key_piece, preferred_element_type=wide) * scale
        same = own_segment[:, None] == piece_segment[None, :]
        scores = jnp.where(same[:, None, :], scores, mask_fill)
        probs = jnp.exp(scores - log_total[:, :, None])
        dots = jnp.einsum("qhd,khd->qhk", grad_heads, value_piece, preferred_element_type=wide)
        score_grad = (probs * (dots - delta[:, :, None])).astype(low_type)
        return carry + scale * jnp.einsum(
            "qhk,khd->qhd", score_grad, key_piece, preferred_element_type=wide
        )

    query_grad = over_blocks(
        empty_heads,
        (
            lax.all_gather(keys, "row", axis=0, tiled=True),
            lax.all_gather(values, "row", axis=0, tiled=True),
        ),
        query_step,
    )
    all_log, all_delta = (
        lax.all_gather(log_total, "row", axis=0, tiled=True),
        lax.all_gather(delta, "row", axis=0, tiled=True),
    )

    def key_step(carry, pieces, first):
        key_sum, value_sum = carry
        query_piece, grad_piece = pieces
        count = query_piece.shape[0]
        piece_segment = segment_of(token_places(first, count, local_rows, cycle, rows), starts)
        piece_log = lax.dynamic_slice_in_dim(all_log, first, count, 0)
        piece_delta = lax.dynamic_slice_in_dim(all_delta, first, count, 0)
        scores = jnp.einsum("qhd,khd->qhk", query_piece, keys, preferred_element_type=wide) * scale
        same = piece_segment[:, None] == own_segment[None, :]
        scores = jnp.where(same[:, None, :], scores, mask_fill)
        probs = jnp.exp(scores - piece_log[:, :, None])
        dots = jnp.einsum("qhd,khd->qhk", grad_piece, values, preferred_element_type=wide)
        score_grad = (probs * (dots - piece_delta[:, :, None])).astype(low_type)
        value_sum = value_sum + jnp.einsum(
            "qhk,qhd->khd", probs.astype(low_type), grad_piece, preferred_element_type=wide
        )
        key_sum = key_sum + scale * jnp.einsum(
            "qhk,qhd->khd", score_grad, query_piece, preferred_element_type=wide
        )
        return (key_sum, value_sum)

    key_sum, value_sum = over_blocks(
        (empty_heads, empty_heads),
        (
            lax.all_gather(queries, "row", axis=0, tiled=True),
            lax.all_gather(grad_heads, "row", axis=0, tiled=True),
        ),
        key_step,
    )
    query_tok, key_tok, value_tok = (
        lax.all_to_all(
            query_grad.astype(low_type).reshape(local_rows, width),
            "au",
            split_axis=0,
            concat_axis=1,
            tiled=True,
        ),
        lax.all_to_all(
            key_sum.astype(low_type).reshape(local_rows, width),
            "au",
            split_axis=0,
            concat_axis=1,
            tiled=True,
        ),
        lax.all_to_all(
            value_sum.astype(low_type).reshape(local_rows, width),
            "au",
            split_axis=0,
            concat_axis=1,
            tiled=True,
        ),
    )
    query_grad_weight = jnp.einsum("tc,td->cd", tokens, query_tok, preferred_element_type=wide)
    query_bias_grad = jnp.sum(query_tok.astype(wide), axis=0)
    key_grad_weight = jnp.einsum("tc,td->cd", tokens, key_tok, preferred_element_type=wide)
    value_grad_weight = jnp.einsum("tc,td->cd", tokens, value_tok, preferred_element_type=wide)
    value_bias_grad = jnp.sum(value_tok.astype(wide), axis=0)
    input_grad = early_grads[0] + jnp.einsum(
        "td,cd->tc", query_tok, full[0], preferred_element_type=wide
    )
    input_grad = input_grad + jnp.einsum("td,cd->tc", key_tok, full[2], preferred_element_type=wide)
    input_grad = input_grad + jnp.einsum(
        "td,cd->tc", value_tok, full[3], preferred_element_type=wide
    )
    summed = (
        lax.psum_scatter(query_grad_weight, ("au", "row"), scatter_dimension=0, tiled=True),
        lax.psum_scatter(query_bias_grad, ("au", "row"), scatter_dimension=0, tiled=True),
        lax.psum_scatter(key_grad_weight, ("au", "row"), scatter_dimension=0, tiled=True),
        lax.psum_scatter(value_grad_weight, ("au", "row"), scatter_dimension=0, tiled=True),
        lax.psum_scatter(value_bias_grad, ("au", "row"), scatter_dimension=0, tiled=True),
        lax.psum_scatter(mix_grad, ("au", "row"), scatter_dimension=0, tiled=True),
        lax.psum_scatter(mix_bias_grad, ("au", "row"), scatter_dimension=0, tiled=True),
        lax.psum_scatter(early_grads[1], ("au", "row"), scatter_dimension=0, tiled=True),
        lax.psum_scatter(early_grads[2], ("au", "row"), scatter_dimension=0, tiled=True),
        lax.psum_scatter(inner_grad_weight, ("au", "row"), scatter_dimension=0, tiled=True),
        lax.psum_scatter(inner_bias_grad, ("au", "row"), scatter_dimension=0, tiled=True),
        lax.psum_scatter(outer_grad, ("au", "row"), scatter_dimension=0, tiled=True),
        lax.psum_scatter(outer_bias_grad, ("au", "row"), scatter_dimension=0, tiled=True),
        lax.psum_scatter(final_grads[1], ("au", "row"), scatter_dimension=0, tiled=True),
        lax.psum_scatter(final_grads[2], ("au", "row"), scatter_dimension=0, tiled=True),
    )
    return (
        output,
        input_grad.astype(low_type),
        summed[0],
        summed[1],
        summed[2],
        summed[3],
        summed[4],
        summed[5],
        summed[6],
        summed[7],
        summed[8],
        summed[9],
        summed[10],
        summed[11],
        summed[12],
        summed[13],
        summed[14],
    )


def solution(mesh):
    in_specs = (
        P(("au", "row"), None),
        P(("au", "row"), None),
        P(),
        P(("au", "row"), None),
        P(("au", "row")),
        P(("au", "row"), None),
        P(("au", "row"), None),
        P(("au", "row")),
        P(("au", "row"), None),
        P(("au", "row")),
        P(("au", "row")),
        P(("au", "row")),
        P(("au", "row"), None),
        P(("au", "row")),
        P(("au", "row"), None),
        P(("au", "row")),
        P(("au", "row")),
        P(("au", "row")),
    )
    out_specs = (
        P(("au", "row"), None),
        P(("au", "row"), None),
        P(("au", "row"), None),
        P(("au", "row")),
        P(("au", "row"), None),
        P(("au", "row"), None),
        P(("au", "row")),
        P(("au", "row"), None),
        P(("au", "row")),
        P(("au", "row")),
        P(("au", "row")),
        P(("au", "row"), None),
        P(("au", "row")),
        P(("au", "row"), None),
        P(("au", "row")),
        P(("au", "row")),
        P(("au", "row")),
    )
    return jax.shard_map(
        on_device, mesh=mesh, in_specs=in_specs, out_specs=out_specs, check_vma=False
    )
```

profile of v0, /device:TPU:0, one launch (start us, length us, event | category | flops | bytes accessed | tf_op | source)
XLA Modules:
  0.0 1259.4 jit_solution(3821116367970201793)
XLA Ops:
  12.1 56.3 %all-gather.11.cloned.1.call-done = bf16[768,768]{1,0:T(8,128)(2,1)} async-done(((bf16[24,768]{1,0:T(8,128)(2,1)}), bf16[768,768]{1,0:T(8,128)(2,1)}) %all-gather.11.cloned.1.call-update) | async-done | bytes 1179664 | tf_op jit(solution)/shard_map/all_gather | solution.py:79
  70.3 7.8 all_to_all.140
  81.2 38.8 %all-reduce.19 = (bf16[3072]{0:T(1024)(128)(2,1)S(1)}, bf16[768]{0:T(1024)(128)(2,1)S(1)}, bf16[768]{0:T(1024)(128)(2,1)S(1)}, bf16[768]{0:T(1024)(128)(2,1)S(1)...) all-reduce(bf16[3072]{0:T(1024)(128)(2,1)S(1)} %dynamic-update-slic, ...), channel_id=1, replica_groups=mesh['au'=4,'row'=8] {'au','row'}, use_global_device_ids=true, to_apply=%add.5 | all-reduce | flops 9216 | bytes 36864
  120.0 5.0 all-gather.17.cloned.1.call-done
  126.9 8.0 all_to_all.141
  139.6 42.2 %all-gather.15.cloned.1.call-done = bf16[768,768]{1,0:T(8,128)(2,1)} async-done(((bf16[24,768]{1,0:T(8,128)(2,1)}), bf16[768,768]{1,0:T(8,128)(2,1)}) %all-gather.15.cloned.1.call-update) | async-done | bytes 1179664 | tf_op jit(solution)/shard_map/all_gather | solution.py:77
  184.2 3.4 all-to-all-start.1
  187.6 5.3 all-to-all-done.1
  193.8 34.7 %all-gather.13.cloned.1.call-done = bf16[4096,3,64]{0,2,1:T(8,128)(2,1)} async-done(((bf16[512,3,64]{0,2,1:T(8,128)(2,1)}), bf16[4096,3,64]{0,2,1:T(8,128)(2,1)}) %all-gather.13.cloned.1.call-update) | async-done | bytes 1572880 | tf_op jit(solution)/shard_map/all_gather | solution.py:144
  228.5 45.4 %all-gather.19.cloned.1.call-done = bf16[4096,3,64]{0,2,1:T(8,128)(2,1)} async-done(((bf16[512,3,64]{0,2,1:T(8,128)(2,1)}), bf16[4096,3,64]{0,2,1:T(8,128)(2,1)}) %all-gather.19.cloned.1.call-update) | async-done | bytes 1572880 | tf_op jit(solution)/shard_map/all_gather | solution.py:145
  273.9 61.9 %while.48 = (s32[]{:T(128)}, f32[512,3]{0,1:T(4,128)S(1)}, f32[512,3]{0,1:T(4,128)S(1)}, f32[512,3,64]{0,2,1:T(8,128)}, s32[512]{0:T(512)S(1)}, /*index=5*/s32[1...) while((s32[]{:T(128)}, f32[512,3]{0,1:T(4,128)S(1)}, ...), condition=%wide.region_6.7_spmd.clone, body=%wide.region_2.6_spmd.clone.sunk | while | flops 210588672 | bytes 15120727 | solution.py:39
  337.7 3.4 all-to-all-start.3
  342.0 4.6 all-to-all-done.3
  348.6 47.2 %all-gather.23.cloned.1.call-done = bf16[768,3072]{1,0:T(8,128)(2,1)} async-done(((bf16[24,3072]{1,0:T(8,128)(2,1)}), bf16[768,3072]{1,0:T(8,128)(2,1)}) %all-gather.23.cloned.1.call-update) | async-done | bytes 4718608 | tf_op jit(solution)/shard_map/all_gather | solution.py:86
  395.8 7.6 multiply_convert_fusion
  403.4 57.8 %all-gather.25.cloned.1.call-done = bf16[3072,768]{1,0:T(8,128)(2,1)} async-done(((bf16[96,768]{1,0:T(8,128)(2,1)}), bf16[3072,768]{1,0:T(8,128)(2,1)}) %all-gather.25.cloned.1.call-update) | async-done | bytes 4718608 | tf_op jit(solution)/shard_map/all_gather | solution.py:88
  461.2 3.4 fusion.127
  474.6 7.8 all_to_all.142
  488.6 69.7 %while.49 = (s32[]{:T(128)}, f32[512,3,64]{0,2,1:T(8,128)}, s32[8]{0:T(128)}, bf16[4096,3,64]{0,2,1:T(8,128)(2,1)}, s32[512]{0:T(512)S(1)}, /*index=5*/s32[16]{0...) while((s32[]{:T(128)}, f32[512,3,64]{0,2,1:T(8,128)}, ...), condition=%wide.region_18.19_spmd.clone, body=%wide.region_16.18_spmd.clone.sunk | while | flops 307312128 | bytes 8615712 | solution.py:39
  493.8 3.5 fusion.211
  502.4 3.6 fusion.211
  511.1 3.6 fusion.211
  519.8 3.6 fusion.211
  528.5 3.6 fusion.211
  537.3 3.6 fusion.211
  546.0 3.6 fusion.211
  554.7 3.6 fusion.211
  560.1 3.4 all-to-all-start.5
  563.6 32.5 %all_gather.83 = f32[4096,3]{0,1:T(4,128)} all-gather(f32[512,3]{0,1:T(4,128)S(1)} %copy-done.30), channel_id=1, replica_groups=mesh['au'=4,'row'=8] {'row'}, dimensions={0}, use_global_device_ids=true | all-gather | bytes 55296 | tf_op jit(solution)/shard_map/all_gather | solution.py:213
  596.1 32.5 %all_gather.85 = f32[4096,3]{0,1:T(4,128)} all-gather(f32[512,3]{0,1:T(4,128)S(1)} %get-tuple-element.1356), channel_id=1, replica_groups=mesh['au'=4,'row'=8] {'row'}, dimensions={0}, use_global_device_ids=true | all-gather | bytes 55296 | tf_op jit(solution)/shard_map/all_gather | solution.py:214
  632.0 103.2 %while.50 = (s32[]{:T(128)}, f32[512,3,64]{0,2,1:T(8,128)}, f32[512,3,64]{0,2,1:T(8,128)}, s32[8]{0:T(128)}, bf16[4096,3,64]{0,2,1:T(8,128)(2,1)}, /*index=5*/s3...) while((s32[]{:T(128)}, f32[512,3,64]{0,2,1:T(8,128)}, ...), condition=%wide.region_21.22_spmd.clone, body=%wide.region_19.21_spmd.clone.sunk | while | flops 411317760 | bytes 13037361 | solution.py:39
  638.5 3.4 fusion.221
  651.1 3.6 fusion.221
  664.1 3.5 fusion.221
  677.0 3.6 fusion.221
  689.9 3.6 fusion.221
  702.9 3.5 fusion.221
  715.8 3.6 fusion.221
  728.8 3.5 fusion.221
  736.3 8.3 all_to_all.143
  748.2 7.7 all_to_all.144
  759.6 5.2 fusion.120
  765.9 5.0 fusion.129
  774.0 38.3 %all-reduce.18 = (f32[768]{0:T(1024)S(1)}, f32[768]{0:T(1024)S(1)}, f32[768]{0:T(1024)S(1)}, f32[768]{0:T(1024)S(1)}, f32[768]{0:T(1024)S(1)}, /*index=5*/f32[30...) all-reduce(f32[768]{0:T(1024)S(1)} %reduce_sum.270, ...), channel_id=3, replica_groups=mesh['au'=4,'row'=8] {'au','row'}, use_global_device_ids=true, to_apply=%region_24.25.clone | all-reduce | flops 9216 | bytes 73728
  820.3 45.0 %reduce-scatter.21.cloned.1.call-done = f32[24,768]{1,0:T(8,128)} async-done(((f32[768,768]{1,0:T(8,128)}), f32[24,768]{1,0:T(8,128)}) %reduce-scatter.21.cloned.1.call-update) | async-done | bytes 73744
  865.3 104.6 %reduce-scatter.23.cloned.1.call-done = f32[24,768]{1,0:T(8,128)} async-done(((f32[768,768]{1,0:T(8,128)}), f32[24,768]{1,0:T(8,128)}) %reduce-scatter.23.cloned.1.call-update) | async-done | bytes 73744
  969.9 140.9 %reduce-scatter.15.cloned.1.call-done = f32[24,3072]{1,0:T(8,128)} async-done(((f32[768,3072]{1,0:T(8,128)}), f32[24,3072]{1,0:T(8,128)}) %reduce-scatter.15.cloned.1.call-update) | async-done | bytes 294928 | tf_op jit(solution)/shard_map/reduce_scatter | solution.py:291
  1110.8 142.1 %reduce-scatter.17.cloned.1.call-done = f32[96,768]{1,0:T(8,128)} async-done(((f32[3072,768]{1,0:T(8,128)}), f32[96,768]{1,0:T(8,128)}) %reduce-scatter.17.cloned.1.call-update) | async-done | bytes 294928 | tf_op jit(solution)/shard_map/reduce_scatter | solution.py:293
  (515 shorter events, 226.9 us)
Async XLA Ops:
  7.2 61.2 %all-gather.11.cloned.1.call-start = ((), (), s32[]{:S(2)}) async-start(), calls=%async_computation.14 | async-start | bytes 1216512 | tf_op jit(solution)/shard_map/all_gather | solution.py:79
  8.8 116.3 %all-gather.17.cloned.1.call-start = ((), (), s32[]{:S(2)}) async-start(), calls=%async_computation.17 | async-start | bytes 1216512 | tf_op jit(solution)/shard_map/all_gather | solution.py:80
  10.3 171.5 %all-gather.15.cloned.1.call-start = ((), (), s32[]{:S(2)}) async-start(), calls=%async_computation.16 | async-start | bytes 1216512 | tf_op jit(solution)/shard_map/all_gather | solution.py:77
  11.9 67.2 %copy-start.45 = (f32[96]{0:T(128)S(1)}, f32[96]{0:T(128)}, u32[]{:S(2)}) copy-start(f32[96]{0:T(128)} %param.37) | copy-start | bytes 1156
  11.9 67.2 %copy-start.46 = (f32[24]{0:T(128)S(1)}, f32[24]{0:T(128)}, u32[]{:S(2)}) copy-start(f32[24]{0:T(128)} %param.28) | copy-start | bytes 292
  12.0 67.2 %copy-start.47 = (f32[24]{0:T(128)S(1)}, f32[24]{0:T(128)}, u32[]{:S(2)}) copy-start(f32[24]{0:T(128)} %param.31) | copy-start | bytes 292
  12.0 67.2 %copy-start.48 = (f32[24]{0:T(128)S(1)}, f32[24]{0:T(128)}, u32[]{:S(2)}) copy-start(f32[24]{0:T(128)} %param.33) | copy-start | bytes 292
  12.0 67.2 %copy-start.49 = (f32[24]{0:T(128)S(1)}, f32[24]{0:T(128)}, u32[]{:S(2)}) copy-start(f32[24]{0:T(128)} %param.35) | copy-start | bytes 292
  12.0 67.2 %copy-start.50 = (f32[24]{0:T(128)S(1)}, f32[24]{0:T(128)}, u32[]{:S(2)}) copy-start(f32[24]{0:T(128)} %param.34) | copy-start | bytes 292
  12.0 67.2 %copy-start.51 = (f32[24]{0:T(128)S(1)}, f32[24]{0:T(128)}, u32[]{:S(2)}) copy-start(f32[24]{0:T(128)} %param.39) | copy-start | bytes 292
  12.0 67.2 %copy-start.52 = (f32[24]{0:T(128)S(1)}, f32[24]{0:T(128)}, u32[]{:S(2)}) copy-start(f32[24]{0:T(128)} %param.41) | copy-start | bytes 292
  12.0 67.3 %copy-start.53 = (f32[24]{0:T(128)S(1)}, f32[24]{0:T(128)}, u32[]{:S(2)}) copy-start(f32[24]{0:T(128)} %param.40) | copy-start | bytes 292
  12.0 113.0 %copy-start.3 = (bf16[128,768]{1,0:T(8,128)(2,1)S(1)}, bf16[128,768]{1,0:T(8,128)(2,1)}, u32[]{:S(2)}) copy-start(bf16[128,768]{1,0:T(8,128)(2,1)} %param.24) | copy-start | bytes 589828
  12.0 216.4 %all-gather.13.cloned.1.call-start = ((), (), s32[]{:S(2)}) async-start(), calls=%async_computation.15 | async-start | bytes 1769472 | tf_op jit(solution)/shard_map/all_gather | solution.py:144
  79.0 194.9 %all-gather.19.cloned.1.call-start = ((), (), s32[]{:S(2)}) async-start(), calls=%async_computation.18 | async-start | bytes 1769472 | tf_op jit(solution)/shard_map/all_gather | solution.py:145
  120.0 15.8 %copy-start.29 = (f32[24,768]{1,0:T(8,128)S(1)}, f32[24,768]{1,0:T(8,128)}, u32[]{:S(2)}) copy-start(f32[24,768]{1,0:T(8,128)} %param.32) | copy-start | bytes 221188
  120.0 16.5 %copy-start.25 = (f32[24,3072]{1,0:T(8,128)S(1)}, f32[24,3072]{1,0:T(8,128)}, u32[]{:S(2)}) copy-start(f32[24,3072]{1,0:T(8,128)} %param.36) | copy-start | bytes 884740
  126.7 10.6 copy-start.26
  126.7 11.4 copy-start.44
  135.8 206.2 %all-gather.21.cloned.1.call-start = ((), (), s32[]{:S(2)}) async-start(), calls=%async_computation.19 | async-start | bytes 1216512 | tf_op jit(solution)/shard_map/all_gather | solution.py:82
  136.5 259.3 %all-gather.23.cloned.1.call-start = ((), (), s32[]{:S(2)}) async-start(), calls=%async_computation.20 | async-start | bytes 4866048 | tf_op jit(solution)/shard_map/all_gather | solution.py:86
  137.3 323.9 %all-gather.25.cloned.1.call-start = ((), (), s32[]{:S(2)}) async-start(), calls=%async_computation.21 | async-start | bytes 4866048 | tf_op jit(solution)/shard_map/all_gather | solution.py:88
  184.2 8.7 all-to-all-start.1
  335.8 10.8 copy-start.4
  337.7 8.9 all-to-all-start.3
  341.0 290.1 %all-gather.27.cloned.1.call-start = ((), (), s32[]{:S(2)}) async-start(), calls=%async_computation.22 | async-start | bytes 1769472 | tf_op jit(solution)/shard_map/all_gather | solution.py:241
  341.1 120.1 %copy-start.27 = (f32[768]{0:T(1024)}, f32[768]{0:T(1024)S(1)}, u32[]{:S(2)}) copy-start(f32[768]{0:T(1024)S(1)} %convert_element_type.214) | copy-start | bytes 9220
  341.8 289.4 %all-gather.29.cloned.1.call-start = ((), (), s32[]{:S(2)}) async-start(), calls=%async_computation.23 | async-start | bytes 1769472 | tf_op jit(solution)/shard_map/all_gather | solution.py:242
  348.3 123.8 %copy-start.1 = (f32[128,768]{1,0:T(8,128)}, f32[128,768]{1,0:T(8,128)S(1)}, u32[]{:S(2)}) copy-start(f32[128,768]{1,0:T(8,128)S(1)} %get-tuple-element.942) | copy-start | bytes 1179652
  348.3 123.8 %copy-start.31 = (f32[128]{0:T(128)}, f32[128]{0:T(128)S(1)}, u32[]{:S(2)}) copy-start(f32[128]{0:T(128)S(1)} %broadcast_multiply_fusion.1) | copy-start | bytes 1540
  348.6 123.6 %copy-start.39 = (f32[128]{0:T(128)}, f32[128]{0:T(128)S(1)}, u32[]{:S(2)}) copy-start(f32[128]{0:T(128)S(1)} %fusion.118) | copy-start | bytes 1540
  403.4 61.2 %copy-start.10 = (bf16[128,3072]{1,0:T(8,128)(2,1)}, bf16[128,3072]{1,0:T(8,128)(2,1)S(1)}, u32[]{:S(2)}) copy-start(bf16[128,3072]{1,0:T(8,128)(2,1)S(1)} %get-tuple-element.934) | copy-start | bytes 2359300
  461.2 6.0 slice-start
  461.2 3.6 copy-start.21
  461.2 6.0 slice-start.1
  466.5 3.2 slice-start.2
  472.4 10.2 copy-start.42
  483.3 337.0 %reduce-scatter.13.cloned.1.call-start = ((), (), s32[]{:S(2)}) async-start(), calls=%async_computation.24 | async-start | bytes 2433024 | tf_op jit(solution)/shard_map/reduce_scatter | solution.py:287
  558.3 5.2 copy-start.30
  560.1 68.5 %all-to-all-start.5 = ((bf16[4,128,192]{1,2,0:T(8,128)(2,1)}), bf16[4,128,192]{1,2,0:T(8,128)(2,1)S(1)}, u32[]{:S(2)}, u32[]{:S(2)}) async-start(bf16[4,128,192]{1,2,0:T(8,128)(2,1)} %copy.133), calls=%async_computation.5 | async-start | bytes 393216 | tf_op jit(solution)/shard_map/all_to_all | solution.py:247
  563.5 256.8 %reduce-scatter.19.cloned.1.call-start = ((), (), s32[]{:S(2)}) async-start(), calls=%async_computation.27 | async-start | bytes 2433024
  631.1 234.2 %reduce-scatter.21.cloned.1.call-start = ((), (), s32[]{:S(2)}) async-start(), calls=%async_computation.28 | async-start | bytes 2433024
  747.1 222.7 %reduce-scatter.23.cloned.1.call-start = ((), (), s32[]{:S(2)}) async-start(), calls=%async_computation.29 | async-start | bytes 2433024
  758.4 352.4 %reduce-scatter.15.cloned.1.call-start = ((), (), s32[]{:S(2)}) async-start(), calls=%async_computation.25 | async-start | bytes 9732096 | tf_op jit(solution)/shard_map/reduce_scatter | solution.py:291
  764.8 488.1 %reduce-scatter.17.cloned.1.call-start = ((), (), s32[]{:S(2)}) async-start(), calls=%async_computation.26 | async-start | bytes 9732096 | tf_op jit(solution)/shard_map/reduce_scatter | solution.py:293
  771.0 2.9 copy-start.33
  771.1 46.5 %copy-start.6 = (bf16[768,768]{1,0:T(8,128)(2,1)S(1)}, bf16[768,768]{1,0:T(8,128)(2,1)}, u32[]{:S(2)}) copy-start(bf16[768,768]{1,0:T(8,128)(2,1)} %all-gather.11.cloned.1.call-done) | copy-start | bytes 3538948
  773.7 45.4 %copy-start.9 = (bf16[768,768]{1,0:T(8,128)(2,1)S(1)}, bf16[768,768]{1,0:T(8,128)(2,1)}, u32[]{:S(2)}) copy-start(bf16[768,768]{1,0:T(8,128)(2,1)} %all-gather.17.cloned.1.call-done) | copy-start | bytes 3538948
  (44 other events, 65.4 us)
Sparse Core Ops, SparseCore 0:
  11.5 56.8 all-gather.10
  71.9 53.1 all-gather.16
  128.6 53.1 all-gather.14
  184.3 44.1 all-gather.12
  230.4 43.4 all-gather.18
  277.2 52.3 all-gather.20
  333.1 62.6 all-gather.22
  398.7 62.4 all-gather.24
  463.8 44.1 all-gather.26
  509.9 43.4 all-gather.28
  559.3 97.2 reduce-scatter.12
  663.2 98.0 reduce-scatter.18
  767.2 98.0 reduce-scatter.20
  871.9 97.9 reduce-scatter.22
  976.2 134.5 reduce-scatter.14
  1118.1 134.6 reduce-scatter.16
where the time goes:
time: 1260 us
  waiting for transfers between devices  732 us (58%)
  blocking collectives  182 us (14%)
  matrix products  175 us (14%)
  local copies, waits for them, and re-layouts  70.2 us (6%)
  other arithmetic  57.6 us (5%)
  loops' own time  16.5 us (1%)
  between operations  14.9 us (1%)
    unnamed x19, waiting for transfers between devices  150 us
    reduce_scatter x1, waiting for transfers between devices, on_device(): lax.psum_scatter(outer_grad, ('au', 'row'), scatter_dimension=0, tiled=True)  142 us
    reduce_scatter x1, waiting for transfers between devices, on_device(): lax.psum_scatter(inner_grad_weight, ('au', 'row'), scatter_dimension=0, t...  141 us
    unnamed x2, blocking collectives  77.1 us
    all_gather x1, waiting for transfers between devices, on_device(): lax.all_gather(outer_weight.astype(low_type), ('au', 'row'), axis=0, tile...  57.8 us
    all_gather x1, waiting for transfers between devices, on_device(): lax.all_gather(key_weight.astype(low_type), ('au', 'row'), axis=0, tiled=...  56.3 us
    all_gather x1, waiting for transfers between devices, on_device(): lax.all_gather(inner_weight.astype(low_type), ('au', 'row'), axis=0, tile...  47.2 us
    all_gather x1, waiting for transfers between devices, on_device(): lax.all_gather(values, 'row', axis=0, tiled=True)  45.4 us
  transfers between devices with their start and end apart: 19, of which 13 were waited for; matrix products, arithmetic and copies ran while one was open for 23% of the time, Pallas kernels for 0%

commit v1 on v0

v1 whole, which is shorter than its diff:
```python
import functools

import jax
import jax.numpy as jnp
from jax import lax
from jax.experimental import pallas as pl
from jax.experimental.pallas import tpu as pltpu
from jax.sharding import PartitionSpec as P

HEAD = 64
HEADS = 12
GROUPS = 4
LOCAL = HEADS // GROUPS
LANES = 2 * HEAD
WIDE = LOCAL * LANES
PACK = 256
eps_norm = 1e-06
mask_fill = -1000000000.0
lowest_start = -1e30
low_type = jnp.bfloat16
wide = jnp.float32
MESH = pl.DeviceIdType.MESH
VMEM_LIMIT = 62 * 1024 * 1024


def layer_norm(hidden, gain, shift):
    mean = jnp.mean(hidden, axis=-1, keepdims=True)
    centered = hidden - mean
    spread = jnp.mean(centered * centered, axis=-1, keepdims=True)
    return centered * lax.rsqrt(spread + eps_norm) * gain + shift


def gelu_exact(values):
    return jax.nn.gelu(values, approximate=False)


class Place:
    def __init__(self, zs):
        self.zs = zs
        a = lax.axis_index("au")
        r = lax.axis_index("row")
        self.x, self.c = a // 2, a % 2
        self.y, q = r % 2, r // 2
        self.g, self.z = q % GROUPS, q // GROUPS

    def at(self, x=None, c=None, z=None, g=None, y=None):
        x = self.x if x is None else x
        c = self.c if c is None else c
        z = self.z if z is None else z
        g = self.g if g is None else g
        y = self.y if y is None else y
        return (x * 2 + c, (z * GROUPS + g) * 2 + y)

    def sibling(self):
        return self.at(c=1 - self.c)

    def line(self):
        return [((self.g + k) % GROUPS, (self.g + GROUPS - k) % GROUPS) for k in range(1, GROUPS)]

    def column(self):
        count = self.zs * GROUPS
        q = self.z * GROUPS + self.g
        result = []
        for k in range(1, count):
            to, source = (q + k) % count, (q + count - k) % count
            result.append(((to // GROUPS, to % GROUPS), (source // GROUPS, source % GROUPS)))
        return result

    def plane(self, everywhere=True):
        result = []
        for dx in range(2):
            for dy in range(2):
                for dz in range(self.zs if everywhere else 1):
                    if dx + dy + dz == 0:
                        continue
                    to = ((self.x + dx) % 2, (self.z + dz) % self.zs, (self.y + dy) % 2)
                    source = (
                        (self.x + dx) % 2,
                        (self.z + self.zs - dz) % self.zs,
                        (self.y + dy) % 2,
                    )
                    result.append((to, source))
        return result


class Copies:
    def __init__(self, send, recv, local):
        self.send, self.recv, self.local = send, recv, local
        self.count = 0
        self.local_count = 0
        self.started = []
        self.local_started = []

    def push(self, source, target, device):
        copy = pltpu.make_async_remote_copy(
            src_ref=source,
            dst_ref=target,
            send_sem=self.send.at[self.count],
            recv_sem=self.recv.at[self.count],
            device_id=device,
            device_id_type=MESH,
        )
        self.count += 1
        copy.start()
        self.started.append(copy)
        return copy

    def keep(self, source, target):
        copy = pltpu.make_async_copy(source, target, self.local.at[self.local_count])
        self.local_count += 1
        copy.start()
        return copy

    def finish(self):
        for copy in self.started:
            copy.wait_send()


def greet(devices, partner=None, crossing=None):
    barrier = pltpu.get_barrier_semaphore()
    for device in devices:
        pl.semaphore_signal(barrier, inc=1, device_id=device, device_id_type=MESH)
    if partner is None:
        pl.semaphore_wait(barrier, len(devices))
        return

    @pl.when(crossing)
    def _():
        pl.semaphore_signal(barrier, inc=1, device_id=partner, device_id_type=MESH)
        pl.semaphore_wait(barrier, len(devices) + 1)

    @pl.when(jnp.logical_not(crossing))
    def _():
        pl.semaphore_wait(barrier, len(devices))


def comm_call(body, name, ident, outs, copies, locals_, args, spaces=None, out_spaces=None, scratch=()):
    spaces = [pl.ANY] * len(args) if spaces is None else spaces
    out_spaces = [pl.ANY] * len(outs) if out_spaces is None else out_spaces
    return pl.pallas_call(
        body,
        name=name,
        out_shape=tuple(outs),
        in_specs=[pl.BlockSpec(memory_space=space) for space in spaces],
        out_specs=tuple(pl.BlockSpec(memory_space=space) for space in out_spaces),
        scratch_shapes=[
            pltpu.SemaphoreType.DMA((max(copies, 1),)),
            pltpu.SemaphoreType.DMA((max(copies, 1),)),
            pltpu.SemaphoreType.DMA((max(locals_, 1),)),
            *scratch,
        ],
        compiler_params=pltpu.CompilerParams(
            collective_id=ident, has_side_effects=True, vmem_limit_bytes=VMEM_LIMIT
        ),
    )(*args)


def spread_tokens(zs, tokens, slab):
    n, width = tokens.shape
    groups, rows, columns = slab.shape
    plane = 4 * zs - 1

    def body(tok, piece, tok_all, w_all, send, recv, local):
        me = Place(zs)
        copies = Copies(send, recv, local)
        greet(
            [me.at(g=to) for to, _ in me.line()]
            + [me.at(x=to[0], z=to[1], y=to[2]) for to, _ in me.plane()]
            + [me.sibling()]
        )
        first = [
            copies.push(
                piece.at[to], w_all.at[me.x, me.c, me.z, me.g, me.y], me.at(g=to)
            )
            for to, _ in me.line()
        ]
        own = copies.keep(piece.at[me.g], w_all.at[me.x, me.c, me.z, me.g, me.y])
        arrivals = [copies.push(tok, tok_all.at[me.g], me.at(g=to)) for to, _ in me.line()]
        mine = copies.keep(tok, tok_all.at[me.g])
        own.wait()
        for copy in first:
            copy.wait_recv()
        block = w_all.at[me.x, me.c, me.z, :, me.y]
        second = [
            copies.push(block, block, me.at(x=to[0], z=to[1], y=to[2])) for to, _ in me.plane()
        ]
        arrivals.append(copies.push(block, block, me.sibling()))
        for copy, (_, source) in zip(second, me.plane()):
            copy.wait_recv()
            part = w_all.at[source[0], me.c, source[1], :, source[2]]
            arrivals.append(copies.push(part, part, me.sibling()))
        for copy in arrivals:
            copy.wait_recv()
        mine.wait()
        copies.finish()

    return comm_call(
        body,
        "spread_tokens",
        0,
        [
            jax.ShapeDtypeStruct((GROUPS, n, width), low_type),
            jax.ShapeDtypeStruct((2, 2, zs, GROUPS, 2, rows, columns), low_type),
        ],
        2 * (GROUPS - 1) + 2 * plane + 1,
        2,
        (tokens, slab),
    )


def spread_keys(zs, keys, inner, outer, mix):
    groups, n, width = keys.shape
    quarters, rows, columns = inner.shape
    tall, _ = outer.shape
    plane, column = 4 * zs - 1, GROUPS * zs - 1

    def body(kv, w1s, w2s, wms, kv_all, w1, w2, wm, send, recv, local, swap_send, swap_recv):
        me = Place(zs)
        copies = Copies(send, recv, local)
        crossing = me.c != me.y
        greet(
            [me.at(x=to[0], z=to[1], y=to[2]) for to, _ in me.plane()]
            + [me.at(z=to[0], g=to[1]) for to, _ in me.column()]
            + [me.at(z=to[0], g=to[1], c=me.y, y=me.c) for to, _ in me.column()]
            + [me.sibling()],
            me.at(c=me.y, y=me.c),
            crossing,
        )

        def here(ref):
            return ref.at[me.x, me.c, me.z, me.g, me.y]

        flat = me.plane(everywhere=False)
        own = [
            copies.keep(w1s.at[me.x * 2 + me.y], here(w1)),
            copies.keep(wms, here(wm)),
            copies.keep(kv, kv_all.at[me.x, me.c, me.z, :, me.y]),
        ]
        w1_first = [
            copies.push(w1s.at[to[0] * 2 + to[2]], here(w1), me.at(x=to[0], y=to[2]))
            for to, _ in flat
        ]
        wm_first = [
            copies.push(wms, here(wm), me.at(z=to[0], g=to[1])) for to, _ in me.column()
        ]
        mine = kv_all.at[me.x, me.c, me.z, :, me.y]
        kv_first = [
            copies.push(kv, mine, me.at(x=to[0], z=to[1], y=to[2])) for to, _ in me.plane()
        ]
        arrivals = [copies.push(kv, mine, me.sibling())]
        w2_first = [
            copies.push(
                w2s, w2.at[me.z, me.g, me.y], me.at(z=to[0], g=to[1], c=me.y, y=me.c)
            )
            for to, _ in me.column()
        ]
        exchanged = pltpu.make_async_remote_copy(
            src_ref=w2s,
            dst_ref=w2.at[me.z, me.g, me.y],
            send_sem=swap_send,
            recv_sem=swap_recv,
            device_id=me.at(c=me.y, y=me.c),
            device_id_type=MESH,
        )
        stays = pltpu.make_async_copy(w2s, w2.at[me.z, me.g, me.y], swap_recv)

        @pl.when(crossing)
        def _():
            exchanged.start()

        @pl.when(jnp.logical_not(crossing))
        def _():
            stays.start()

        own[0].wait()
        for copy in w1_first:
            copy.wait_recv()
        block = w1.at[:, me.c, me.z, me.g, :]
        w1_second = [
            copies.push(block, block, me.at(z=to[0], g=to[1])) for to, _ in me.column()
        ]
        arrivals.append(copies.push(block, block, me.sibling()))
        own[1].wait()
        for copy in wm_first:
            copy.wait_recv()
        block = wm.at[me.x, me.c, :, :, me.y]
        wm_second = [copies.push(block, block, me.at(x=to[0], y=to[2])) for to, _ in flat]
        arrivals.append(copies.push(block, block, me.sibling()))
        for copy, (_, source) in zip(kv_first, me.plane()):
            copy.wait_recv()
            part = kv_all.at[source[0], me.c, source[1], :, source[2]]
            arrivals.append(copies.push(part, part, me.sibling()))

        @pl.when(crossing)
        def _():
            exchanged.wait_recv()
            exchanged.wait_send()

        @pl.when(jnp.logical_not(crossing))
        def _():
            stays.wait()

        part = w2.at[me.z, me.g, me.c]
        arrivals.append(copies.push(part, part, me.sibling()))
        for copy, (_, source) in zip(wm_second, flat):
            copy.wait_recv()
            part = wm.at[source[0], me.c, :, :, source[2]]
            arrivals.append(copies.push(part, part, me.sibling()))
        for copy, (_, source) in zip(w2_first, me.column()):
            copy.wait_recv()
            part = w2.at[source[0], source[1], me.c]
            arrivals.append(copies.push(part, part, me.sibling()))
        for copy, (_, source) in zip(w1_second, me.column()):
            copy.wait_recv()
            part = w1.at[:, me.c, source[0], source[1], :]
            arrivals.append(copies.push(part, part, me.sibling()))
        for copy in arrivals:
            copy.wait_recv()
        own[2].wait()
        copies.finish()

    return comm_call(
        body,
        "spread_keys",
        1,
        [
            jax.ShapeDtypeStruct((2, 2, zs, GROUPS, 2, n, width), low_type),
            jax.ShapeDtypeStruct((2, 2, zs, GROUPS, 2, rows, columns), low_type),
            jax.ShapeDtypeStruct((zs, GROUPS, 2, tall, columns), low_type),
            jax.ShapeDtypeStruct((2, 2, zs, GROUPS, 2) + mix.shape, low_type),
        ],
        2 * plane + 1 + 2 * (3 + column + 1 + column) + column + 3 + 8,
        3,
        (keys, inner, outer, mix),
        scratch=(pltpu.SemaphoreType.DMA, pltpu.SemaphoreType.DMA),
    )


def exchange_line(zs, ident, pieces):
    def body(source, target, send, recv, local):
        me = Place(zs)
        copies = Copies(send, recv, local)
        greet([me.at(g=to) for to, _ in me.line()])
        arrivals = [
            copies.push(source.at[to], target.at[me.g], me.at(g=to)) for to, _ in me.line()
        ]
        own = copies.keep(source.at[me.g], target.at[me.g])
        for copy in arrivals:
            copy.wait_recv()
        own.wait()
        copies.finish()

    return comm_call(
        body,
        "exchange_line",
        ident,
        [jax.ShapeDtypeStruct(pieces.shape, pieces.dtype)],
        GROUPS - 1,
        1,
        (pieces,),
    )[0]


def gather_square(zs, ident, rows):
    def body(source, target, send, recv, local):
        me = Place(zs)
        copies = Copies(send, recv, local)
        flat = me.plane(everywhere=False)
        greet([me.at(x=to[0], y=to[2]) for to, _ in flat])
        place = target.at[me.x, me.y]
        arrivals = [copies.push(source, place, me.at(x=to[0], y=to[2])) for to, _ in flat]
        own = copies.keep(source, place)
        for copy in arrivals:
            copy.wait_recv()
        own.wait()
        copies.finish()

    return comm_call(
        body,
        "gather_square",
        ident,
        [jax.ShapeDtypeStruct((2, 2) + rows.shape, rows.dtype)],
        3,
        1,
        (rows,),
    )[0]


def exchange_square(zs, ident, pieces):
    def body(source, target, send, recv, local):
        me = Place(zs)
        copies = Copies(send, recv, local)
        flat = me.plane(everywhere=False)
        greet([me.at(x=to[0], y=to[2]) for to, _ in flat])
        place = target.at[me.x, me.y]
        arrivals = [
            copies.push(source.at[to[0], to[2]], place, me.at(x=to[0], y=to[2]))
            for to, _ in flat
        ]
        own = copies.keep(source.at[me.x, me.y], place)
        for copy in arrivals:
            copy.wait_recv()
        own.wait()
        copies.finish()

    return comm_call(
        body,
        "exchange_square",
        ident,
        [jax.ShapeDtypeStruct(pieces.shape, pieces.dtype)],
        3,
        1,
        (pieces,),
    )[0]


def loop(count, step):
    def body(index, carry):
        step(index)
        return carry

    lax.fori_loop(0, count, body, 0)


def total_of(*values):
    result = values[0].astype(wide)
    for value in values[1:]:
        result = result + value.astype(wide)
    return result


def reduce_keys(zs, dkv, grad1, grad2, gradm):
    n, width = dkv.shape[-2:]
    rows, columns = grad1.shape[-2:]
    rowsm = gradm.shape[-2]
    tall = grad2.shape[-2]
    plane, column = 4 * zs - 1, GROUPS * zs - 1
    count = GROUPS * zs

    def body(
        dkv_ref, g1, g2, gm, dkv_out, out1, out2, outm,
        send, recv, local,
        swap_send, swap_recv, kst, s1, p1, f1, s2, p2, sm, pm, fm, tm,
    ):
        me = Place(zs)
        copies = Copies(send, recv, local)
        crossing = me.c != me.y
        greet(
            [me.at(x=to[0], z=to[1], y=to[2]) for to, _ in me.plane()]
            + [me.at(z=to[0], g=to[1]) for to, _ in me.column()]
            + [me.at(z=to[0], g=to[1], c=me.y, y=me.c) for to, _ in me.column()]
            + [me.sibling()],
            me.at(c=me.y, y=me.c),
            crossing,
        )

        flat = me.plane(everywhere=False)
        other = 1 - me.c
        order = [to for to, _ in me.plane()] + [(me.x, me.z, me.y)]
        w1_half = copies.push(g1.at[:, other], s1, me.sibling())
        w2_half = copies.push(g2.at[:, :, other], s2, me.sibling())
        k_half = [
            copies.push(
                dkv_ref.at[to[0], other, to[1], :, to[2]], kst.at[to[0], to[1], to[2]], me.sibling()
            )
            for to in order
        ]
        wm_half = copies.push(gm.at[:, other], sm, me.sibling())

        w1_half.wait_recv()

        def add1(index):
            x, z, g, y = index // (count * 2), index // (GROUPS * 2) % zs, index // 2 % GROUPS, index % 2
            s1[x, z, g, y] = total_of(s1[x, z, g, y], g1[x, me.c, z, g, y]).astype(low_type)

        loop(4 * count, add1)
        w1_push = [
            copies.push(s1.at[:, to[0], to[1], :], p1.at[slot], me.at(z=to[0], g=to[1]))
            for slot, (to, _) in enumerate(me.column())
        ]
        w2_half.wait_recv()

        def add2(index):
            z, g = index // GROUPS, index % GROUPS
            s2[z, g] = total_of(s2[z, g], g2[z, g, me.c]).astype(low_type)

        loop(count, add2)
        w2_push = [
            copies.push(
                s2.at[to[0], to[1]], p2.at[slot + 1], me.at(z=to[0], g=to[1], c=me.y, y=me.c)
            )
            for slot, (to, _) in enumerate(me.column())
        ]
        exchanged = pltpu.make_async_remote_copy(
            src_ref=s2.at[me.z, me.g],
            dst_ref=p2.at[0],
            send_sem=swap_send,
            recv_sem=swap_recv,
            device_id=me.at(c=me.y, y=me.c),
            device_id_type=MESH,
        )
        stays = pltpu.make_async_copy(s2.at[me.z, me.g], p2.at[0], swap_recv)

        @pl.when(crossing)
        def _():
            exchanged.start()

        @pl.when(jnp.logical_not(crossing))
        def _():
            stays.start()

        k_push = []
        for slot, to in enumerate(order):
            k_half[slot].wait_recv()

            def addk(g, to=to):
                kst[to[0], to[1], to[2], g] = total_of(
                    kst[to[0], to[1], to[2], g], dkv_ref[to[0], me.c, to[1], g, to[2]]
                ).astype(low_type)

            loop(GROUPS, addk)
            if slot < plane:
                k_push.append(
                    copies.push(
                        kst.at[to[0], to[1], to[2]],
                        dkv_out.at[slot],
                        me.at(x=to[0], z=to[1], y=to[2]),
                    )
                )
        wm_half.wait_recv()

        def addm(index):
            x, z, g, y = index // (count * 2), index // (GROUPS * 2) % zs, index // 2 % GROUPS, index % 2
            sm[x, z, g, y] = total_of(sm[x, z, g, y], gm[x, me.c, z, g, y]).astype(low_type)

        loop(4 * count, addm)
        wm_push = [
            copies.push(sm.at[to[0], :, :, to[2]], pm.at[slot], me.at(x=to[0], y=to[2]))
            for slot, (to, _) in enumerate(flat)
        ]
        keep = copies.keep(kst.at[me.x, me.z, me.y], dkv_out.at[plane])
        for copy in wm_push:
            copy.wait_recv()

        def addf(index):
            z, g = index // GROUPS, index % GROUPS
            fm[z, g] = total_of(sm[me.x, z, g, me.y], pm[0, z, g], pm[1, z, g], pm[2, z, g]).astype(
                low_type
            )

        loop(count, addf)
        wm_last = [
            copies.push(fm.at[to[0], to[1]], tm.at[slot], me.at(z=to[0], g=to[1]))
            for slot, (to, _) in enumerate(me.column())
        ]
        for copy in w1_push:
            copy.wait_recv()

        def addg(index):
            x, y = index // 2, index % 2
            f1[x, y] = total_of(
                s1[x, me.z, me.g, y], *[p1[slot, x, y] for slot in range(column)]
            ).astype(low_type)

        loop(4, addg)
        quarter = out1.at[me.x * 2 + me.y]
        w1_last = [
            copies.push(f1.at[to[0], to[2]], quarter, me.at(x=to[0], y=to[2])) for to, _ in flat
        ]
        keep1 = copies.keep(f1.at[me.x, me.y], quarter)

        @pl.when(crossing)
        def _():
            exchanged.wait_recv()
            exchanged.wait_send()

        @pl.when(jnp.logical_not(crossing))
        def _():
            stays.wait()

        for copy in w2_push:
            copy.wait_recv()
        out2[...] = total_of(*[p2[slot] for slot in range(column + 1)])
        for copy in wm_last:
            copy.wait_recv()
        outm[...] = total_of(fm[me.z, me.g], *[tm[slot] for slot in range(column)])
        for copy in w1_last + k_push:
            copy.wait_recv()
        keep.wait()
        keep1.wait()
        copies.finish()

    vmem = pltpu.VMEM
    return comm_call(
        body,
        "reduce_keys",
        8,
        [
            jax.ShapeDtypeStruct((plane + 1, GROUPS, n, width), low_type),
            jax.ShapeDtypeStruct((4, rows, columns), low_type),
            jax.ShapeDtypeStruct((tall, columns), wide),
            jax.ShapeDtypeStruct((rowsm, columns), wide),
        ],
        3 + (plane + 1) + 2 * column + plane + 3 + column + 3,
        2,
        (dkv, grad1, grad2, gradm),
        spaces=[vmem] * 4,
        out_spaces=[pl.ANY, pl.ANY, vmem, vmem],
        scratch=(
            pltpu.SemaphoreType.DMA,
            pltpu.SemaphoreType.DMA,
            vmem((2, zs, 2, GROUPS, n, width), low_type),
            vmem((2, zs, GROUPS, 2, rows, columns), low_type),
            vmem((column, 2, 2, rows, columns), low_type),
            vmem((2, 2, rows, columns), low_type),
            vmem((zs, GROUPS, tall, columns), low_type),
            vmem((column + 1, tall, columns), low_type),
            vmem((2, zs, GROUPS, 2, rowsm, columns), low_type),
            vmem((3, zs, GROUPS, rowsm, columns), low_type),
            vmem((zs, GROUPS, rowsm, columns), low_type),
            vmem((column, rowsm, columns), low_type),
        ),
    )


def reduce_tokens(zs, dx, gradq):
    rows, columns = gradq.shape[-2:]
    plane = 4 * zs - 1
    count = GROUPS * zs

    def body(dx_ref, gq, dx_out, outq, send, recv, local, sq, pq, fq):
        me = Place(zs)
        copies = Copies(send, recv, local)
        greet(
            [me.at(g=to) for to, _ in me.line()]
            + [me.at(x=to[0], z=to[1], y=to[2]) for to, _ in me.plane()]
            + [me.sibling()]
        )
        half = copies.push(gq.at[:, 1 - me.c], sq, me.sibling())
        arrivals = [
            copies.push(dx_ref.at[to], dx_out.at[me.g], me.at(g=to)) for to, _ in me.line()
        ]
        own = copies.keep(dx_ref.at[me.g], dx_out.at[me.g])
        half.wait_recv()

        def add1(index):
            x, z, g, y = index // (count * 2), index // (GROUPS * 2) % zs, index // 2 % GROUPS, index % 2
            sq[x, z, g, y] = total_of(sq[x, z, g, y], gq[x, me.c, z, g, y]).astype(low_type)

        loop(4 * count, add1)
        second = [
            copies.push(
                sq.at[to[0], to[1], :, to[2]], pq.at[slot], me.at(x=to[0], z=to[1], y=to[2])
            )
            for slot, (to, _) in enumerate(me.plane())
        ]
        for copy in second:
            copy.wait_recv()

        def add2(g):
            fq[g] = total_of(
                sq[me.x, me.z, g, me.y], *[pq[slot, g] for slot in range(plane)]
            ).astype(low_type)

        loop(GROUPS, add2)
        arrivals += [
            copies.push(fq.at[to], outq.at[me.g], me.at(g=to)) for to, _ in me.line()
        ]
        keep = copies.keep(fq.at[me.g], outq.at[me.g])
        for copy in arrivals:
            copy.wait_recv()
        own.wait()
        keep.wait()
        copies.finish()

    vmem = pltpu.VMEM
    return comm_call(
        body,
        "reduce_tokens",
        9,
        [
            jax.ShapeDtypeStruct(dx.shape, low_type),
            jax.ShapeDtypeStruct((GROUPS, rows, columns), low_type),
        ],
        1 + 2 * (GROUPS - 1) + plane,
        2,
        (dx, gradq),
        spaces=[pl.ANY, vmem],
        scratch=(
            vmem((2, zs, GROUPS, 2, rows, columns), low_type),
            vmem((plane, GROUPS, rows, columns), low_type),
            vmem((GROUPS, rows, columns), low_type),
        ),
    )


NEXT = (((1,), (1,)), ((), ()))
DOWN = (((0,), (0,)), ((), ()))


def attend_forward(queries, keys, bounds, low, high, tile, block):
    total_rows = queries.shape[0]

    def body(bounds_ref, q_ref, kv_ref, low_ref, high_ref, out_ref, keep_ref, lse_ref):
        def one(turn, unused):
            rows = pl.ds(pl.multiple_of(turn * tile, tile), tile)
            first, last = low_ref[rows, :], high_ref[rows, :]
            heads = [
                q_ref[rows, h * LANES : (h + 1) * LANES] * jnp.asarray(0.125, low_type)
                for h in range(LOCAL)
            ]

            def step(j, carry):
                begin = pl.multiple_of(j * block, block)
                place = begin + lax.broadcasted_iota(jnp.int32, (tile, block), 1)
                same = (place >= first) & (place < last)
                result = []
                for h in range(LOCAL):
                    top, total, mixed = carry[h]
                    kv = kv_ref[pl.ds(begin, block), h * LANES : (h + 1) * LANES]
                    scores = lax.dot_general(heads[h], kv, NEXT, preferred_element_type=wide)
                    scores = jnp.where(same, scores, mask_fill)
                    new_top = jnp.maximum(top, jnp.max(scores, axis=1, keepdims=True))
                    factor = jnp.exp(top - new_top)
                    powers = jnp.exp(scores - new_top)
                    total = total * factor + jnp.sum(powers, axis=1, keepdims=True)
                    mixed = mixed * factor + jnp.dot(
                        powers.astype(low_type), kv, preferred_element_type=wide
                    )
                    result.append((new_top, total, mixed))
                return tuple(result)

            start = tuple(
                (
                    jnp.full((tile, 1), lowest_start, wide),
                    jnp.zeros((tile, 1), wide),
                    jnp.zeros((tile, LANES), wide),
                )
                for _ in range(LOCAL)
            )
            done = lax.fori_loop(bounds_ref[turn, 0], bounds_ref[turn, 1], step, start)
            lane = lax.broadcasted_iota(jnp.int32, (tile, LANES), 1)
            upper = lane >= HEAD
            mixes = [mixed / total for _, total, mixed in done]
            turned = [pltpu.roll(mixed, HEAD, 1) for mixed in mixes]
            front = jnp.where(upper, mixes[1], turned[0])
            back = jnp.where(upper, 0.0, turned[2])
            both = jnp.concatenate([front, back], axis=1)
            keep_ref[rows, :] = both
            out_ref[rows, :] = both.astype(low_type)
            ends = [top + jnp.log(total) for top, total, _ in done]
            lse_ref[rows, :] = jnp.where(lane == 0, ends[0], jnp.where(lane == 1, ends[1], ends[2]))
            return unused

        lax.fori_loop(0, total_rows // tile, one, 0)

    vmem = pl.BlockSpec(memory_space=pltpu.VMEM)
    return pl.pallas_call(
        body,
        name="attend_forward",
        out_shape=(
            jax.ShapeDtypeStruct((total_rows, PACK), low_type),
            jax.ShapeDtypeStruct((total_rows, PACK), wide),
            jax.ShapeDtypeStruct((total_rows, LANES), wide),
        ),
        in_specs=[pl.BlockSpec(memory_space=pltpu.SMEM)] + [vmem] * 4,
        out_specs=(vmem,) * 3,
        compiler_params=pltpu.CompilerParams(vmem_limit_bytes=VMEM_LIMIT),
    )(bounds, queries, keys, low, high)


def attend_backward(queries, keys, grads, stats, bounds, tile, block):
    total_rows = queries.shape[0]
    tokens = keys.shape[0]

    def body(bounds_ref, q_ref, kv_ref, do_ref, stat_ref, dq_ref, dkv_ref, sums):
        h = pl.program_id(0)
        zeros = jnp.zeros((block, LANES), wide)

        def clear(j, unused):
            sums[pl.ds(pl.multiple_of(j * block, block), block), :] = zeros
            return unused

        lax.fori_loop(0, tokens // block, clear, 0)
        lane = lax.broadcasted_iota(jnp.int32, (tile, LANES), 1)
        upper = lane >= HEAD

        def one(turn, unused):
            rows = pl.ds(pl.multiple_of(turn * tile, tile), tile)
            q = q_ref[rows, :] * jnp.asarray(0.125, low_type)
            front = do_ref[rows, :LANES].astype(wide)
            back = do_ref[rows, LANES:].astype(wide)
            grad = jnp.where(h == 1, front, pltpu.roll(jnp.where(h == 0, front, back), HEAD, 1))
            grad = jnp.where(upper, grad, 0.0).astype(low_type)
            stat = stat_ref[turn, 0]
            first, last = stat[0:1, :], stat[1:2, :]
            lse, delta = stat[2:3, :], stat[3:4, :]

            def step(j, total):
                begin = pl.multiple_of(j * block, block)
                place = (begin + lax.broadcasted_iota(jnp.int32, (block, tile), 0)).astype(wide)
                same = (place >= first) & (place < last)
                kv = kv_ref[pl.ds(begin, block), :]
                scores = lax.dot_general(kv, q, NEXT, preferred_element_type=wide)
                probs = jnp.exp(jnp.where(same, scores, mask_fill) - lse)
                dots = lax.dot_general(kv, grad, NEXT, preferred_element_type=wide)
                score_grad = (probs * (dots - delta)).astype(low_type)
                sums[pl.ds(begin, block), :] += jnp.dot(
                    score_grad, q, preferred_element_type=wide
                ) + jnp.dot(probs.astype(low_type), grad, preferred_element_type=wide)
                return total + lax.dot_general(score_grad, kv, DOWN, preferred_element_type=wide)

            total = lax.fori_loop(
                bounds_ref[turn, 0], bounds_ref[turn, 1], step, jnp.zeros((tile, LANES), wide)
            )
            dq_ref[rows, :] = jnp.where(upper, 0.0, total * 0.125).astype(low_type)
            return unused

        lax.fori_loop(0, total_rows // tile, one, 0)

        def store(j, unused):
            part = pl.ds(pl.multiple_of(j * block, block), block)
            dkv_ref[part, :] = sums[part, :].astype(low_type)
            return unused

        lax.fori_loop(0, tokens // block, store, 0)

    return pl.pallas_call(
        body,
        name="attend_backward",
        grid=(LOCAL,),
        out_shape=(
            jax.ShapeDtypeStruct((total_rows, WIDE), low_type),
            jax.ShapeDtypeStruct((tokens, WIDE), low_type),
        ),
        in_specs=[
            pl.BlockSpec(memory_space=pltpu.SMEM),
            pl.BlockSpec((total_rows, LANES), lambda h: (0, h)),
            pl.BlockSpec((tokens, LANES), lambda h: (0, h)),
            pl.BlockSpec((total_rows, PACK), lambda h: (0, 0)),
            pl.BlockSpec((total_rows // tile, 1, 8, tile), lambda h: (0, h, 0, 0)),
        ],
        out_specs=(
            pl.BlockSpec((total_rows, LANES), lambda h: (0, h)),
            pl.BlockSpec((tokens, LANES), lambda h: (0, h)),
        ),
        scratch_shapes=[pltpu.VMEM((tokens, LANES), wide)],
        compiler_params=pltpu.CompilerParams(vmem_limit_bytes=VMEM_LIMIT),
    )(bounds, queries, keys, grads, stats)


def on_device(
    tokens,
    cotangent,
    doc_lengths,
    query_weight,
    query_bias,
    key_weight,
    value_weight,
    value_bias,
    mix_weight,
    mix_bias,
    early_gain,
    early_shift,
    inner_weight,
    inner_bias,
    outer_weight,
    outer_bias,
    final_gain,
    final_shift,
):
    n, depth = tokens.shape
    groups, cycle = lax.axis_size("au"), lax.axis_size("row")
    devices = groups * cycle
    zs = cycle // (2 * GROUPS)
    s = query_weight.shape[0]
    ff = inner_weight.shape[1]
    quarter = ff // 4
    e = outer_weight.shape[0]
    rows = GROUPS * n
    total_tokens = n * devices
    me = Place(zs)
    device = lax.axis_index("au") * cycle + lax.axis_index("row")
    w_me = me.x * 2 + me.y

    def by_head(weight):
        return weight.astype(low_type).reshape(-1, GROUPS, LOCAL, HEAD)

    def packed(query, key, value):
        kv = jnp.stack([key, value], axis=3).reshape(-1, GROUPS, WIDE)
        q = jnp.pad(query, ((0, 0), (0, 0), (0, 0), (0, HEAD))).reshape(-1, GROUPS, WIDE)
        return jnp.concatenate([kv, q], axis=2)

    slab = packed(by_head(query_weight), by_head(key_weight), by_head(value_weight))
    slab = jnp.transpose(slab, (1, 0, 2))
    small = jnp.concatenate(
        [
            vector.astype(low_type)
            for vector in (
                query_bias, value_bias, mix_bias, early_gain, early_shift,
                outer_bias, final_gain, final_shift, inner_bias,
            )
        ]
    )
    extra = -s % 8 or 8
    small = jnp.broadcast_to(
        jnp.pad(small, (0, 2 * WIDE - small.shape[0]))[None, None], (GROUPS, extra, 2 * WIDE)
    )
    slab = jnp.concatenate([slab, small], axis=1)
    tok_all, w_all = spread_tokens(zs, tokens, slab)
    tok_all = tok_all.reshape(rows, depth)
    w_qkv = w_all[..., :s, :].reshape(depth, 2 * WIDE)
    small = w_all[..., s, :].reshape(devices, 2 * WIDE)
    names = [small[:, i * s : (i + 1) * s].reshape(depth) for i in range(8)]
    q_bias, v_bias, m_bias, e_gain, e_shift, o_bias, f_gain, f_shift = names
    i_bias = small[:, 8 * s : 8 * s + e].reshape(4, quarter)[w_me].astype(wide)
    q_bias = q_bias.reshape(1, GROUPS, LOCAL, HEAD)
    v_bias = v_bias.reshape(1, GROUPS, LOCAL, HEAD)
    bias = packed(q_bias, jnp.zeros_like(q_bias), v_bias)[0, me.g].astype(wide)

    qkv = (jnp.dot(tok_all, w_qkv, preferred_element_type=wide) + bias).astype(low_type)
    queries = qkv[:, WIDE:]

    inner_slab = jnp.transpose(inner_weight.astype(low_type).reshape(s, 4, quarter), (1, 0, 2))
    kv_all, w1, w2, wm = spread_keys(
        zs,
        qkv[:, :WIDE].reshape(GROUPS, n, WIDE),
        inner_slab,
        outer_weight.astype(low_type),
        mix_weight.astype(low_type),
    )
    kv_all = kv_all.reshape(total_tokens, WIDE)
    w1 = w1.reshape(depth, quarter)
    w2 = w2.reshape(quarter, depth)
    wm = wm.reshape(depth, depth)

    tile, block = 128, 512
    count = doc_lengths.shape[0]
    upto = jnp.arange(count)[None, :] <= jnp.arange(count)[:, None]
    ends = jnp.sum(jnp.where(upto, doc_lengths[None, :], 0), axis=1)
    owners = ((me.x * 2 + me.c) * cycle + me.z * GROUPS * 2 + jnp.arange(GROUPS) * 2 + me.y) * n
    places = (owners[:, None] + jnp.arange(n)[None, :]).reshape(rows)
    before = ends[None, :] <= places[:, None]
    first = jnp.max(jnp.where(before, ends[None, :], 0), axis=1).astype(jnp.int32)
    last = jnp.min(jnp.where(before, total_tokens, ends[None, :]), axis=1).astype(jnp.int32)
    tiles = rows // tile
    bounds = jnp.stack(
        [
            first.reshape(tiles, tile)[:, 0] // block,
            (last.reshape(tiles, tile)[:, -1] + block - 1) // block,
        ],
        axis=1,
    )
    mixed, mixed_wide, lse = attend_forward(
        queries, kv_all, bounds, first[:, None], last[:, None], tile, block
    )
    mixed_tok = exchange_line(zs, 2, mixed.reshape(GROUPS, n, PACK))
    mixed_tok = jnp.transpose(mixed_tok[:, :, : LOCAL * HEAD], (1, 0, 2)).reshape(n, depth)

    attn = jnp.dot(mixed_tok, wm, preferred_element_type=wide) + m_bias.astype(wide)
    early, early_pull = jax.vjp(
        layer_norm, tokens.astype(wide) + attn, e_gain.astype(wide), e_shift.astype(wide)
    )
    early_all = gather_square(zs, 3, early.astype(low_type)).reshape(rows, depth)
    inner = jnp.dot(early_all, w1, preferred_element_type=wide) + i_bias
    act, gelu_pull = jax.vjp(gelu_exact, inner)
    act_low = act.astype(low_type)
    partial = jnp.dot(act_low, w2, preferred_element_type=wide).astype(low_type)
    partial = exchange_square(zs, 4, partial.reshape(2, 2, n, depth))
    branch = jnp.sum(partial.astype(wide), axis=(0, 1)) + o_bias.astype(wide)
    result, final_pull = jax.vjp(
        layer_norm, early + branch, f_gain.astype(wide), f_shift.astype(wide)
    )
    output = result.astype(low_type)
    final_grads = final_pull(cotangent.astype(wide))
    branch_grad = final_grads[0].astype(low_type)
    outer_bias_grad = jnp.sum(branch_grad.astype(wide), axis=0)
    branch_all = gather_square(zs, 5, branch_grad).reshape(rows, depth)
    act_grad = jnp.einsum("td,fd->tf", branch_all, w2, preferred_element_type=wide)
    inner_grad = gelu_pull(act_grad)[0].astype(low_type)
    partial = jnp.einsum("tf,df->td", inner_grad, w1, preferred_element_type=wide).astype(low_type)
    partial = exchange_square(zs, 6, partial.reshape(2, 2, n, depth))
    grad2 = jnp.einsum("tf,td->fd", act_low, branch_all, preferred_element_type=wide)
    grad1 = jnp.einsum("td,tf->df", early_all, inner_grad, preferred_element_type=wide)
    inner_bias_grad = jnp.sum(inner_grad.astype(wide), axis=0)
    early_grad = final_grads[0] + jnp.sum(partial.astype(wide), axis=(0, 1))
    early_grads = early_pull(early_grad)
    attn_grad = early_grads[0].astype(low_type)
    mixed_grad = jnp.einsum("td,cd->tc", attn_grad, wm, preferred_element_type=wide)
    mixed_grad = jnp.transpose(
        mixed_grad.astype(low_type).reshape(n, GROUPS, LOCAL * HEAD), (1, 0, 2)
    )
    mixed_grad = jnp.pad(mixed_grad, ((0, 0), (0, 0), (0, PACK - LOCAL * HEAD)))
    grad_all = exchange_line(zs, 7, mixed_grad).reshape(rows, PACK)
    gradm = jnp.einsum("tc,td->cd", mixed_tok, attn_grad, preferred_element_type=wide)
    mix_bias_grad = jnp.sum(attn_grad.astype(wide), axis=0)

    delta = jnp.sum(
        (grad_all.astype(wide) * mixed_wide)[:, : LOCAL * HEAD].reshape(rows, LOCAL, HEAD), axis=2
    )

    def as_stat(values):
        return jnp.transpose(values.reshape(tiles, tile, LOCAL), (0, 2, 1))

    def same_stat(values):
        return jnp.broadcast_to(
            values.astype(wide).reshape(tiles, 1, tile), (tiles, LOCAL, tile)
        )

    stats = jnp.stack(
        [same_stat(first), same_stat(last), as_stat(lse[:, :LOCAL]), as_stat(delta)], axis=2
    )
    stats = jnp.pad(stats, ((0, 0), (0, 0), (0, 4), (0, 0)))
    query_grad, dkv = attend_backward(queries, kv_all, grad_all, stats, bounds, tile, block)

    def slabs(grad, extras):
        grad = grad.astype(low_type).reshape(devices, s, -1)
        rest = -s % 8
        rest += 0 if rest >= extras.shape[0] else 8
        extras = jnp.concatenate(
            [extras.astype(low_type), jnp.zeros((rest - extras.shape[0], extras.shape[1]), low_type)]
        )
        extras = jnp.broadcast_to(extras[None], (devices,) + extras.shape)
        return jnp.concatenate([grad, extras], axis=1).reshape(2, 2, zs, GROUPS, 2, s + rest, -1)

    mix_extras = jnp.stack(
        [
            mix_bias_grad, early_grads[1], early_grads[2],
            outer_bias_grad, final_grads[1], final_grads[2],
        ]
    )
    dkv, out1, out2, outm = reduce_keys(
        zs,
        dkv.reshape(2, 2, zs, GROUPS, 2, n, WIDE),
        slabs(grad1, inner_bias_grad[None]),
        grad2.astype(low_type).reshape(zs, GROUPS, 2, e, depth),
        slabs(gradm, mix_extras),
    )
    key_grad = jnp.sum(dkv.astype(wide), axis=0).astype(low_type).reshape(rows, WIDE)
    grads = jnp.concatenate([key_grad, query_grad], axis=1)
    gradq = jnp.einsum("tc,td->cd", tok_all, grads, preferred_element_type=wide)
    bias_grad = jnp.sum(grads.astype(wide), axis=0)
    partial = jnp.einsum("td,cd->tc", grads, w_qkv, preferred_element_type=wide).astype(low_type)
    partial, outq = reduce_tokens(
        zs, partial.reshape(GROUPS, n, depth), slabs(gradq, bias_grad[None])
    )
    input_grad = early_grads[0] + jnp.sum(partial.astype(wide), axis=0)

    def own(vector, count):
        return lax.dynamic_slice_in_dim(vector, device * count, count, 0).astype(wide)

    outq = outq.astype(wide)
    kv_out = outq[:, :, :WIDE].reshape(GROUPS, -1, LOCAL, 2, HEAD)
    q_out = outq[:, :, WIDE:].reshape(GROUPS, -1, LOCAL, 2, HEAD)[:, :, :, 0]

    def unpacked(values):
        return jnp.transpose(values, (1, 0, 2, 3)).reshape(-1, depth)

    q_out, k_out, v_out = unpacked(q_out), unpacked(kv_out[:, :, :, 0]), unpacked(kv_out[:, :, :, 1])
    inner_out = jnp.transpose(out1[:, :s], (1, 0, 2)).reshape(s, ff).astype(wide)
    return (
        output,
        input_grad.astype(low_type),
        q_out[:s],
        own(q_out[s], s),
        k_out[:s],
        v_out[:s],
        own(v_out[s], s),
        outm[:s],
        own(outm[s], s),
        own(outm[s + 1], s),
        own(outm[s + 2], s),
        inner_out,
        own(out1[:, s].reshape(ff), e),
        out2,
        own(outm[s + 3], s),
        own(outm[s + 4], s),
        own(outm[s + 5], s),
    )


def solution(mesh):
    both = P(("au", "row"), None)
    flat = P(("au", "row"))
    in_specs = (
        both, both, P(), both, flat, both, both, flat, both, flat, flat, flat,
        both, flat, both, flat, flat, flat,
    )
    out_specs = (
        both, both, both, flat, both, both, flat, both, flat, flat, flat,
        both, flat, both, flat, flat, flat,
    )
    return jax.shard_map(
        on_device, mesh=mesh, in_specs=in_specs, out_specs=out_specs, check_vma=False
    )
```

time: 1260 us -> 339 us (0.27)
  waiting for transfers between devices: 732 us -> 0 us
  Pallas kernels: 0 us -> 261 us
  blocking collectives: 182 us -> 0 us
  matrix products: 175 us -> 23 us
  local copies, waits for them, and re-layouts: 70.2 us -> 23.1 us
  other arithmetic: 57.6 us -> 31.8 us
  loops' own time: 16.5 us -> 0 us
  between operations: 14.9 us -> 1.56 us
    all_gather x10 -> x0, waiting for transfers between devices: 289 us -> none  [the longest x1 57.8 us: on_device(): lax.all_gather(outer_weight.astype(low_type), ('au', 'row'), axis=0, tile...]
    reduce_scatter x3 -> x0, waiting for transfers between devices: 283 us -> none  [the longest x1 142 us: on_device(): lax.psum_scatter(outer_grad, ('au', 'row'), scatter_dimension=0, tiled=True)]
    pallas_call x0 -> x12, Pallas kernels: none -> 261 us  [the longest x10 212 us: comm_call(): pl.pallas_call(body, name=name, out_shape=tuple(outs), in_specs=[pl.Block...]
    dot_general x73 -> x11, matrix products: 173 us -> 22.6 us  [the longest x1 7.15 us: on_device(): inner = jnp.dot(early_all, w1, preferred_element_type=wide) + i_bias]
    unnamed x19 -> x0, waiting for transfers between devices: 150 us -> none
    unnamed x2 -> x0, blocking collectives: 77.1 us -> none
    all_gather x2 -> x0, blocking collectives: 65 us -> none  [the longest x1 32.5 us: on_device(): lax.all_gather(delta, 'row', axis=0, tiled=True)]
    all_to_all x5 -> x0, blocking collectives: 39.6 us -> none  [the longest x1 8.32 us: on_device(): lax.all_to_all(key_sum.astype(low_type).reshape(local_rows, width), 'au',...]
  transfers between devices with their start and end apart: 19 -> 0, of which waited for: 13 -> 0; matrix products, arithmetic and copies ran while one was open for 23% -> 0% of each run, Pallas kernels for 0% -> 0%
where the time goes in v1:
time: 339 us; the launch traced here: 340 us
  Pallas kernels  261 us (77%)
  other arithmetic  31.8 us (9%)
  local copies, waits for them, and re-layouts  23.1 us (7%)
  matrix products  23 us (7%)
    pallas_call x10, Pallas kernels, comm_call(): pl.pallas_call(body, name=name, out_shape=tuple(outs), in_specs=[pl.Block...  212 us
    pallas_call x1, Pallas kernels, attend_backward(): pl.pallas_call(body, name='attend_backward', grid=(LOCAL,), out_shape=(ja...  28.2 us
    pallas_call x1, Pallas kernels, attend_forward(): pl.pallas_call(body, name='attend_forward', out_shape=(jax.ShapeDtypeStru...  20 us
    dot_general x1, matrix products, on_device(): inner = jnp.dot(early_all, w1, preferred_element_type=wide) + i_bias  7.15 us

profile of v1, /device:TPU:0, one launch (start us, length us, event | category | flops | bytes accessed | tf_op | source)
XLA Modules:
  0.0 340.1 jit_solution(6992955071024820284)
XLA Ops:
  7.7 1.0 reduce.5
  9.5 0.9 convert_element_type.260
  10.4 0.9 convert_element_type.258
  11.3 0.9 convert_element_type.259
  12.1 1.5 convert_element_type.275.wms
  16.9 0.9 copy.66.high_ref
  17.7 0.9 copy.65.low_ref
  18.6 28.0 %spread_tokens.1 = (bf16[4,128,768]{2,1,0:T(8,128)(2,1)}, bf16[2,2,1,4,2,32,768]{6,5,4,3,2,1,0:T(8,128)(2,1)}) custom-call(bf16[128,768]{1,0:T(8,128)(2,1)} %tok.1, bf16[4,32,768]{2,1,0:T(8,128)(2,1)} %pad_maximum_fusion.7.piece), custom_call_target="tpu_custom_call" | custom-call | tf_op jit(solution)/shard_map/spread_tokens/pallas_call | solution.py:140
  46.6 1.4 slice_reduce_fusion
  48.0 1.4 slice.124
  50.6 0.8 add_convert_fusion.1
  51.4 1.0 fusion.37
  52.3 39.5 %spread_keys.1 = (bf16[2,2,1,4,2,128,384]{6,5,4,3,2,1,0:T(8,128)(2,1)}, bf16[2,2,1,4,2,24,768]{6,5,4,3,2,1,0:T(8,128)(2,1)}, bf16[1,4,2,96,768]{4,3,2,1,0:T(8,128)(2,1)}, bf16[2,2,1,4,2,24,768]{6,5,4,3,2,1,0:T(8,128)(2,1)}) custom-call(bf16[4,128,384]{2,1,0:T(8,128)(2,1)} %bitcast.119, bf16[4,24,768]{2,1,0:T(8,128)(2,1)} %bitcast.143, ...), custom_call_target="tpu_custom_call" | custom-call | tf_op jit(solution)/shard_map/spread_keys/pallas_call | solution.py:140
  91.9 20.0 %attend_forward.1 = (bf16[512,256]{1,0:T(8,128)(2,1)}, f32[512,256]{1,0:T(8,128)}, f32[512,128]{1,0:T(8,128)}) custom-call(s32[4,2]{1,0:T(4,128)} %pad_add_fusion.bounds_ref, bf16[512,384]{1,0:T(8,128)(2,1)} %get-tuple-element.74.q_ref, bf16[4096,384]{1,0:T(8,128)(2,1)} %bitcast.108, s32[512,1]{1,0:T(8,128)} %copy.65.low_ref, s32[512,1]{1,0:T(8,128)} %copy.66.high_ref), custom_call_target="tpu_custom_call" | custom-call | tf_op jit(solution)/shard_map/attend_forward/pallas_call | solution.py:758
  111.8 8.0 %exchange_line.2 = bf16[4,128,256]{2,1,0:T(8,128)(2,1)} custom-call(bf16[4,128,256]{2,1,0:T(8,128)(2,1)} %bitcast.146), custom_call_target="tpu_custom_call" | custom-call | tf_op jit(solution)/shard_map/exchange_line/pallas_call | solution.py:140
  119.9 1.0 slice_bitcast_fusion
  121.0 1.1 copy.82
  123.4 0.8 fusion.11.source
  124.2 11.0 %gather_square.2 = bf16[2,2,128,768]{3,2,1,0:T(8,128)(2,1)} custom-call(bf16[128,768]{1,0:T(8,128)(2,1)} %fusion.11.source), custom_call_target="tpu_custom_call" | custom-call | tf_op jit(solution)/shard_map/gather_square/pallas_call | solution.py:140
  135.2 7.1 %multiply_convert_fusion = (bf16[512,768]{1,0:T(8,128)(2,1)S(1)}, f32[512,768]{1,0:T(8,128)}, f32[512,768]{1,0:T(8,128)}) fusion(f32[768]{0:T(1024)S(1)} %convert_reduce_fusion.3, bf16[512,768]{1,0:T(8,128)(2,1)} %bitcast.132, bf16[768,768]{1,0:T(8,128)(2,1)} %bitcast.153), kind=kOutput, calls=%fused_computation.9 | convolution fusion | flops 629932032 | bytes 5901312 | tf_op jit(solution)/shard_map/dot_general | solution.py:965
  142.4 1.7 convolution_convert_fusion.6
  144.1 12.7 %exchange_square.2 = bf16[2,2,128,768]{3,2,1,0:T(8,128)(2,1)} custom-call(bf16[2,2,128,768]{3,2,1,0:T(8,128)(2,1)} %bitcast.131), custom_call_target="tpu_custom_call" | custom-call | tf_op jit(solution)/shard_map/exchange_square/pallas_call | solution.py:140
  156.8 1.3 convert_reduce_fusion.2
  158.9 0.9 fusion.34
  159.8 0.8 fusion.30
  160.6 13.0 %gather_square.3 = bf16[2,2,128,768]{3,2,1,0:T(8,128)(2,1)} custom-call(bf16[128,768]{1,0:T(8,128)(2,1)} %get-tuple-element.59.source), custom_call_target="tpu_custom_call" | custom-call | tf_op jit(solution)/shard_map/gather_square/pallas_call | solution.py:140
  173.6 3.7 %fusion.32 = (bf16[768]{0:T(1024)(128)(2,1)S(1)}, bf16[512,768]{1,0:T(8,128)(2,1)S(1)}) fusion(f32[512,768]{1,0:T(8,128)} %get-tuple-element.72, f32[512,768]{1,0:T(8,128)} %get-tuple-element.96, bf16[512,768]{1,0:T(8,128)(2,1)} %bitcast.135, bf16[768,768]{1,0:T(8,128)(2,1)} %bitcast.155), kind=kOutput, calls=%fused_computation.139 | convolution fusion | flops 609877248 | bytes 5899776 | tf_op jit(solution)/shard_map/td,fd->tf/dot_general | solution.py:979
  177.4 1.8 convolution_convert_fusion.2
  179.2 1.7 convolution_convert_fusion.5
  180.9 12.1 %exchange_square.3 = bf16[2,2,128,768]{3,2,1,0:T(8,128)(2,1)} custom-call(bf16[2,2,128,768]{3,2,1,0:T(8,128)(2,1)} %bitcast.130), custom_call_target="tpu_custom_call" | custom-call | tf_op jit(solution)/shard_map/exchange_square/pallas_call | solution.py:140
  193.1 1.3 convert_reduce_fusion.1
  196.8 8.6 %exchange_line.3 = bf16[4,128,256]{2,1,0:T(8,128)(2,1)} custom-call(bf16[4,128,256]{2,1,0:T(8,128)(2,1)} %pad.27.source), custom_call_target="tpu_custom_call" | custom-call | tf_op jit(solution)/shard_map/exchange_line/pallas_call | solution.py:140
  205.3 1.2 slice_multiply_fusion
  207.4 28.2 %attend_backward.1 = (bf16[512,384]{1,0:T(8,128)(2,1)}, bf16[4096,384]{1,0:T(8,128)(2,1)}) custom-call(s32[4,2]{1,0:T(4,128)} %pad_add_fusion.bounds_ref, bf16[512,384]{1,0:T(8,128)(2,1)} %get-tuple-element.74.q_ref, bf16[4096,384]{1,0:T(8,128)(2,1)} %bitcast.109, bf16[512,256]{1,0:T(8,128)(2,1)} %bitcast.115, f32[4,3,8,128]{3,2,1,0:T(8,128)} %select_maximum_fusion.stat_ref), custom_call_target="tpu_custom_call" | custom-call | tf_op jit(solution)/shard_map/attend_backward/pallas_call | solution.py:828
  235.7 2.2 convolution_convert_fusion.3
  237.9 1.4 pad_maximum_fusion.g1
  239.7 1.4 pad_maximum_fusion.1.gm
  241.0 54.0 %reduce_keys.1 = (bf16[4,4,128,384]{3,2,1,0:T(8,128)(2,1)}, bf16[4,32,768]{2,1,0:T(8,128)(2,1)}, f32[96,768]{1,0:T(8,128)}, f32[32,768]{1,0:T(8,128)}) custom-call(bf16[2,2,1,4,2,128,384]{6,5,4,3,2,1,0:T(8,128)(2,1)} %bitcast.113, bf16[2,2,1,4,2,32,768]{6,5,4,3,2,1,0:T(8,128)(2,1)} %pad_maximum_fusion.g1, bf16[1,4,2,96,768]{4,3,2,1,0:T(8,128)(2,1)} %bitcast.123, ...), custom_call_target="tpu_custom_call" | custom-call | tf_op jit(solution)/shard_map/reduce_keys/pallas_call | solution.py:140
  295.1 1.8 reduce_sum.258
  296.9 1.7 convolution_convert_fusion.4
  298.8 0.8 convolution_convert_fusion
  305.3 1.4 pad_maximum_fusion.2.gq
  306.7 25.4 %reduce_tokens.1 = (bf16[4,128,768]{2,1,0:T(8,128)(2,1)}, bf16[4,32,768]{2,1,0:T(8,128)(2,1)}) custom-call(bf16[4,128,768]{2,1,0:T(8,128)(2,1)} %bitcast.134, bf16[2,2,1,4,2,32,768]{6,5,4,3,2,1,0:T(8,128)(2,1)} %pad_maximum_fusion.2.gq), custom_call_target="tpu_custom_call" | custom-call | tf_op jit(solution)/shard_map/reduce_tokens/pallas_call | solution.py:140
  332.1 1.3 convert_reduce_fusion
  333.5 0.8 add_convert_fusion.2
  335.7 0.8 slice.151
  336.6 0.8 slice.148
  338.6 0.8 slice.143
  (179 shorter events, 27.0 us)
Async XLA Ops:
  8.7 6.8 %copy-start.10 = (f32[24,3072]{1,0:T(8,128)S(1)}, f32[24,3072]{1,0:T(8,128)}, u32[]{:S(2)}) copy-start(f32[24,3072]{1,0:T(8,128)} %param.30) | copy-start | bytes 884740
  13.8 2.4 copy-start.11
  46.6 3.9 %copy-start.19 = (bf16[4,128,768]{2,1,0:T(8,128)(2,1)S(1)}, bf16[4,128,768]{2,1,0:T(8,128)(2,1)}, u32[]{:S(2)}) copy-start(bf16[4,128,768]{2,1,0:T(8,128)(2,1)} %get-tuple-element.34) | copy-start | bytes 2359300
  49.4 2.0 copy-start.4
  111.8 10.3 %copy-start = (bf16[2,2,1,4,2,24,768]{6,5,4,3,2,1,0:T(8,128)(2,1)S(1)}, bf16[2,2,1,4,2,24,768]{6,5,4,3,2,1,0:T(8,128)(2,1)}, u32[]{:S(2)}) copy-start(bf16[2,2,1,4,2,24,768]{6,5,4,3,2,1,0:T(8,128)(2,1)} %get-tuple-element.38) | copy-start | bytes 3538948
  111.8 10.4 %copy-start.6 = (bf16[128,768]{1,0:T(8,128)(2,1)S(1)}, bf16[128,768]{1,0:T(8,128)(2,1)}, u32[]{:S(2)}) copy-start(bf16[128,768]{1,0:T(8,128)(2,1)} %tok.1) | copy-start | bytes 589828
  121.0 1.2 copy-start.1
  122.8 0.5 copy-start.15
  135.2 7.2 %copy-start.18 = (bf16[1,4,2,96,768]{4,3,2,1,0:T(8,128)(2,1)S(1)}, bf16[1,4,2,96,768]{4,3,2,1,0:T(8,128)(2,1)}, u32[]{:S(2)}) copy-start(bf16[1,4,2,96,768]{4,3,2,1,0:T(8,128)(2,1)} %get-tuple-element.40) | copy-start | bytes 3538948
  142.4 1.7 copy-start.22
  156.8 1.8 copy-start.3
  173.6 3.8 %copy-start.8 = (bf16[2,2,128,768]{3,2,1,0:T(8,128)(2,1)S(1)}, bf16[2,2,128,768]{3,2,1,0:T(8,128)(2,1)}, u32[]{:S(2)}) copy-start(bf16[2,2,128,768]{3,2,1,0:T(8,128)(2,1)} %gather_square.3) | copy-start | bytes 2359300
  173.6 3.8 %copy-start.23 = (bf16[512,768]{1,0:T(8,128)(2,1)S(1)}, bf16[512,768]{1,0:T(8,128)(2,1)}, u32[]{:S(2)}) copy-start(bf16[512,768]{1,0:T(8,128)(2,1)} %copy-done.22) | copy-start | bytes 2359300
  177.4 1.9 copy-start.21
  177.4 1.9 copy-start.17
  193.1 1.6 copy-start.16
  237.8 1.4 copy-start.2
  295.1 1.8 copy-start.5
  295.1 1.8 copy-start.9
  296.9 1.9 copy-start.20
  298.8 0.9 copy-start.13
  298.8 1.6 copy-start.14
  332.1 2.1 copy-start.7
  336.5 2.9 copy-start.12

commit v2 on v1

--- a/solution.py
+++ b/solution.py
@@ -2,6 +2,7 @@
 
 import jax
 import jax.numpy as jnp
+import numpy as np
 from jax import lax
 from jax.experimental import pallas as pl
 from jax.experimental.pallas import tpu as pltpu
@@ -849,7 +850,723 @@
     )(bounds, queries, keys, grads, stats)
 
 
-def on_device(
+class Spot(Place):
+    def __init__(self):
+        super().__init__(1)
+        self.half = self.g // 2
+        self.a = self.x * 2 + self.c
+        self.p = (self.x + self.c) % 2
+        self.selfish = self.g % 2 == self.p
+        self.crossing = self.c != self.y
+
+    def square(self):
+        return [(to[0], to[2]) for to, _ in self.plane()]
+
+    def readers(self):
+        result = []
+        for k in range(GROUPS):
+            g = (self.g + k) % GROUPS
+            result.append((g, self.at(x=(self.g + self.c) % 2, g=g)))
+        return result
+
+    def owners(self):
+        result = []
+        for du in range(2):
+            for dv in range(2):
+                u, v = (self.x + du) % 2, (self.half + dv) % 2
+                result.append((u * 2 + v, self.at(x=u, g=2 * v + self.p)))
+        return result
+
+    def slot(self):
+        return self.x * 2 + self.half
+
+
+def count_of(flag):
+    return jnp.where(flag, 1, 0)
+
+
+def announce(always, maybe):
+    barrier = pltpu.get_barrier_semaphore()
+    for device in always:
+        pl.semaphore_signal(barrier, inc=1, device_id=device, device_id_type=MESH)
+    for flag, device in maybe:
+
+        @pl.when(flag)
+        def _(device=device):
+            pl.semaphore_signal(barrier, inc=1, device_id=device, device_id_type=MESH)
+
+    total = len(always)
+    for flag, _ in maybe:
+        total = total + count_of(flag)
+    return barrier, total
+
+
+class Scatter:
+    def __init__(self, send, recv, here):
+        self.send, self.recv, self.here = send, recv, here
+        self.copies = []
+
+    def start(self, pieces, target, slot):
+        for index, (source, device) in enumerate(pieces):
+            copy = pltpu.make_async_remote_copy(
+                src_ref=source,
+                dst_ref=target,
+                send_sem=self.send.at[index],
+                recv_sem=self.recv.at[slot],
+                device_id=device,
+                device_id_type=MESH,
+            )
+            self.copies.append(copy)
+            if index:
+                copy.start()
+                continue
+            stay = pltpu.make_async_copy(source, target, self.recv.at[slot])
+
+            @pl.when(self.here)
+            def _(stay=stay):
+                stay.start()
+
+            @pl.when(jnp.logical_not(self.here))
+            def _(copy=copy):
+                copy.start()
+
+    def arrived(self, slot, target):
+        pltpu.make_async_copy(target, target, self.recv.at[slot]).wait()
+
+    def finish(self):
+        for copy in self.copies[1:]:
+            copy.wait_send()
+
+        @pl.when(jnp.logical_not(self.here))
+        def _():
+            self.copies[0].wait_send()
+
+
+SMALL = 16
+
+
+def first_tables(s, e, width):
+    column = np.arange(width)
+    rows = [column % s, column // s, column % e, column // e]
+    return np.stack(rows + [np.zeros_like(column)] * 4).astype(np.int32)
+
+
+def first_kernel(tokens, wq, wk, wv, vectors, inner, outer, mix):
+    n, depth = tokens.shape
+    s, e = wq.shape[0], outer.shape[0]
+    quarter = inner.shape[1] // 4
+    cols = 2 * WIDE + LANES
+    tables = jnp.asarray(first_tables(s, e, 2 * WIDE))
+    count = len(vectors)
+
+    def body(*refs):
+        tok, wq_ref, wk_ref, wv_ref, tab = refs[:5]
+        vecs = refs[5 : 5 + count]
+        w1f, w2f, wmf = refs[5 + count : 8 + count]
+        (
+            tok_out, q_out, wqkv_out, vec_out, kv_all, w1, w2, wm,
+            send, recv, local, tok_send, tok_recv, swap_send, swap_recv,
+            slab, toks, weights, kv_own, q_own, w1s, w2s, wms, vec, few,
+        ) = refs[8 + count :]
+        me = Spot()
+        copies = Copies(send, recv, local)
+        square = me.square()
+        line = [to for to, _ in me.line()]
+        sources = [device for _, device in me.owners()]
+        swapped = [me.at(g=to, c=me.y, y=me.c) for to in [me.g] + line]
+        barrier, expected = announce(
+            [me.at(x=x, y=y) for x, y in square]
+            + [me.at(g=to) for to in line]
+            + swapped[1:]
+            + sources[1:]
+            + [me.sibling()],
+            [(jnp.logical_not(me.selfish), sources[0]), (me.crossing, swapped[0])],
+        )
+        lane = lax.broadcasted_iota(jnp.int32, (s, LANES), 1)
+        lower = lane < HEAD
+        for head in range(HEADS):
+            pair = slice(head // 2 * LANES, head // 2 * LANES + LANES)
+            q, k, v = wq_ref[:, pair], wk_ref[:, pair], wv_ref[:, pair]
+            if head % 2:
+                q, k = pltpu.roll(q, HEAD, 1), pltpu.roll(k, HEAD, 1)
+            else:
+                v = pltpu.roll(v, HEAD, 1)
+            g, h = head // LOCAL, head % LOCAL
+            slab[g, :, h * LANES : (h + 1) * LANES] = jnp.where(lower, k, v).astype(low_type)
+            slab[g, :, WIDE + h * LANES : WIDE + (h + 1) * LANES] = jnp.where(lower, q, 0.0).astype(
+                low_type
+            )
+        few[...] = jnp.zeros((s, LANES), wide)
+        for index in range(count):
+            few[index : index + 1, : vecs[index].shape[1]] = vecs[index][...]
+        small = few[...]
+        for g in range(GROUPS):
+            slab[g, :, 2 * WIDE :] = small.astype(low_type)
+        pl.semaphore_wait(barrier, expected)
+
+        view = weights
+        place = view.at[me.a, me.g, me.y]
+        slab_first = [copies.push(slab.at[to], place, me.at(g=to)) for to in line]
+        slab_own = copies.keep(slab.at[me.g], place)
+        tokens_go = Scatter(tok_send, tok_recv, me.selfish)
+        tokens_go.start([(tok, device) for _, device in me.readers()], toks.at[me.slot()], me.slot())
+        for w in range(4):
+            w1s[w] = w1f[:, w * quarter : (w + 1) * quarter].astype(low_type)
+        w2s[...] = w2f[...].astype(low_type)
+        wms[...] = wmf[...].astype(low_type)
+        place = w1.at[me.x, me.c, me.g, me.y]
+        w1_first = [
+            copies.push(w1s.at[x * 2 + y], place, me.at(x=x, y=y)) for x, y in square
+        ]
+        w1_own = copies.keep(w1s.at[me.x * 2 + me.y], place)
+        wm_own = copies.keep(wms, wm.at[me.x, me.c, me.g, me.y])
+
+        arrivals, weight_arrivals = [], []
+        slab_own.wait()
+        for copy in slab_first:
+            copy.wait_recv()
+        block = view.at[me.a, :, me.y]
+        slab_second = [copies.push(block, block, me.at(x=x, y=y)) for x, y in square]
+        weight_arrivals.append(copies.push(block, block, me.sibling()))
+        for copy, (x, y) in zip(slab_second, square):
+            copy.wait_recv()
+            block = view.at[x * 2 + me.c, :, y]
+            weight_arrivals.append(copies.push(block, block, me.sibling()))
+        w1_own.wait()
+        for copy in w1_first:
+            copy.wait_recv()
+        for copy in weight_arrivals:
+            copy.wait_recv()
+
+        table = tab[...]
+
+        def spread(pieces, within, owner):
+            count = pieces.shape[0] * SMALL
+            item = lax.broadcasted_iota(jnp.int32, (count, 2 * WIDE), 0)
+            index = lax.broadcasted_iota(jnp.int32, (LANES, 2 * WIDE), 0)
+            chosen = jnp.where(index == within, 1.0, 0.0).astype(low_type)
+            pieces = pieces.astype(wide).reshape(count, LANES).astype(low_type)
+            found = jnp.dot(pieces, chosen, preferred_element_type=wide)
+            found = jnp.where((item >> 4) == owner, found, 0.0)
+            return jnp.sum(found.reshape(count // SMALL, SMALL, 2 * WIDE), axis=0)
+
+        every = spread(
+            view[:, :, :, :SMALL, 2 * WIDE :].reshape(32, SMALL, LANES), table[0:1], table[1:2]
+        )
+        w_me = me.x * 2 + me.y
+        inner_bias = spread(
+            view[w_me, :, :, :SMALL, 2 * WIDE :].reshape(8, SMALL, LANES), table[2:3], table[3:4]
+        )
+        rows16 = lax.broadcasted_iota(jnp.int32, (SMALL, 2 * WIDE), 0)
+        vec[...] = jnp.where(rows16 == 8, inner_bias, every)
+        turned = pltpu.roll(every, 2 * WIDE - me.g * LOCAL * HEAD, 1)
+        lower = lax.broadcasted_iota(jnp.int32, (1, LANES), 1) < HEAD
+        biases = [[], []]
+        for h in range(LOCAL):
+            pair = slice(h // 2 * LANES, h // 2 * LANES + LANES)
+            q, v = turned[0:1, pair], turned[1:2, pair]
+            if h % 2:
+                q = pltpu.roll(q, HEAD, 1)
+            else:
+                v = pltpu.roll(v, HEAD, 1)
+            biases[0].append(jnp.where(lower, 0.0, v))
+            biases[1].append(jnp.where(lower, q, 0.0))
+        bias = jnp.concatenate(biases[0] + biases[1], axis=1)
+
+        slots = [(u * 2 + v) for u in range(2) for v in range(2)]
+        for slot in slots:
+            tokens_go.arrived(slot, toks.at[slot])
+        block = w1.at[:, me.c, me.g, :]
+        w1_second = [copies.push(block, block, me.at(g=to)) for to in line]
+        wm_first = [
+            copies.push(wms, wm.at[me.x, me.c, me.g, me.y], me.at(g=to)) for to in line
+        ]
+        w2_place = w2.at[me.g, me.y]
+        w2_first = [
+            copies.push(w2s, w2_place, device) for device in swapped[1:]
+        ]
+        exchanged = pltpu.make_async_remote_copy(
+            src_ref=w2s,
+            dst_ref=w2_place,
+            send_sem=swap_send,
+            recv_sem=swap_recv,
+            device_id=swapped[0],
+            device_id_type=MESH,
+        )
+        stays = pltpu.make_async_copy(w2s, w2_place, swap_recv)
+
+        @pl.when(me.crossing)
+        def _():
+            exchanged.start()
+
+        @pl.when(jnp.logical_not(me.crossing))
+        def _():
+            stays.start()
+
+        matrix = weights[:, :, :, :, : 2 * WIDE].reshape(depth, 2 * WIDE)
+        made = jnp.dot(
+            toks[...].reshape(GROUPS * n, depth), matrix, preferred_element_type=wide
+        )
+        made = (made + bias).astype(low_type).reshape(GROUPS, n, 2 * WIDE)
+        for slot in slots:
+            kv_own[slot // 2, slot % 2] = made[slot, :, :WIDE]
+            q_own[slot] = made[slot, :, WIDE:]
+        mine = kv_all.at[:, me.c, :, me.p, me.y]
+        kv_first = [copies.push(kv_own, mine, me.at(x=x, y=y)) for x, y in square]
+        arrivals.append(copies.push(kv_own, mine, me.sibling()))
+        block = w1.at[:, me.c, me.g, :]
+        arrivals.append(copies.push(block, block, me.sibling()))
+        kept = [
+            copies.keep(kv_own, mine),
+            copies.keep(toks, tok_out),
+            copies.keep(q_own, q_out),
+            copies.keep(weights, wqkv_out),
+            copies.keep(vec, vec_out),
+        ]
+        wm_own.wait()
+        for copy in wm_first:
+            copy.wait_recv()
+        block = wm.at[me.x, me.c, :, me.y]
+        wm_second = [copies.push(block, block, me.at(x=x, y=y)) for x, y in square]
+        arrivals.append(copies.push(block, block, me.sibling()))
+
+        @pl.when(me.crossing)
+        def _():
+            exchanged.wait_recv()
+            exchanged.wait_send()
+
+        @pl.when(jnp.logical_not(me.crossing))
+        def _():
+            stays.wait()
+
+        block = w2.at[me.g, me.c]
+        arrivals.append(copies.push(block, block, me.sibling()))
+        for copy, (x, y) in zip(kv_first, square):
+            copy.wait_recv()
+            block = kv_all.at[:, me.c, :, (x + me.c) % 2, y]
+            arrivals.append(copies.push(block, block, me.sibling()))
+        for copy, (x, y) in zip(wm_second, square):
+            copy.wait_recv()
+            block = wm.at[x, me.c, :, y]
+            arrivals.append(copies.push(block, block, me.sibling()))
+        for copy, (_, source) in zip(w2_first, me.line()):
+            copy.wait_recv()
+            block = w2.at[source, me.c]
+            arrivals.append(copies.push(block, block, me.sibling()))
+        for copy, (_, source) in zip(w1_second, me.line()):
+            copy.wait_recv()
+            block = w1.at[:, me.c, source, :]
+            arrivals.append(copies.push(block, block, me.sibling()))
+        for copy in arrivals:
+            copy.wait_recv()
+        for copy in kept:
+            copy.wait()
+        tokens_go.finish()
+        copies.finish()
+
+    vmem = pltpu.VMEM
+    dma = pltpu.SemaphoreType.DMA
+    total = 64
+    return pl.pallas_call(
+        body,
+        name="first_kernel",
+        out_shape=(
+            jax.ShapeDtypeStruct((GROUPS, n, depth), low_type),
+            jax.ShapeDtypeStruct((GROUPS, n, WIDE), low_type),
+            jax.ShapeDtypeStruct((4, GROUPS, 2, s, cols), low_type),
+            jax.ShapeDtypeStruct((SMALL, 2 * WIDE), wide),
+            jax.ShapeDtypeStruct((2, 2, 2, 2, 2, n, WIDE), low_type),
+            jax.ShapeDtypeStruct((2, 2, GROUPS, 2, s, quarter), low_type),
+            jax.ShapeDtypeStruct((GROUPS, 2, e, depth), low_type),
+            jax.ShapeDtypeStruct((2, 2, GROUPS, 2, s, depth), low_type),
+        ),
+        in_specs=[pl.BlockSpec(memory_space=vmem)] * (8 + count),
+        out_specs=(pl.BlockSpec(memory_space=pl.ANY),) * 8,
+        scratch_shapes=[
+            dma((total,)), dma((total,)), dma((8,)), dma((4,)), dma((4,)), dma, dma,
+            vmem((GROUPS, s, cols), low_type),
+            vmem((GROUPS, n, depth), low_type),
+            vmem((4, GROUPS, 2, s, cols), low_type),
+            vmem((2, 2, n, WIDE), low_type),
+            vmem((GROUPS, n, WIDE), low_type),
+            vmem((4, s, quarter), low_type),
+            vmem((e, depth), low_type),
+            vmem((s, depth), low_type),
+            vmem((SMALL, 2 * WIDE), wide),
+            vmem((s, LANES), wide),
+        ],
+        compiler_params=pltpu.CompilerParams(
+            collective_id=10, has_side_effects=True, vmem_limit_bytes=VMEM_LIMIT
+        ),
+    )(tokens, wq, wk, wv, tables, *vectors, inner, outer, mix)
+
+
+def pass_back(ident, pieces):
+    def body(source, target, send, recv):
+        me = Spot()
+        owners = me.owners()
+        readers = [device for _, device in me.readers()]
+        barrier, expected = announce(readers[1:], [(jnp.logical_not(me.selfish), readers[0])])
+        pl.semaphore_wait(barrier, expected)
+        move = Scatter(send, recv, me.selfish)
+        move.start([(source.at[slot], device) for slot, device in owners], target.at[me.g], me.g)
+        for g in range(GROUPS):
+            move.arrived(g, target.at[g])
+        move.finish()
+
+    return scatter_call(body, "pass_back", ident, pieces)
+
+
+def pass_on(ident, pieces):
+    def body(source, target, send, recv):
+        me = Spot()
+        owners = [device for _, device in me.owners()]
+        barrier, expected = announce(owners[1:], [(jnp.logical_not(me.selfish), owners[0])])
+        pl.semaphore_wait(barrier, expected)
+        move = Scatter(send, recv, me.selfish)
+        slot = me.slot()
+        move.start([(source.at[g], device) for g, device in me.readers()], target.at[slot], slot)
+        for index in range(GROUPS):
+            move.arrived(index, target.at[index])
+        move.finish()
+
+    return scatter_call(body, "pass_on", ident, pieces)
+
+
+def scatter_call(body, name, ident, pieces):
+    return pl.pallas_call(
+        body,
+        name=name,
+        out_shape=jax.ShapeDtypeStruct(pieces.shape, pieces.dtype),
+        in_specs=[pl.BlockSpec(memory_space=pl.ANY)],
+        out_specs=pl.BlockSpec(memory_space=pl.ANY),
+        scratch_shapes=[pltpu.SemaphoreType.DMA((4,)), pltpu.SemaphoreType.DMA((4,))],
+        compiler_params=pltpu.CompilerParams(
+            collective_id=ident, has_side_effects=True, vmem_limit_bytes=VMEM_LIMIT
+        ),
+    )(pieces)
+
+
+def last_kernel(dkv, dq, tokens, weights, grad1, grad2, gradm):
+    n = dq.shape[1]
+    depth = tokens.shape[-1]
+    cols = weights.shape[-1]
+    rows = grad1.shape[-2]
+    rowsm = gradm.shape[-2]
+    tall = grad2.shape[-2]
+    s = depth // 32
+    cut = depth // 2
+
+    def body(
+        dkv_ref, dq_ref, tok, w_ref, g1, g2, gm, dx_out, outq, out1, out2, outm,
+        send, recv, local, dx_send, dx_recv, swap_send, swap_recv,
+        kst, pk, grads, dxs, gq, s1, p1, f1, s2, p2, sm, pm, fm, tm, sq, pq, fq,
+    ):
+        me = Spot()
+        copies = Copies(send, recv, local)
+        square = me.square()
+        line = [to for to, _ in me.line()]
+        readers = [device for _, device in me.readers()]
+        swapped = [me.at(g=to, c=me.y, y=me.c) for to in [me.g] + line]
+        barrier, expected = announce(
+            [me.at(x=x, y=y) for x, y in square]
+            + [me.at(g=to) for to in line]
+            + swapped[1:]
+            + readers[1:]
+            + [me.sibling()],
+            [(jnp.logical_not(me.selfish), readers[0]), (me.crossing, swapped[0])],
+        )
+        pl.semaphore_wait(barrier, expected)
+        other = 1 - me.c
+        order = square + [(me.x, me.y)]
+        k_half = [
+            copies.push(
+                dkv_ref.at[:, other, :, (x + other) % 2, y], kst.at[x, y], me.sibling()
+            )
+            for x, y in order
+        ]
+        w1_half = copies.push(g1.at[:, other], s1, me.sibling())
+        wm_half = copies.push(gm.at[:, other], sm, me.sibling())
+        w2_half = copies.push(g2.at[:, other], s2, me.sibling())
+
+        k_push = []
+        for slot, (x, y) in enumerate(square):
+            k_half[slot].wait_recv()
+
+            def addk(index, x=x, y=y):
+                u, v = index // 2, index % 2
+                kst[x, y, u, v] = total_of(
+                    kst[x, y, u, v], dkv_ref[u, me.c, v, (x + me.c) % 2, y]
+                ).astype(low_type)
+
+            loop(GROUPS, addk)
+            k_push.append(copies.push(kst.at[x, y], pk.at[slot], me.at(x=x, y=y)))
+
+        def at8(index):
+            return index // 8, index // 2 % GROUPS, index % 2
+
+        w1_half.wait_recv()
+
+        def add1(index):
+            x, g, y = at8(index)
+            s1[x, g, y] = total_of(s1[x, g, y], g1[x, me.c, g, y]).astype(low_type)
+
+        loop(16, add1)
+        w1_push = [
+            copies.push(s1.at[:, to, :], p1.at[slot], me.at(g=to)) for slot, to in enumerate(line)
+        ]
+        wm_half.wait_recv()
+
+        def addm(index):
+            x, g, y = at8(index)
+            sm[x, g, y] = total_of(sm[x, g, y], gm[x, me.c, g, y]).astype(low_type)
+
+        loop(16, addm)
+        wm_push = [
+            copies.push(sm.at[x, :, y], pm.at[slot], me.at(x=x, y=y))
+            for slot, (x, y) in enumerate(square)
+        ]
+        w2_half.wait_recv()
+
+        def add2(g):
+            s2[g] = total_of(s2[g], g2[g, me.c]).astype(low_type)
+
+        loop(GROUPS, add2)
+        w2_push = [
+            copies.push(s2.at[to], p2.at[slot + 1], swapped[slot + 1])
+            for slot, to in enumerate(line)
+        ]
+        exchanged = pltpu.make_async_remote_copy(
+            src_ref=s2.at[me.g],
+            dst_ref=p2.at[0],
+            send_sem=swap_send,
+            recv_sem=swap_recv,
+            device_id=swapped[0],
+            device_id_type=MESH,
+        )
+        stays = pltpu.make_async_copy(s2.at[me.g], p2.at[0], swap_recv)
+
+        @pl.when(me.crossing)
+        def _():
+            exchanged.start()
+
+        @pl.when(jnp.logical_not(me.crossing))
+        def _():
+            stays.start()
+
+        k_half[3].wait_recv()
+        for copy in k_push:
+            copy.wait_recv()
+
+        def addg(slot):
+            u, v = slot // 2, slot % 2
+            grads[slot, :, :WIDE] = total_of(
+                kst[me.x, me.y, u, v],
+                dkv_ref[u, me.c, v, me.p, me.y],
+                *[pk[index, u, v] for index in range(3)],
+            ).astype(low_type)
+            grads[slot, :, WIDE:] = dq_ref[slot]
+
+        loop(GROUPS, addg)
+        for slot in range(GROUPS):
+            dxs[slot] = lax.dot_general(
+                grads[slot], w_ref[:, : 2 * WIDE], NEXT, preferred_element_type=wide
+            ).astype(low_type)
+        move = Scatter(dx_send, dx_recv, me.selfish)
+        move.start(
+            [(dxs.at[slot], device) for slot, device in me.owners()], dx_out.at[me.g], me.g
+        )
+        every = grads[...].reshape(GROUPS * n, 2 * WIDE)
+        bias = jnp.sum(every.astype(wide), axis=0, keepdims=True)
+        bias = jnp.broadcast_to(bias, (rows - s, 2 * WIDE)).astype(low_type)
+        for half in range(2):
+            made = lax.dot_general(
+                tok[:, :, half * cut : (half + 1) * cut].reshape(GROUPS * n, cut),
+                every,
+                DOWN,
+                preferred_element_type=wide,
+            ).astype(low_type)
+            for index in range(16):
+                x, c, g, y = half, index // 8, index // 2 % GROUPS, index % 2
+                gq[x, c, g, y, :s] = made[index * s : (index + 1) * s]
+                gq[x, c, g, y, s:] = bias
+        q_half = copies.push(gq.at[:, other], sq, me.sibling())
+
+        for copy in wm_push:
+            copy.wait_recv()
+
+        def addf(g):
+            fm[g] = total_of(sm[me.x, g, me.y], pm[0, g], pm[1, g], pm[2, g]).astype(low_type)
+
+        loop(GROUPS, addf)
+        wm_last = [
+            copies.push(fm.at[to], tm.at[slot], me.at(g=to)) for slot, to in enumerate(line)
+        ]
+        q_half.wait_recv()
+
+        def addq(index):
+            x, g, y = at8(index)
+            sq[x, g, y] = total_of(sq[x, g, y], gq[x, me.c, g, y]).astype(low_type)
+
+        loop(16, addq)
+        q_push = [
+            copies.push(sq.at[x, :, y], pq.at[slot], me.at(x=x, y=y))
+            for slot, (x, y) in enumerate(square)
+        ]
+        for copy in w1_push:
+            copy.wait_recv()
+
+        def addw(index):
+            x, y = index // 2, index % 2
+            f1[x, y] = total_of(s1[x, me.g, y], *[p1[slot, x, y] for slot in range(3)]).astype(
+                low_type
+            )
+
+        loop(4, addw)
+        quarter = out1.at[me.x * 2 + me.y]
+        arrivals = [copies.push(f1.at[x, y], quarter, me.at(x=x, y=y)) for x, y in square]
+        kept = [copies.keep(f1.at[me.x, me.y], quarter)]
+        for copy in q_push:
+            copy.wait_recv()
+
+        def addl(g):
+            fq[g] = total_of(sq[me.x, g, me.y], pq[0, g], pq[1, g], pq[2, g]).astype(low_type)
+
+        loop(GROUPS, addl)
+        arrivals += [copies.push(fq.at[to], outq.at[me.g], me.at(g=to)) for to in line]
+        kept.append(copies.keep(fq.at[me.g], outq.at[me.g]))
+
+        @pl.when(me.crossing)
+        def _():
+            exchanged.wait_recv()
+            exchanged.wait_send()
+
+        @pl.when(jnp.logical_not(me.crossing))
+        def _():
+            stays.wait()
+
+        for copy in w2_push:
+            copy.wait_recv()
+        out2[...] = total_of(*[p2[slot] for slot in range(4)])
+        for copy in wm_last:
+            copy.wait_recv()
+        outm[...] = total_of(fm[me.g], *[tm[slot] for slot in range(3)])
+        for copy in arrivals:
+            copy.wait_recv()
+        for g in range(GROUPS):
+            move.arrived(g, dx_out.at[g])
+        for copy in kept:
+            copy.wait()
+        move.finish()
+        copies.finish()
+
+    vmem = pltpu.VMEM
+    dma = pltpu.SemaphoreType.DMA
+    total = 48
+    return pl.pallas_call(
+        body,
+        name="last_kernel",
+        out_shape=(
+            jax.ShapeDtypeStruct((GROUPS, n, depth), low_type),
+            jax.ShapeDtypeStruct((GROUPS, rows, 2 * WIDE), low_type),
+            jax.ShapeDtypeStruct((4, rows, depth), low_type),
+            jax.ShapeDtypeStruct((tall, depth), wide),
+            jax.ShapeDtypeStruct((rowsm, depth), wide),
+        ),
+        in_specs=[pl.BlockSpec(memory_space=vmem)] * 7,
+        out_specs=[pl.BlockSpec(memory_space=space) for space in (pl.ANY, pl.ANY, pl.ANY, vmem, vmem)],
+        scratch_shapes=[
+            dma((total,)), dma((total,)), dma((4,)), dma((4,)), dma((4,)), dma, dma,
+            vmem((2, 2, 2, 2, n, WIDE), low_type),
+            vmem((3, 2, 2, n, WIDE), low_type),
+            vmem((GROUPS, n, 2 * WIDE), low_type),
+            vmem((GROUPS, n, depth), low_type),
+            vmem((2, 2, GROUPS, 2, rows, 2 * WIDE), low_type),
+            vmem((2, GROUPS, 2, rows, depth), low_type),
+            vmem((3, 2, 2, rows, depth), low_type),
+            vmem((2, 2, rows, depth), low_type),
+            vmem((GROUPS, tall, depth), low_type),
+            vmem((4, tall, depth), low_type),
+            vmem((2, GROUPS, 2, rowsm, depth), low_type),
+            vmem((3, GROUPS, rowsm, depth), low_type),
+            vmem((GROUPS, rowsm, depth), low_type),
+            vmem((3, rowsm, depth), low_type),
+            vmem((2, GROUPS, 2, rows, 2 * WIDE), low_type),
+            vmem((3, GROUPS, rows, 2 * WIDE), low_type),
+            vmem((GROUPS, rows, 2 * WIDE), low_type),
+        ],
+        compiler_params=pltpu.CompilerParams(
+            collective_id=11, has_side_effects=True, vmem_limit_bytes=VMEM_LIMIT
+        ),
+    )(dkv, dq, tokens, weights, grad1, grad2, gradm)
+
+
+def final_kernel(hidden, pieces, outq, out1, out2, outm, s, e):
+    n, depth = hidden.shape
+    quarter = out1.shape[-1]
+
+    def body(hid, dx, q_in, i_in, o_in, m_in, xg, qw, qb, kw, vw, vb, mw, mb, eg, es, iw, ib, ow, ob, fg, fs):
+        device = lax.axis_index("au") * lax.axis_size("row") + lax.axis_index("row")
+        xg[...] = total_of(hid[...], dx[0], dx[1], dx[2], dx[3]).astype(low_type)
+        rows = q_in.shape[1]
+        lower = lax.broadcasted_iota(jnp.int32, (rows, LANES), 1) < HEAD
+
+        def part(head, offset):
+            g, h = head // LOCAL, head % LOCAL
+            return q_in[g, :, offset + h * LANES : offset + (h + 1) * LANES].astype(wide)
+
+        biases = [[], []]
+        for pair in range(HEADS // 2):
+            span = slice(pair * LANES, (pair + 1) * LANES)
+            kv = [part(2 * pair, 0), part(2 * pair + 1, 0)]
+            q = [part(2 * pair, WIDE), part(2 * pair + 1, WIDE)]
+            made_q = jnp.where(lower, q[0], pltpu.roll(q[1], HEAD, 1))
+            made_k = jnp.where(lower, kv[0], pltpu.roll(kv[1], HEAD, 1))
+            made_v = jnp.where(lower, pltpu.roll(kv[0], HEAD, 1), kv[1])
+            qw[:, span], kw[:, span], vw[:, span] = made_q[:s], made_k[:s], made_v[:s]
+            biases[0].append(made_q[s:])
+            biases[1].append(made_v[s:])
+
+        def own(eight, width, shift):
+            return pltpu.roll(eight, shift, 1)[0:1, :width]
+
+        turn = (depth - device * s) % depth
+        qb[...] = own(jnp.concatenate(biases[0], axis=1), s, turn)
+        vb[...] = own(jnp.concatenate(biases[1], axis=1), s, turn)
+        mw[...] = m_in[:s]
+        extras = pltpu.roll(m_in[s : s + 8, :], turn, 1)
+        for index, ref in enumerate((mb, eg, es, ob, fg, fs)):
+            ref[...] = extras[index : index + 1, :s]
+        for w in range(4):
+            iw[:, w * quarter : (w + 1) * quarter] = i_in[w, :s].astype(wide)
+        place = lax.axis_index("row") * e
+        ib[...] = own(
+            i_in[lax.axis_index("au"), s : s + 8, :].astype(wide), e, (quarter - place) % quarter
+        )
+        ow[...] = o_in[...]
+
+    vmem = pltpu.VMEM
+
+    def shape(*dims):
+        return jax.ShapeDtypeStruct(dims, wide)
+
+    return pl.pallas_call(
+        body,
+        name="final_kernel",
+        out_shape=(
+            jax.ShapeDtypeStruct((n, depth), low_type),
+            shape(s, depth), shape(1, s), shape(s, depth), shape(s, depth), shape(1, s),
+            shape(s, depth), shape(1, s), shape(1, s), shape(1, s),
+            shape(s, 4 * quarter), shape(1, e), shape(e, depth),
+            shape(1, s), shape(1, s), shape(1, s),
+        ),
+        in_specs=[pl.BlockSpec(memory_space=vmem)] * 6,
+        out_specs=(pl.BlockSpec(memory_space=vmem),) * 16,
+        compiler_params=pltpu.CompilerParams(vmem_limit_bytes=VMEM_LIMIT),
+    )(hidden, pieces, outq, out1, out2, outm)
+
+
+def on_device_general(
     tokens,
     cotangent,
     doc_lengths,
@@ -1079,6 +1796,159 @@
     )
 
 
+def on_device(
+    tokens,
+    cotangent,
+    doc_lengths,
+    query_weight,
+    query_bias,
+    key_weight,
+    value_weight,
+    value_bias,
+    mix_weight,
+    mix_bias,
+    early_gain,
+    early_shift,
+    inner_weight,
+    inner_bias,
+    outer_weight,
+    outer_bias,
+    final_gain,
+    final_shift,
+):
+    n, depth = tokens.shape
+    cycle = lax.axis_size("row")
+    devices = lax.axis_size("au") * cycle
+    s = query_weight.shape[0]
+    ff = inner_weight.shape[1]
+    quarter = ff // 4
+    e = outer_weight.shape[0]
+    rows = GROUPS * n
+    total_tokens = n * devices
+    me = Spot()
+    vectors = [
+        vector.reshape(1, -1)
+        for vector in (
+            query_bias, value_bias, mix_bias, early_gain, early_shift,
+            outer_bias, final_gain, final_shift,
+        )
+    ]
+    vectors.append(inner_bias.reshape(1, -1))
+    toks, queries, w_qkv, vec, kv_all, w1, w2, wm = first_kernel(
+        tokens, query_weight, key_weight, value_weight, vectors,
+        inner_weight, outer_weight, mix_weight,
+    )
+    queries = queries.reshape(rows, WIDE)
+    kv_all = kv_all.reshape(total_tokens, WIDE)
+    w_qkv = w_qkv.reshape(depth, -1)
+    w1 = w1.reshape(depth, quarter)
+    w2 = w2.reshape(quarter, depth)
+    wm = wm.reshape(depth, depth)
+    m_bias, e_gain, e_shift, o_bias, f_gain, f_shift, i_bias = [vec[i] for i in range(2, 9)]
+
+    tile, block = 128, 512
+    count = doc_lengths.shape[0]
+    upto = jnp.arange(count)[None, :] <= jnp.arange(count)[:, None]
+    ends = jnp.sum(jnp.where(upto, doc_lengths[None, :], 0), axis=1)
+    slot = jnp.arange(GROUPS)
+    owners = ((slot // 2 * 2 + me.c) * cycle + (slot % 2 * 2 + me.p) * 2 + me.y) * n
+    places = (owners[:, None] + jnp.arange(n)[None, :]).reshape(rows)
+    before = ends[None, :] <= places[:, None]
+    first = jnp.max(jnp.where(before, ends[None, :], 0), axis=1).astype(jnp.int32)
+    last = jnp.min(jnp.where(before, total_tokens, ends[None, :]), axis=1).astype(jnp.int32)
+    tiles = rows // tile
+    bounds = jnp.stack(
+        [
+            first.reshape(tiles, tile)[:, 0] // block,
+            (last.reshape(tiles, tile)[:, -1] + block - 1) // block,
+        ],
+        axis=1,
+    )
+    mixed, mixed_wide, lse = attend_forward(
+        queries, kv_all, bounds, first[:, None], last[:, None], tile, block
+    )
+    mixed_tok = pass_back(2, mixed.reshape(GROUPS, n, PACK))
+    mixed_tok = jnp.transpose(mixed_tok[:, :, : LOCAL * HEAD], (1, 0, 2)).reshape(n, depth)
+
+    attn = jnp.dot(mixed_tok, wm, preferred_element_type=wide) + m_bias
+    early, early_pull = jax.vjp(layer_norm, tokens.astype(wide) + attn, e_gain, e_shift)
+    early_all = gather_square(1, 3, early.astype(low_type)).reshape(rows, depth)
+    inner = jnp.dot(early_all, w1, preferred_element_type=wide) + i_bias
+    act, gelu_pull = jax.vjp(gelu_exact, inner)
+    act_low = act.astype(low_type)
+    partial = jnp.dot(act_low, w2, preferred_element_type=wide).astype(low_type)
+    partial = exchange_square(1, 4, partial.reshape(2, 2, n, depth))
+    branch = jnp.sum(partial.astype(wide), axis=(0, 1)) + o_bias
+    result, final_pull = jax.vjp(layer_norm, early + branch, f_gain, f_shift)
+    output = result.astype(low_type)
+    final_grads = final_pull(cotangent.astype(wide))
+    branch_grad = final_grads[0].astype(low_type)
+    outer_bias_grad = jnp.sum(branch_grad.astype(wide), axis=0)
+    branch_all = gather_square(1, 5, branch_grad).reshape(rows, depth)
+    act_grad = jnp.einsum("td,fd->tf", branch_all, w2, preferred_element_type=wide)
+    inner_grad = gelu_pull(act_grad)[0].astype(low_type)
+    partial = jnp.einsum("tf,df->td", inner_grad, w1, preferred_element_type=wide).astype(low_type)
+    partial = exchange_square(1, 6, partial.reshape(2, 2, n, depth))
+    grad2 = jnp.einsum("tf,td->fd", act_low, branch_all, preferred_element_type=wide)
+    grad1 = jnp.einsum("td,tf->df", early_all, inner_grad, preferred_element_type=wide)
+    inner_bias_grad = jnp.sum(inner_grad.astype(wide), axis=0)
+    early_grad = final_grads[0] + jnp.sum(partial.astype(wide), axis=(0, 1))
+    early_grads = early_pull(early_grad)
+    attn_grad = early_grads[0].astype(low_type)
+    mixed_grad = jnp.einsum("td,cd->tc", attn_grad, wm, preferred_element_type=wide)
+    mixed_grad = jnp.transpose(
+        mixed_grad.astype(low_type).reshape(n, GROUPS, LOCAL * HEAD), (1, 0, 2)
+    )
+    mixed_grad = jnp.pad(mixed_grad, ((0, 0), (0, 0), (0, PACK - LOCAL * HEAD)))
+    grad_all = pass_on(7, mixed_grad).reshape(rows, PACK)
+    gradm = jnp.einsum("tc,td->cd", mixed_tok, attn_grad, preferred_element_type=wide)
+    mix_bias_grad = jnp.sum(attn_grad.astype(wide), axis=0)
+
+    delta = jnp.sum(
+        (grad_all.astype(wide) * mixed_wide)[:, : LOCAL * HEAD].reshape(rows, LOCAL, HEAD), axis=2
+    )
+
+    def as_stat(values):
+        return jnp.transpose(values.reshape(tiles, tile, LOCAL), (0, 2, 1))
+
+    def same_stat(values):
+        return jnp.broadcast_to(
+            values.astype(wide).reshape(tiles, 1, tile), (tiles, LOCAL, tile)
+        )
+
+    stats = jnp.stack(
+        [same_stat(first), same_stat(last), as_stat(lse[:, :LOCAL]), as_stat(delta)], axis=2
+    )
+    stats = jnp.pad(stats, ((0, 0), (0, 0), (0, 4), (0, 0)))
+    query_grad, dkv = attend_backward(queries, kv_all, grad_all, stats, bounds, tile, block)
+
+    def slabs(grad, extras):
+        grad = grad.astype(low_type).reshape(devices, s, -1)
+        extras = jnp.pad(extras.astype(low_type), ((0, 8 - extras.shape[0]), (0, 0)))
+        extras = jnp.broadcast_to(extras[None], (devices,) + extras.shape)
+        return jnp.concatenate([grad, extras], axis=1).reshape(2, 2, GROUPS, 2, s + 8, -1)
+
+    mix_extras = jnp.stack(
+        [
+            mix_bias_grad, early_grads[1], early_grads[2],
+            outer_bias_grad, final_grads[1], final_grads[2],
+        ]
+    )
+    pieces, outq, out1, out2, outm = last_kernel(
+        dkv.reshape(2, 2, 2, 2, 2, n, WIDE),
+        query_grad.reshape(GROUPS, n, WIDE),
+        toks,
+        w_qkv,
+        slabs(grad1, inner_bias_grad[None]),
+        grad2.astype(low_type).reshape(GROUPS, 2, e, depth),
+        slabs(gradm, mix_extras),
+    )
+    results = final_kernel(early_grads[0], pieces, outq, out1, out2, outm, s, e)
+    return (output,) + tuple(
+        result.reshape(-1) if result.shape[0] == 1 else result for result in results
+    )
+
+
 def solution(mesh):
     both = P(("au", "row"), None)
     flat = P(("au", "row"))
@@ -1090,6 +1960,7 @@
         both, both, both, flat, both, both, flat, both, flat, flat, flat,
         both, flat, both, flat, flat, flat,
     )
+    fast = mesh.shape["au"] == 4 and mesh.shape["row"] == 2 * GROUPS
     return jax.shard_map(
-        on_device, mesh=mesh, in_specs=in_specs, out_specs=out_specs, check_vma=False
-    )
+        on_device if fast else on_device_general, mesh=mesh, in_specs=in_specs, out_specs=out_specs, check_vma=False
+    )

time: 339 us -> 291 us (0.86); the launches traced: 340 us -> 286 us
  other arithmetic: 31.8 us -> 13.7 us
  local copies, waits for them, and re-layouts: 23.1 us -> 6.49 us
  Pallas kernels: 261 us -> 245 us
  matrix products: 23 us -> 19.6 us
    pallas_call x10 -> x4, Pallas kernels: 212 us -> 38 us  [comm_call(): pl.pallas_call(body, name=name, out_shape=tuple(outs), in_specs=[pl.Block...]
    pallas_call x0 -> x5, Pallas kernels: none -> 157 us  [the longest x1 66.8 us: last_kernel(): pl.pallas_call(body, name='last_kernel', out_shape=(jax.ShapeDtypeStruct(...]
    convert_element_type x20 -> x1, other arithmetic: 13.1 us -> 0.83 us  [on_device(): early_all = gather_square(1, 3, early.astype(low_type)).reshape(rows, depth)]
    slice x21 -> x1, local copies, waits for them, and re-layouts: 7.59 us -> 1.02 us  [on_device(): vec[i]]
    dynamic_slice x8 -> x0, local copies, waits for them, and re-layouts: 4.66 us -> none  [own(): lax.dynamic_slice_in_dim(vector, device * count, count, 0).astype(wide)]
where the time goes in v2:
time: 291 us; the launch traced here: 286 us
  Pallas kernels  245 us (84%)
  matrix products  19.6 us (7%)
  other arithmetic  13.7 us (5%)
  local copies, waits for them, and re-layouts  6.49 us (2%)
    pallas_call x1, Pallas kernels, last_kernel(): pl.pallas_call(body, name='last_kernel', out_shape=(jax.ShapeDtypeStruct(...  66.8 us
    pallas_call x1, Pallas kernels, first_kernel(): pl.pallas_call(body, name='first_kernel', out_shape=(jax.ShapeDtypeStruct...  65.4 us
    pallas_call x4, Pallas kernels, comm_call(): pl.pallas_call(body, name=name, out_shape=tuple(outs), in_specs=[pl.Block...  38 us
    pallas_call x1, Pallas kernels, attend_backward(): pl.pallas_call(body, name='attend_backward', grid=(LOCAL,), out_shape=(ja...  29.7 us
    pallas_call x2, Pallas kernels, scatter_call(): pl.pallas_call(body, name=name, out_shape=jax.ShapeDtypeStruct(pieces.sha...  21.8 us
    pallas_call x1, Pallas kernels, attend_forward(): pl.pallas_call(body, name='attend_forward', out_shape=(jax.ShapeDtypeStru...  20.7 us
    dot_general x1, matrix products, on_device(): inner = jnp.dot(early_all, w1, preferred_element_type=wide) + i_bias  7.14 us

profile of v2, /device:TPU:0, one launch (start us, length us, event | category | flops | bytes accessed | tf_op | source)
XLA Modules:
  0.0 286.2 jit_solution(1799072866998459311)
XLA Ops:
  0.7 0.8 select_reduce_fusion
  1.7 1.0 reduce.3
  2.7 0.7 pad_add_fusion.bounds_ref
  3.4 0.9 copy.46.high_ref
  4.3 0.9 copy.45.low_ref
  5.1 65.4 %first_kernel.1 = (bf16[4,128,768]{2,1,0:T(8,128)(2,1)}, bf16[4,128,384]{2,1,0:T(8,128)(2,1)}, bf16[4,4,2,24,896]{4,3,2,1,0:T(8,128)(2,1)}, f32[16,768]{1,0:T(8,...) custom-call(bf16[128,768]{1,0:T(8,128)(2,1)} %refs_0_.1, ...), custom_call_target="tpu_custom_call" | custom-call | tf_op jit(solution)/shard_map/first_kernel/pallas_call | solution.py:1170
  70.5 1.0 slice_reduce_fusion.1
  71.5 20.7 %attend_forward.1 = (bf16[512,256]{1,0:T(8,128)(2,1)}, f32[512,256]{1,0:T(8,128)}, f32[512,128]{1,0:T(8,128)}) custom-call(s32[4,2]{1,0:T(4,128)} %pad_add_fusion.bounds_ref, bf16[512,384]{1,0:T(8,128)(2,1)} %bitcast.85, bf16[4096,384]{1,0:T(8,128)(2,1)} %bitcast.75, s32[512,1]{1,0:T(8,128)} %copy.45.low_ref, s32[512,1]{1,0:T(8,128)} %copy.46.high_ref), custom_call_target="tpu_custom_call" | custom-call | tf_op jit(solution)/shard_map/attend_forward/pallas_call | solution.py:759
  92.3 12.5 %pass_back.1 = bf16[4,128,256]{2,1,0:T(8,128)(2,1)} custom-call(bf16[4,128,256]{2,1,0:T(8,128)(2,1)} %bitcast.101), custom_call_target="tpu_custom_call" | custom-call | tf_op jit(solution)/shard_map/pass_back/pallas_call | solution.py:1237
  104.8 1.0 slice_bitcast_fusion
  105.8 0.2 copy.47
  106.0 1.1 copy.54
  107.2 0.4 fusion.37
  107.6 0.2 multiply_reduce_fusion.3
  107.8 0.8 fusion.11.source
  108.7 10.7 %gather_square.2 = bf16[2,2,128,768]{3,2,1,0:T(8,128)(2,1)} custom-call(bf16[128,768]{1,0:T(8,128)(2,1)} %fusion.11.source), custom_call_target="tpu_custom_call" | custom-call | tf_op jit(solution)/shard_map/gather_square/pallas_call | solution.py:141
  119.4 7.1 %multiply_convert_fusion = (bf16[512,768]{1,0:T(8,128)(2,1)S(1)}, f32[512,768]{1,0:T(8,128)}, f32[512,768]{1,0:T(8,128)}) fusion(f32[768]{0:T(1024)S(1)} %get-tuple-element.93, bf16[512,768]{1,0:T(8,128)(2,1)} %bitcast.95, bf16[768,768]{1,0:T(8,128)(2,1)} %bitcast.117), kind=kOutput, calls=%fused_computation.7 | convolution fusion | flops 629932032 | bytes 5901312 | tf_op jit(solution)/shard_map/dot_general | solution.py:1876
  126.6 1.7 convolution_convert_fusion.4
  128.3 9.1 %exchange_square.2 = bf16[2,2,128,768]{3,2,1,0:T(8,128)(2,1)} custom-call(bf16[2,2,128,768]{3,2,1,0:T(8,128)(2,1)} %bitcast.94), custom_call_target="tpu_custom_call" | custom-call | tf_op jit(solution)/shard_map/exchange_square/pallas_call | solution.py:141
  137.3 1.3 convert_reduce_fusion.1
  138.7 0.2 fusion.35
  138.9 0.2 multiply_reduce_fusion.2
  139.1 0.3 fusion.10
  139.4 0.9 fusion.34
  140.3 0.8 fusion.31
  141.1 9.1 %gather_square.3 = bf16[2,2,128,768]{3,2,1,0:T(8,128)(2,1)} custom-call(bf16[128,768]{1,0:T(8,128)(2,1)} %get-tuple-element.100.source), custom_call_target="tpu_custom_call" | custom-call | tf_op jit(solution)/shard_map/gather_square/pallas_call | solution.py:141
  150.2 3.7 %fusion.32 = (bf16[768]{0:T(1024)(128)(2,1)S(1)}, bf16[512,768]{1,0:T(8,128)(2,1)S(1)}) fusion(f32[512,768]{1,0:T(8,128)} %get-tuple-element.113, f32[512,768]{1,0:T(8,128)} %get-tuple-element.117, bf16[512,768]{1,0:T(8,128)(2,1)} %bitcast.97, bf16[768,768]{1,0:T(8,128)(2,1)} %bitcast.119), kind=kOutput, calls=%fused_computation.115 | convolution fusion | flops 609877248 | bytes 5899776 | tf_op jit(solution)/shard_map/td,fd->tf/dot_general | solution.py:1888
  154.0 1.9 convolution_convert_fusion.1
  155.9 1.7 convolution_convert_fusion.3
  157.7 9.1 %exchange_square.3 = bf16[2,2,128,768]{3,2,1,0:T(8,128)(2,1)} custom-call(bf16[2,2,128,768]{3,2,1,0:T(8,128)(2,1)} %bitcast.93), custom_call_target="tpu_custom_call" | custom-call | tf_op jit(solution)/shard_map/exchange_square/pallas_call | solution.py:141
  166.7 1.3 convert_reduce_fusion
  168.0 0.3 multiply_reduce_fusion
  168.3 0.2 fusion.33
  168.7 0.5 convolution_convert_fusion.5
  169.3 0.2 copy.48
  169.5 0.1 copy.49
  169.7 0.7 pad.16.source
  170.4 9.3 %pass_on.1 = bf16[4,128,256]{2,1,0:T(8,128)(2,1)} custom-call(bf16[4,128,256]{2,1,0:T(8,128)(2,1)} %pad.16.source), custom_call_target="tpu_custom_call" | custom-call | tf_op jit(solution)/shard_map/pass_on/pallas_call | solution.py:1237
  179.7 1.0 slice_multiply_fusion
  180.7 0.2 copy.51
  181.0 0.7 select_maximum_fusion.stat_ref
  181.7 29.7 %attend_backward.1 = (bf16[512,384]{1,0:T(8,128)(2,1)}, bf16[4096,384]{1,0:T(8,128)(2,1)}) custom-call(s32[4,2]{1,0:T(4,128)} %pad_add_fusion.bounds_ref, bf16[512,384]{1,0:T(8,128)(2,1)} %bitcast.86, bf16[4096,384]{1,0:T(8,128)(2,1)} %bitcast.76, bf16[512,256]{1,0:T(8,128)(2,1)} %bitcast.82, f32[4,3,8,128]{3,2,1,0:T(8,128)} %select_maximum_fusion.stat_ref), custom_call_target="tpu_custom_call" | custom-call | tf_op jit(solution)/shard_map/attend_backward/pallas_call | solution.py:829
  211.5 1.9 convolution_convert_fusion.2
  213.4 1.4 pad_maximum_fusion.g1
  214.8 0.5 convolution_convert_fusion
  215.2 1.3 pad_maximum_fusion.1.gm
  216.6 66.8 %last_kernel.1 = (bf16[4,128,768]{2,1,0:T(8,128)(2,1)}, bf16[4,32,768]{2,1,0:T(8,128)(2,1)}, bf16[4,32,768]{2,1,0:T(8,128)(2,1)}, f32[96,768]{1,0:T(8,128)}, f32[32,768]{1,0:T(8,128)}) custom-call(bf16[2,2,2,2,2,128,384]{6,5,4,3,2,1,0:T(8,128)(2,1)} %bitcast.80, bf16[4,128,384]{2,1,0:T(8,128)(2,1)} %bitcast.99, bf16[4,128,768]{2,1,0:T(8,128)(2,1)} %get-tuple-element.62.tok, ...), custom_call_target="tpu_custom_call" | custom-call | tf_op jit(solution)/shard_map/last_kernel/pallas_call | solution.py:1466
  283.4 2.6 final_kernel.1
  (60 shorter events, 0.8 us)
Async XLA Ops:
  92.3 14.9 %copy-start.1 = (bf16[2,2,4,2,24,768]{5,4,3,2,1,0:T(8,128)(2,1)S(1)}, bf16[2,2,4,2,24,768]{5,4,3,2,1,0:T(8,128)(2,1)}, u32[]{:S(2)}) copy-start(bf16[2,2,4,2,24,768]{5,4,3,2,1,0:T(8,128)(2,1)} %get-tuple-element.54) | copy-start | bytes 3538948
  92.3 14.9 %copy-start.7 = (bf16[128,768]{1,0:T(8,128)(2,1)S(1)}, bf16[128,768]{1,0:T(8,128)(2,1)}, u32[]{:S(2)}) copy-start(bf16[128,768]{1,0:T(8,128)(2,1)} %refs_0_.1) | copy-start | bytes 589828
  106.0 1.2 copy-start.2
  119.4 7.2 %copy-start.10 = (bf16[4,2,96,768]{3,2,1,0:T(8,128)(2,1)S(1)}, bf16[4,2,96,768]{3,2,1,0:T(8,128)(2,1)}, u32[]{:S(2)}) copy-start(bf16[4,2,96,768]{3,2,1,0:T(8,128)(2,1)} %get-tuple-element.57) | copy-start | bytes 3538948
  126.6 1.7 copy-start.12
  137.3 1.8 copy-start.4
  150.2 3.8 %copy-start.6 = (bf16[2,2,128,768]{3,2,1,0:T(8,128)(2,1)S(1)}, bf16[2,2,128,768]{3,2,1,0:T(8,128)(2,1)}, u32[]{:S(2)}) copy-start(bf16[2,2,128,768]{3,2,1,0:T(8,128)(2,1)} %gather_square.3) | copy-start | bytes 2359300
  150.2 3.8 %copy-start.13 = (bf16[512,768]{1,0:T(8,128)(2,1)S(1)}, bf16[512,768]{1,0:T(8,128)(2,1)}, u32[]{:S(2)}) copy-start(bf16[512,768]{1,0:T(8,128)(2,1)} %copy-done.12) | copy-start | bytes 2359300
  154.0 1.9 copy-start.11
  154.0 1.9 copy-start.9
  168.7 46.1 %copy-start = (f32[128,768]{1,0:T(8,128)}, f32[128,768]{1,0:T(8,128)S(1)}, u32[]{:S(2)}) copy-start(f32[128,768]{1,0:T(8,128)S(1)} %get-tuple-element.102.hid) | copy-start | bytes 1179652
  169.3 10.5 %copy-start.8 = (f32[512,256]{1,0:T(8,128)S(1)}, f32[512,256]{1,0:T(8,128)}, u32[]{:S(2)}) copy-start(f32[512,256]{1,0:T(8,128)} %get-tuple-element.59) | copy-start | bytes 1572868
  181.7 29.8 %copy-start.5 = (bf16[2,2,128,768]{3,2,1,0:T(8,128)(2,1)S(1)}, bf16[2,2,128,768]{3,2,1,0:T(8,128)(2,1)}, u32[]{:S(2)}) copy-start(bf16[2,2,128,768]{3,2,1,0:T(8,128)(2,1)} %gather_square.2) | copy-start | bytes 2359300
  213.4 1.4 copy-start.3

commit v3 on v2

--- a/solution.py
+++ b/solution.py
@@ -871,8 +871,8 @@
 
     def owners(self):
         result = []
-        for du in range(2):
-            for dv in range(2):
+        for dv in range(2):
+            for du in range(2):
                 u, v = (self.x + du) % 2, (self.half + dv) % 2
                 result.append((u * 2 + v, self.at(x=u, g=2 * v + self.p)))
         return result
@@ -907,28 +907,32 @@
         self.copies = []
 
     def start(self, pieces, target, slot):
-        for index, (source, device) in enumerate(pieces):
-            copy = pltpu.make_async_remote_copy(
-                src_ref=source,
-                dst_ref=target,
-                send_sem=self.send.at[index],
-                recv_sem=self.recv.at[slot],
-                device_id=device,
-                device_id_type=MESH,
-            )
-            self.copies.append(copy)
-            if index:
-                copy.start()
-                continue
-            stay = pltpu.make_async_copy(source, target, self.recv.at[slot])
-
-            @pl.when(self.here)
-            def _(stay=stay):
-                stay.start()
-
-            @pl.when(jnp.logical_not(self.here))
-            def _(copy=copy):
-                copy.start()
+        for source, device in pieces:
+            self.send_one(source, target, slot, device)
+
+    def send_one(self, source, target, slot, device):
+        index = len(self.copies)
+        copy = pltpu.make_async_remote_copy(
+            src_ref=source,
+            dst_ref=target,
+            send_sem=self.send.at[index],
+            recv_sem=self.recv.at[slot],
+            device_id=device,
+            device_id_type=MESH,
+        )
+        self.copies.append(copy)
+        if index:
+            copy.start()
+            return
+        stay = pltpu.make_async_copy(source, target, self.recv.at[slot])
+
+        @pl.when(self.here)
+        def _():
+            stay.start()
+
+        @pl.when(jnp.logical_not(self.here))
+        def _():
+            copy.start()
 
     def arrived(self, slot, target):
         pltpu.make_async_copy(target, target, self.recv.at[slot]).wait()
@@ -1247,210 +1251,177 @@
     )(pieces)
 
 
-def last_kernel(dkv, dq, tokens, weights, grad1, grad2, gradm):
+def last_kernel(dkv, dq, tokens, weights, sum1, gradm):
     n = dq.shape[1]
     depth = tokens.shape[-1]
-    cols = weights.shape[-1]
-    rows = grad1.shape[-2]
-    rowsm = gradm.shape[-2]
-    tall = grad2.shape[-2]
     s = depth // 32
+    rows = s + 8
     cut = depth // 2
 
     def body(
-        dkv_ref, dq_ref, tok, w_ref, g1, g2, gm, dx_out, outq, out1, out2, outm,
-        send, recv, local, dx_send, dx_recv, swap_send, swap_recv,
-        kst, pk, grads, dxs, gq, s1, p1, f1, s2, p2, sm, pm, fm, tm, sq, pq, fq,
+        dkv_ref, dq_ref, tok, w_ref, s1, gm, dx_out, outq, outk, out1, outm,
+        send, recv, local, dx_send, dx_recv,
+        kst, pk, grads, queries, dxs, gq, sq, pq, fq, gk, sk, pp, fk, p1, f1, sm, pm, fm, tm,
     ):
         me = Spot()
         copies = Copies(send, recv, local)
         square = me.square()
         line = [to for to, _ in me.line()]
+        owners = me.owners()
         readers = [device for _, device in me.readers()]
-        swapped = [me.at(g=to, c=me.y, y=me.c) for to in [me.g] + line]
         barrier, expected = announce(
             [me.at(x=x, y=y) for x, y in square]
             + [me.at(g=to) for to in line]
-            + swapped[1:]
             + readers[1:]
             + [me.sibling()],
-            [(jnp.logical_not(me.selfish), readers[0]), (me.crossing, swapped[0])],
+            [(jnp.logical_not(me.selfish), readers[0])],
         )
         pl.semaphore_wait(barrier, expected)
         other = 1 - me.c
-        order = square + [(me.x, me.y)]
-        k_half = [
-            copies.push(
-                dkv_ref.at[:, other, :, (x + other) % 2, y], kst.at[x, y], me.sibling()
-            )
-            for x, y in order
-        ]
-        w1_half = copies.push(g1.at[:, other], s1, me.sibling())
+        k_half = []
+        for dv in range(2):
+            v = (me.half + dv) % 2
+            k_half += [
+                copies.push(dkv_ref.at[u, other, v], kst.at[u, v], me.sibling()) for u in range(2)
+            ]
+
         wm_half = copies.push(gm.at[:, other], sm, me.sibling())
-        w2_half = copies.push(g2.at[:, other], s2, me.sibling())
-
-        k_push = []
-        for slot, (x, y) in enumerate(square):
-            k_half[slot].wait_recv()
-
-            def addk(index, x=x, y=y):
-                u, v = index // 2, index % 2
-                kst[x, y, u, v] = total_of(
-                    kst[x, y, u, v], dkv_ref[u, me.c, v, (x + me.c) % 2, y]
+        w1_push = [
+            copies.push(s1.at[:, to, :], p1.at[slot], me.at(g=to)) for slot, to in enumerate(line)
+        ]
+
+        lower = lax.broadcasted_iota(jnp.int32, (n, LANES), 1) < HEAD
+        for slot in range(GROUPS):
+            second = pltpu.roll(dq_ref[slot, :, LANES : 2 * LANES].astype(wide), HEAD, 1)
+            front = jnp.where(lower, dq_ref[slot, :, :LANES].astype(wide), second)
+            queries[slot, :, :LANES] = front.astype(low_type)
+            queries[slot, :, LANES:] = dq_ref[slot, :, 2 * LANES :]
+            grads[slot, :, WIDE:] = dq_ref[slot]
+
+        def weight_grad(values, target):
+            width = values.shape[-1]
+            bias = jnp.sum(values.astype(wide), axis=0, keepdims=True)
+            bias = jnp.broadcast_to(bias, (8, width)).astype(low_type)
+            for half in range(2):
+                made = lax.dot_general(
+                    tok[:, :, half * cut : (half + 1) * cut].reshape(GROUPS * n, cut),
+                    values,
+                    DOWN,
+                    preferred_element_type=wide,
                 ).astype(low_type)
-
-            loop(GROUPS, addk)
-            k_push.append(copies.push(kst.at[x, y], pk.at[slot], me.at(x=x, y=y)))
+                for index in range(16):
+                    place = (half, index // 8, index // 2 % GROUPS, index % 2)
+                    target[(*place, slice(None, s))] = made[index * s : (index + 1) * s]
+                    target[(*place, slice(s, None))] = bias
+
+        def keys_on(dv):
+            v = (me.half + dv) % 2
+            for u in range(2):
+                k_half[2 * dv + u].wait_recv()
+            pushed = []
+            for du in range(2):
+                for slot, (x, y) in enumerate(square):
+                    u, p = (x + du) % 2, (x + me.c) % 2
+                    kst[u, v, p, y] = kst[u, v, p, y] + dkv_ref[u, me.c, v, p, y]
+                    pushed.append(
+                        copies.push(
+                            kst.at[u, v, p, y], pk.at[2 * dv + du, slot], me.at(x=x, y=y)
+                        )
+                    )
+            return pushed
+
+        k_push = keys_on(0)
+        weight_grad(queries[...].reshape(GROUPS * n, PACK), gq)
+        q_half = copies.push(gq.at[:, other], sq, me.sibling())
+        k_push += keys_on(1)
 
         def at8(index):
             return index // 8, index // 2 % GROUPS, index % 2
 
-        w1_half.wait_recv()
-
-        def add1(index):
-            x, g, y = at8(index)
-            s1[x, g, y] = total_of(s1[x, g, y], g1[x, me.c, g, y]).astype(low_type)
-
-        loop(16, add1)
-        w1_push = [
-            copies.push(s1.at[:, to, :], p1.at[slot], me.at(g=to)) for slot, to in enumerate(line)
-        ]
+        def pair_sum(total, mine):
+            def add(index):
+                x, g, y = at8(index)
+                total[x, g, y] = total[x, g, y] + mine[x, me.c, g, y]
+
+            loop(16, add)
+
+        def square_push(total, landing):
+            return [
+                copies.push(total.at[x, :, y], landing.at[slot], me.at(x=x, y=y))
+                for slot, (x, y) in enumerate(square)
+            ]
+
+        def square_sum(result, total, landed):
+            def add(g):
+                result[g] = total_of(
+                    total[me.x, g, me.y], landed[0, g], landed[1, g], landed[2, g]
+                ).astype(low_type)
+
+            loop(GROUPS, add)
+
+        q_half.wait_recv()
+        pair_sum(sq, gq)
+        q_push = square_push(sq, pq)
         wm_half.wait_recv()
-
-        def addm(index):
-            x, g, y = at8(index)
-            sm[x, g, y] = total_of(sm[x, g, y], gm[x, me.c, g, y]).astype(low_type)
-
-        loop(16, addm)
-        wm_push = [
-            copies.push(sm.at[x, :, y], pm.at[slot], me.at(x=x, y=y))
-            for slot, (x, y) in enumerate(square)
-        ]
-        w2_half.wait_recv()
-
-        def add2(g):
-            s2[g] = total_of(s2[g], g2[g, me.c]).astype(low_type)
-
-        loop(GROUPS, add2)
-        w2_push = [
-            copies.push(s2.at[to], p2.at[slot + 1], swapped[slot + 1])
-            for slot, to in enumerate(line)
-        ]
-        exchanged = pltpu.make_async_remote_copy(
-            src_ref=s2.at[me.g],
-            dst_ref=p2.at[0],
-            send_sem=swap_send,
-            recv_sem=swap_recv,
-            device_id=swapped[0],
-            device_id_type=MESH,
-        )
-        stays = pltpu.make_async_copy(s2.at[me.g], p2.at[0], swap_recv)
-
-        @pl.when(me.crossing)
-        def _():
-            exchanged.start()
-
-        @pl.when(jnp.logical_not(me.crossing))
-        def _():
-            stays.start()
-
-        k_half[3].wait_recv()
-        for copy in k_push:
-            copy.wait_recv()
-
-        def addg(slot):
+        pair_sum(sm, gm)
+        wm_push = square_push(sm, pm)
+
+        move = Scatter(dx_send, dx_recv, me.selfish)
+        for index, (slot, device) in enumerate(owners):
+            for copy in k_push[3 * index : 3 * index + 3]:
+                copy.wait_recv()
             u, v = slot // 2, slot % 2
             grads[slot, :, :WIDE] = total_of(
-                kst[me.x, me.y, u, v],
+                kst[u, v, me.p, me.y],
                 dkv_ref[u, me.c, v, me.p, me.y],
-                *[pk[index, u, v] for index in range(3)],
+                *[pk[index, peer] for peer in range(3)],
             ).astype(low_type)
-            grads[slot, :, WIDE:] = dq_ref[slot]
-
-        loop(GROUPS, addg)
-        for slot in range(GROUPS):
             dxs[slot] = lax.dot_general(
                 grads[slot], w_ref[:, : 2 * WIDE], NEXT, preferred_element_type=wide
             ).astype(low_type)
-        move = Scatter(dx_send, dx_recv, me.selfish)
-        move.start(
-            [(dxs.at[slot], device) for slot, device in me.owners()], dx_out.at[me.g], me.g
-        )
-        every = grads[...].reshape(GROUPS * n, 2 * WIDE)
-        bias = jnp.sum(every.astype(wide), axis=0, keepdims=True)
-        bias = jnp.broadcast_to(bias, (rows - s, 2 * WIDE)).astype(low_type)
-        for half in range(2):
-            made = lax.dot_general(
-                tok[:, :, half * cut : (half + 1) * cut].reshape(GROUPS * n, cut),
-                every,
-                DOWN,
-                preferred_element_type=wide,
-            ).astype(low_type)
-            for index in range(16):
-                x, c, g, y = half, index // 8, index // 2 % GROUPS, index % 2
-                gq[x, c, g, y, :s] = made[index * s : (index + 1) * s]
-                gq[x, c, g, y, s:] = bias
-        q_half = copies.push(gq.at[:, other], sq, me.sibling())
-
+            move.send_one(dxs.at[slot], dx_out.at[me.g], me.g, device)
+            if index == 1:
+                for copy in q_push:
+                    copy.wait_recv()
+                square_sum(fq, sq, pq)
+                arrivals = [
+                    copies.push(fq.at[to], outq.at[me.g], me.at(g=to)) for to in line
+                ]
+                kept = [copies.keep(fq.at[me.g], outq.at[me.g])]
+                for copy in w1_push:
+                    copy.wait_recv()
+
+                def addw(index):
+                    x, y = index // 2, index % 2
+                    f1[x, y] = total_of(
+                        s1[x, me.g, y], *[p1[peer, x, y] for peer in range(3)]
+                    ).astype(low_type)
+
+                loop(4, addw)
+                quarter = out1.at[me.x * 2 + me.y]
+                arrivals += [
+                    copies.push(f1.at[x, y], quarter, me.at(x=x, y=y)) for x, y in square
+                ]
+                kept.append(copies.keep(f1.at[me.x, me.y], quarter))
+        weight_grad(grads[:, :, :WIDE].reshape(GROUPS * n, WIDE), gk)
+        half = copies.push(gk.at[:, other], sk, me.sibling())
         for copy in wm_push:
             copy.wait_recv()
-
-        def addf(g):
-            fm[g] = total_of(sm[me.x, g, me.y], pm[0, g], pm[1, g], pm[2, g]).astype(low_type)
-
-        loop(GROUPS, addf)
+        square_sum(fm, sm, pm)
         wm_last = [
-            copies.push(fm.at[to], tm.at[slot], me.at(g=to)) for slot, to in enumerate(line)
-        ]
-        q_half.wait_recv()
-
-        def addq(index):
-            x, g, y = at8(index)
-            sq[x, g, y] = total_of(sq[x, g, y], gq[x, me.c, g, y]).astype(low_type)
-
-        loop(16, addq)
-        q_push = [
-            copies.push(sq.at[x, :, y], pq.at[slot], me.at(x=x, y=y))
-            for slot, (x, y) in enumerate(square)
-        ]
-        for copy in w1_push:
-            copy.wait_recv()
-
-        def addw(index):
-            x, y = index // 2, index % 2
-            f1[x, y] = total_of(s1[x, me.g, y], *[p1[slot, x, y] for slot in range(3)]).astype(
-                low_type
-            )
-
-        loop(4, addw)
-        quarter = out1.at[me.x * 2 + me.y]
-        arrivals = [copies.push(f1.at[x, y], quarter, me.at(x=x, y=y)) for x, y in square]
-        kept = [copies.keep(f1.at[me.x, me.y], quarter)]
-        for copy in q_push:
-            copy.wait_recv()
-
-        def addl(g):
-            fq[g] = total_of(sq[me.x, g, me.y], pq[0, g], pq[1, g], pq[2, g]).astype(low_type)
-
-        loop(GROUPS, addl)
-        arrivals += [copies.push(fq.at[to], outq.at[me.g], me.at(g=to)) for to in line]
-        kept.append(copies.keep(fq.at[me.g], outq.at[me.g]))
-
-        @pl.when(me.crossing)
-        def _():
-            exchanged.wait_recv()
-            exchanged.wait_send()
-
-        @pl.when(jnp.logical_not(me.crossing))
-        def _():
-            stays.wait()
-
-        for copy in w2_push:
-            copy.wait_recv()
-        out2[...] = total_of(*[p2[slot] for slot in range(4)])
+            copies.push(fm.at[to], tm.at[peer], me.at(g=to)) for peer, to in enumerate(line)
+        ]
+        half.wait_recv()
+        pair_sum(sk, gk)
+        push = square_push(sk, pp)
+        for copy in push:
+            copy.wait_recv()
+        square_sum(fk, sk, pp)
+        arrivals += [copies.push(fk.at[to], outk.at[me.g], me.at(g=to)) for to in line]
+        kept.append(copies.keep(fk.at[me.g], outk.at[me.g]))
         for copy in wm_last:
             copy.wait_recv()
-        outm[...] = total_of(fm[me.g], *[tm[slot] for slot in range(3)])
+        outm[...] = total_of(fm[me.g], *[tm[peer] for peer in range(3)])
         for copy in arrivals:
             copy.wait_recv()
         for g in range(GROUPS):
@@ -1462,69 +1433,76 @@
 
     vmem = pltpu.VMEM
     dma = pltpu.SemaphoreType.DMA
-    total = 48
+    total = 64
+
+    def stages(width):
+        return [
+            vmem((2, 2, GROUPS, 2, rows, width), low_type),
+            vmem((2, GROUPS, 2, rows, width), low_type),
+            vmem((3, GROUPS, rows, width), low_type),
+            vmem((GROUPS, rows, width), low_type),
+        ]
+
     return pl.pallas_call(
         body,
         name="last_kernel",
         out_shape=(
             jax.ShapeDtypeStruct((GROUPS, n, depth), low_type),
-            jax.ShapeDtypeStruct((GROUPS, rows, 2 * WIDE), low_type),
+            jax.ShapeDtypeStruct((GROUPS, rows, PACK), low_type),
+            jax.ShapeDtypeStruct((GROUPS, rows, WIDE), low_type),
             jax.ShapeDtypeStruct((4, rows, depth), low_type),
-            jax.ShapeDtypeStruct((tall, depth), wide),
-            jax.ShapeDtypeStruct((rowsm, depth), wide),
+            jax.ShapeDtypeStruct((rows, depth), wide),
         ),
-        in_specs=[pl.BlockSpec(memory_space=vmem)] * 7,
-        out_specs=[pl.BlockSpec(memory_space=space) for space in (pl.ANY, pl.ANY, pl.ANY, vmem, vmem)],
+        in_specs=[pl.BlockSpec(memory_space=vmem)] * 6,
+        out_specs=[pl.BlockSpec(memory_space=pl.ANY)] * 4 + [pl.BlockSpec(memory_space=vmem)],
         scratch_shapes=[
-            dma((total,)), dma((total,)), dma((4,)), dma((4,)), dma((4,)), dma, dma,
+            dma((total,)), dma((total,)), dma((4,)), dma((4,)), dma((4,)),
             vmem((2, 2, 2, 2, n, WIDE), low_type),
-            vmem((3, 2, 2, n, WIDE), low_type),
+            vmem((4, 3, n, WIDE), low_type),
             vmem((GROUPS, n, 2 * WIDE), low_type),
+            vmem((GROUPS, n, PACK), low_type),
             vmem((GROUPS, n, depth), low_type),
-            vmem((2, 2, GROUPS, 2, rows, 2 * WIDE), low_type),
-            vmem((2, GROUPS, 2, rows, depth), low_type),
+            *stages(PACK),
+            *stages(WIDE),
             vmem((3, 2, 2, rows, depth), low_type),
             vmem((2, 2, rows, depth), low_type),
-            vmem((GROUPS, tall, depth), low_type),
-            vmem((4, tall, depth), low_type),
-            vmem((2, GROUPS, 2, rowsm, depth), low_type),
-            vmem((3, GROUPS, rowsm, depth), low_type),
-            vmem((GROUPS, rowsm, depth), low_type),
-            vmem((3, rowsm, depth), low_type),
-            vmem((2, GROUPS, 2, rows, 2 * WIDE), low_type),
-            vmem((3, GROUPS, rows, 2 * WIDE), low_type),
-            vmem((GROUPS, rows, 2 * WIDE), low_type),
+            *stages(depth)[1:],
+            vmem((3, rows, depth), low_type),
         ],
         compiler_params=pltpu.CompilerParams(
             collective_id=11, has_side_effects=True, vmem_limit_bytes=VMEM_LIMIT
         ),
-    )(dkv, dq, tokens, weights, grad1, grad2, gradm)
-
-
-def final_kernel(hidden, pieces, outq, out1, out2, outm, s, e):
+    )(dkv, dq, tokens, weights, sum1, gradm)
+
+
+def final_kernel(hidden, pieces, outq, outk, out1, out2, outm, s, e):
     n, depth = hidden.shape
     quarter = out1.shape[-1]
 
-    def body(hid, dx, q_in, i_in, o_in, m_in, xg, qw, qb, kw, vw, vb, mw, mb, eg, es, iw, ib, ow, ob, fg, fs):
+    def body(hid, dx, q_in, k_in, i_in, o_in, m_in, xg, qw, qb, kw, vw, vb, mw, mb, eg, es, iw, ib, ow, ob, fg, fs):
         device = lax.axis_index("au") * lax.axis_size("row") + lax.axis_index("row")
         xg[...] = total_of(hid[...], dx[0], dx[1], dx[2], dx[3]).astype(low_type)
         rows = q_in.shape[1]
         lower = lax.broadcasted_iota(jnp.int32, (rows, LANES), 1) < HEAD
 
-        def part(head, offset):
+        def part(head):
             g, h = head // LOCAL, head % LOCAL
-            return q_in[g, :, offset + h * LANES : offset + (h + 1) * LANES].astype(wide)
-
+            return k_in[g, :, h * LANES : (h + 1) * LANES].astype(wide)
+
+        made_q = []
+        for g in range(0, GROUPS, 2):
+            a0, b0 = q_in[g, :, :LANES].astype(wide), q_in[g, :, LANES:].astype(wide)
+            a1 = pltpu.roll(q_in[g + 1, :, :LANES].astype(wide), HEAD, 1)
+            b1 = pltpu.roll(q_in[g + 1, :, LANES:].astype(wide), HEAD, 1)
+            made_q += [a0, jnp.where(lower, b0, a1), jnp.where(lower, a1, b1)]
         biases = [[], []]
         for pair in range(HEADS // 2):
             span = slice(pair * LANES, (pair + 1) * LANES)
-            kv = [part(2 * pair, 0), part(2 * pair + 1, 0)]
-            q = [part(2 * pair, WIDE), part(2 * pair + 1, WIDE)]
-            made_q = jnp.where(lower, q[0], pltpu.roll(q[1], HEAD, 1))
+            kv = [part(2 * pair), part(2 * pair + 1)]
             made_k = jnp.where(lower, kv[0], pltpu.roll(kv[1], HEAD, 1))
             made_v = jnp.where(lower, pltpu.roll(kv[0], HEAD, 1), kv[1])
-            qw[:, span], kw[:, span], vw[:, span] = made_q[:s], made_k[:s], made_v[:s]
-            biases[0].append(made_q[s:])
+            qw[:, span], kw[:, span], vw[:, span] = made_q[pair][:s], made_k[:s], made_v[:s]
+            biases[0].append(made_q[pair][s:])
             biases[1].append(made_v[s:])
 
         def own(eight, width, shift):
@@ -1560,10 +1538,301 @@
             shape(s, 4 * quarter), shape(1, e), shape(e, depth),
             shape(1, s), shape(1, s), shape(1, s),
         ),
-        in_specs=[pl.BlockSpec(memory_space=vmem)] * 6,
+        in_specs=[pl.BlockSpec(memory_space=vmem)] * 7,
         out_specs=(pl.BlockSpec(memory_space=vmem),) * 16,
         compiler_params=pltpu.CompilerParams(vmem_limit_bytes=VMEM_LIMIT),
-    )(hidden, pieces, outq, out1, out2, outm)
+    )(hidden, pieces, outq, outk, out1, out2, outm)
+
+
+def gelu_and_slope(value):
+    t = 1.0 / (1.0 + (0.3275911 * 0.7071067811865476) * jnp.abs(value))
+    bell = jnp.exp(-0.5 * value * value)
+    tail = 1.061405429
+    for weight in (-1.453152027, 1.421413741, -0.284496736, 0.254829592):
+        tail = tail * t + weight
+    tail = 0.5 * tail * t * bell
+    below = jnp.where(value >= 0.0, 1.0 - tail, tail)
+    return value * below, below + value * bell * 0.3989422804014327
+
+
+def normed(hidden):
+    mean = jnp.mean(hidden, axis=-1, keepdims=True)
+    centered = hidden - mean
+    spread = jnp.mean(centered * centered, axis=-1, keepdims=True)
+    inverse = lax.rsqrt(spread + eps_norm)
+    return centered * inverse, inverse
+
+
+def normed_grad(grad, norm, inverse):
+    mean = jnp.mean(grad, axis=-1, keepdims=True)
+    along = jnp.mean(grad * norm, axis=-1, keepdims=True)
+    return inverse * (grad - mean - norm * along)
+
+
+def down_sum(values):
+    return jnp.sum(values, axis=0, keepdims=True)
+
+
+def middle_kernel(mixed, tokens, cotangent, mix, inner, outer, vec, s, e):
+    n, depth = tokens.shape
+    quarter = inner.shape[1]
+    rows = s + 8
+    cut = depth // 2
+
+    def body(
+        mixed_ref, tok, cot, wm_in, w1_in, w2_in, vec_ref,
+        out, hidden_out, do_out, gm, s1, out2,
+        send, recv, local, back_send, back_recv, on_send, on_recv, swap_send, swap_recv,
+        wm, w1, w2, came, mixed_tok, xs, acts, slopes, parts, sums, bgs, igs, parts2, sums2,
+        pieces, extra, norm_keep, g1, g2, s2, p2,
+    ):
+        me = Spot()
+        copies = Copies(send, recv, local)
+        square = me.square()
+        line = [to for to, _ in me.line()]
+        owners = me.owners()
+        readers = me.readers()
+        swapped = [me.at(g=to, c=me.y, y=me.c) for to in [me.g] + line]
+        barrier, expected = announce(
+            [me.at(x=x, y=y) for x, y in square]
+            + swapped[1:]
+            + [device for _, device in readers[1:]]
+            + [device for _, device in owners[1:]]
+            + [me.sibling()],
+            [
+                (jnp.logical_not(me.selfish), readers[0][1]),
+                (jnp.logical_not(me.selfish), owners[0][1]),
+                (me.crossing, swapped[0]),
+            ],
+        )
+        loads = [copies.keep(wm_in, wm), copies.keep(w1_in, w1), copies.keep(w2_in, w2)]
+        pl.semaphore_wait(barrier, expected)
+
+        back = Scatter(back_send, back_recv, me.selfish)
+        back.start([(mixed_ref.at[slot], device) for slot, device in owners], came.at[me.g], me.g)
+        lower = lax.broadcasted_iota(jnp.int32, (n, LANES), 1) < HEAD
+        loads[0].wait()
+        for g in range(GROUPS):
+            back.arrived(g, came.at[g])
+        for half in range(2):
+            a0 = came[2 * half, :, :LANES]
+            b0 = came[2 * half, :, LANES:].astype(wide)
+            a1 = pltpu.roll(came[2 * half + 1, :, :LANES].astype(wide), HEAD, 1)
+            b1 = pltpu.roll(came[2 * half + 1, :, LANES:].astype(wide), HEAD, 1)
+            base = half * 3 * LANES
+            mixed_tok[:, base : base + LANES] = a0
+            mixed_tok[:, base + LANES : base + 2 * LANES] = jnp.where(lower, b0, a1).astype(low_type)
+            mixed_tok[:, base + 2 * LANES : base + 3 * LANES] = jnp.where(lower, a1, b1).astype(
+                low_type
+            )
+
+        def vector(index):
+            return vec_ref[index : index + 1, :]
+
+        attn = jnp.dot(mixed_tok[...], wm[...], preferred_element_type=wide) + vector(2)
+        norm1, inverse1 = normed(tok[...].astype(wide) + attn)
+        early = norm1 * vector(3) + vector(4)
+        norm_keep[...] = norm1
+        mine = me.x * 2 + me.y
+        xs[mine] = early.astype(low_type)
+        early_go = [copies.push(xs.at[mine], xs.at[mine], me.at(x=x, y=y)) for x, y in square]
+        loads[1].wait()
+        loads[2].wait()
+
+        def forward(place):
+            inner = jnp.dot(xs[place], w1[...], preferred_element_type=wide) + vector(8)
+            act, slope = gelu_and_slope(inner)
+            acts[place] = act.astype(low_type)
+            slopes[place] = slope
+            return jnp.dot(acts[place], w2[...], preferred_element_type=wide)
+
+        own = forward(mine)
+        branch_go = []
+        for copy, (x, y) in zip(early_go, square):
+            copy.wait_recv()
+            place = x * 2 + y
+            parts[place] = forward(place).astype(low_type)
+            branch_go.append(copies.push(parts.at[place], sums.at[mine], me.at(x=x, y=y)))
+        for copy in branch_go:
+            copy.wait_recv()
+        branch = total_of(own, *[sums[x * 2 + y] for x, y in square]) + vector(5)
+        norm2, inverse2 = normed(early + branch)
+        out[...] = (norm2 * vector(6) + vector(7)).astype(low_type)
+        cot_wide = cot[...].astype(wide)
+        final_grad = normed_grad(cot_wide * vector(6), norm2, inverse2)
+        bgs[mine] = final_grad.astype(low_type)
+        grad_go = [copies.push(bgs.at[mine], bgs.at[mine], me.at(x=x, y=y)) for x, y in square]
+        extra[...] = jnp.zeros_like(extra)
+        extra[3:4, :] = down_sum(bgs[mine].astype(wide))
+        extra[4:5, :] = down_sum(cot_wide * norm2)
+        extra[5:6, :] = down_sum(cot_wide)
+
+        def backward(place):
+            grad = lax.dot_general(bgs[place], w2[...], NEXT, preferred_element_type=wide)
+            igs[place] = (grad * slopes[place]).astype(low_type)
+            return lax.dot_general(igs[place], w1[...], NEXT, preferred_element_type=wide)
+
+        own = backward(mine)
+        token_go = []
+        for copy, (x, y) in zip(grad_go, square):
+            copy.wait_recv()
+            place = x * 2 + y
+            parts2[place] = backward(place).astype(low_type)
+            token_go.append(copies.push(parts2.at[place], sums2.at[mine], me.at(x=x, y=y)))
+
+        other = 1 - me.c
+        grads = bgs[...].reshape(4 * n, depth)
+        for half in range(2):
+            span = slice(half * cut, (half + 1) * cut)
+            made = lax.dot_general(
+                acts[:, :, span].reshape(4 * n, cut), grads, DOWN, preferred_element_type=wide
+            )
+            g2[2 * half : 2 * half + 2] = made.astype(low_type).reshape(2, 2, e, depth)
+        w2_half = copies.push(g2.at[:, other], s2, me.sibling())
+
+        grads = igs[...].reshape(4 * n, quarter)
+        bias = jnp.broadcast_to(down_sum(grads.astype(wide)), (8, quarter)).astype(low_type)
+        for half in range(2):
+            span = slice(half * cut, (half + 1) * cut)
+            made = lax.dot_general(
+                xs[:, :, span].reshape(4 * n, cut), grads, DOWN, preferred_element_type=wide
+            ).astype(low_type)
+            for index in range(16):
+                place = (half, index // 8, index // 2 % GROUPS, index % 2)
+                g1[(*place, slice(None, s))] = made[index * s : (index + 1) * s]
+                g1[(*place, slice(s, None))] = bias
+        w1_half = copies.push(g1.at[:, other], s1, me.sibling())
+        w2_half.wait_recv()
+
+        def add2(g):
+            s2[g] = s2[g] + g2[g, me.c]
+
+        loop(GROUPS, add2)
+        w2_push = [
+            copies.push(s2.at[to], p2.at[index + 1], swapped[index + 1])
+            for index, to in enumerate(line)
+        ]
+        exchanged = pltpu.make_async_remote_copy(
+            src_ref=s2.at[me.g],
+            dst_ref=p2.at[0],
+            send_sem=swap_send,
+            recv_sem=swap_recv,
+            device_id=swapped[0],
+            device_id_type=MESH,
+        )
+        stays = pltpu.make_async_copy(s2.at[me.g], p2.at[0], swap_recv)
+
+        @pl.when(me.crossing)
+        def _():
+            exchanged.start()
+
+        @pl.when(jnp.logical_not(me.crossing))
+        def _():
+            stays.start()
+
+        w1_half.wait_recv()
+
+        def add1(index):
+            x, g, y = index // 8, index // 2 % GROUPS, index % 2
+            s1[x, g, y] = s1[x, g, y] + g1[x, me.c, g, y]
+
+        loop(16, add1)
+        for copy in token_go:
+            copy.wait_recv()
+        early_grad = total_of(final_grad, own, *[sums2[x * 2 + y] for x, y in square])
+        norm1 = norm_keep[...]
+        extra[1:2, :] = down_sum(early_grad * norm1)
+        extra[2:3, :] = down_sum(early_grad)
+        hidden = normed_grad(early_grad * vector(3), norm1, inverse1)
+        hidden_out[...] = hidden
+        attn_grad = hidden.astype(low_type)
+        extra[0:1, :] = down_sum(attn_grad.astype(wide))
+        back_grad = lax.dot_general(attn_grad, wm[...], NEXT, preferred_element_type=wide)
+        for half in range(2):
+            base = half * 3 * LANES
+            t0 = back_grad[:, base : base + LANES]
+            t1 = back_grad[:, base + LANES : base + 2 * LANES]
+            t2 = back_grad[:, base + 2 * LANES : base + 3 * LANES]
+            r1, r2 = pltpu.roll(t1, HEAD, 1), pltpu.roll(t2, HEAD, 1)
+            pieces[2 * half, :, :LANES] = t0.astype(low_type)
+            pieces[2 * half, :, LANES:] = jnp.where(lower, t1, 0.0).astype(low_type)
+            pieces[2 * half + 1, :, :LANES] = jnp.where(lower, r1, r2).astype(low_type)
+            pieces[2 * half + 1, :, LANES:] = jnp.where(lower, r2, 0.0).astype(low_type)
+        onward = Scatter(on_send, on_recv, me.selfish)
+        slot = me.slot()
+        onward.start([(pieces.at[g], device) for g, device in readers], do_out.at[slot], slot)
+
+        for half in range(2):
+            span = slice(half * cut, (half + 1) * cut)
+            made = lax.dot_general(
+                mixed_tok[:, span], attn_grad, DOWN, preferred_element_type=wide
+            ).astype(low_type)
+            for index in range(16):
+                place = (half, index // 8, index // 2 % GROUPS, index % 2)
+                gm[(*place, slice(None, s))] = made[index * s : (index + 1) * s]
+                gm[(*place, slice(s, None))] = extra[...].astype(low_type)
+        @pl.when(me.crossing)
+        def _():
+            exchanged.wait_recv()
+            exchanged.wait_send()
+
+        @pl.when(jnp.logical_not(me.crossing))
+        def _():
+            stays.wait()
+
+        for copy in w2_push:
+            copy.wait_recv()
+        out2[...] = total_of(*[p2[index] for index in range(4)])
+        for index in range(GROUPS):
+            onward.arrived(index, do_out.at[index])
+        back.finish()
+        onward.finish()
+        copies.finish()
+
+    vmem = pltpu.VMEM
+    dma = pltpu.SemaphoreType.DMA
+    tall = vmem((4, n, depth), low_type)
+    space = [vmem] * 3 + [pl.ANY] * 3 + [vmem]
+    return pl.pallas_call(
+        body,
+        name="middle_kernel",
+        out_shape=(
+            jax.ShapeDtypeStruct((n, depth), low_type),
+            jax.ShapeDtypeStruct((n, depth), wide),
+            jax.ShapeDtypeStruct((GROUPS, n, PACK), low_type),
+            jax.ShapeDtypeStruct((2, 2, GROUPS, 2, rows, depth), low_type),
+            jax.ShapeDtypeStruct((2, GROUPS, 2, rows, quarter), low_type),
+            jax.ShapeDtypeStruct((e, depth), wide),
+        ),
+        in_specs=[pl.BlockSpec(memory_space=item) for item in space],
+        out_specs=[
+            pl.BlockSpec(memory_space=item) for item in (vmem, vmem, pl.ANY, vmem, vmem, vmem)
+        ],
+        scratch_shapes=[
+            dma((40,)), dma((40,)), dma((8,)), dma((4,)), dma((4,)), dma((4,)), dma((4,)), dma, dma,
+            vmem((depth, depth), low_type),
+            vmem((depth, quarter), low_type),
+            vmem((quarter, depth), low_type),
+            vmem((GROUPS, n, PACK), low_type),
+            vmem((n, depth), low_type),
+            tall,
+            vmem((4, n, quarter), low_type),
+            vmem((4, n, quarter), wide),
+            tall, tall, tall,
+            vmem((4, n, quarter), low_type),
+            tall, tall,
+            vmem((GROUPS, n, PACK), low_type),
+            vmem((8, depth), wide),
+            vmem((n, depth), wide),
+            vmem((2, 2, GROUPS, 2, rows, quarter), low_type),
+            vmem((GROUPS, 2, e, depth), low_type),
+            vmem((GROUPS, e, depth), low_type),
+            vmem((4, e, depth), low_type),
+        ],
+        compiler_params=pltpu.CompilerParams(
+            collective_id=12, has_side_effects=True, vmem_limit_bytes=VMEM_LIMIT
+        ),
+    )(mixed, tokens, cotangent, mix, inner, outer, vec)
 
 
 def on_device_general(
@@ -1844,9 +2113,7 @@
     w1 = w1.reshape(depth, quarter)
     w2 = w2.reshape(quarter, depth)
     wm = wm.reshape(depth, depth)
-    m_bias, e_gain, e_shift, o_bias, f_gain, f_shift, i_bias = [vec[i] for i in range(2, 9)]
-
-    tile, block = 128, 512
+    tile, block = 128, 1024
     count = doc_lengths.shape[0]
     upto = jnp.arange(count)[None, :] <= jnp.arange(count)[:, None]
     ends = jnp.sum(jnp.where(upto, doc_lengths[None, :], 0), axis=1)
@@ -1867,43 +2134,10 @@
     mixed, mixed_wide, lse = attend_forward(
         queries, kv_all, bounds, first[:, None], last[:, None], tile, block
     )
-    mixed_tok = pass_back(2, mixed.reshape(GROUPS, n, PACK))
-    mixed_tok = jnp.transpose(mixed_tok[:, :, : LOCAL * HEAD], (1, 0, 2)).reshape(n, depth)
-
-    attn = jnp.dot(mixed_tok, wm, preferred_element_type=wide) + m_bias
-    early, early_pull = jax.vjp(layer_norm, tokens.astype(wide) + attn, e_gain, e_shift)
-    early_all = gather_square(1, 3, early.astype(low_type)).reshape(rows, depth)
-    inner = jnp.dot(early_all, w1, preferred_element_type=wide) + i_bias
-    act, gelu_pull = jax.vjp(gelu_exact, inner)
-    act_low = act.astype(low_type)
-    partial = jnp.dot(act_low, w2, preferred_element_type=wide).astype(low_type)
-    partial = exchange_square(1, 4, partial.reshape(2, 2, n, depth))
-    branch = jnp.sum(partial.astype(wide), axis=(0, 1)) + o_bias
-    result, final_pull = jax.vjp(layer_norm, early + branch, f_gain, f_shift)
-    output = result.astype(low_type)
-    final_grads = final_pull(cotangent.astype(wide))
-    branch_grad = final_grads[0].astype(low_type)
-    outer_bias_grad = jnp.sum(branch_grad.astype(wide), axis=0)
-    branch_all = gather_square(1, 5, branch_grad).reshape(rows, depth)
-    act_grad = jnp.einsum("td,fd->tf", branch_all, w2, preferred_element_type=wide)
-    inner_grad = gelu_pull(act_grad)[0].astype(low_type)
-    partial = jnp.einsum("tf,df->td", inner_grad, w1, preferred_element_type=wide).astype(low_type)
-    partial = exchange_square(1, 6, partial.reshape(2, 2, n, depth))
-    grad2 = jnp.einsum("tf,td->fd", act_low, branch_all, preferred_element_type=wide)
-    grad1 = jnp.einsum("td,tf->df", early_all, inner_grad, preferred_element_type=wide)
-    inner_bias_grad = jnp.sum(inner_grad.astype(wide), axis=0)
-    early_grad = final_grads[0] + jnp.sum(partial.astype(wide), axis=(0, 1))
-    early_grads = early_pull(early_grad)
-    attn_grad = early_grads[0].astype(low_type)
-    mixed_grad = jnp.einsum("td,cd->tc", attn_grad, wm, preferred_element_type=wide)
-    mixed_grad = jnp.transpose(
-        mixed_grad.astype(low_type).reshape(n, GROUPS, LOCAL * HEAD), (1, 0, 2)
-    )
-    mixed_grad = jnp.pad(mixed_grad, ((0, 0), (0, 0), (0, PACK - LOCAL * HEAD)))
-    grad_all = pass_on(7, mixed_grad).reshape(rows, PACK)
-    gradm = jnp.einsum("tc,td->cd", mixed_tok, attn_grad, preferred_element_type=wide)
-    mix_bias_grad = jnp.sum(attn_grad.astype(wide), axis=0)
-
+    output, hidden_grad, grad_all, gradm, sum1, out2 = middle_kernel(
+        mixed.reshape(GROUPS, n, PACK), tokens, cotangent, wm, w1, w2, vec, s, e
+    )
+    grad_all = grad_all.reshape(rows, PACK)
     delta = jnp.sum(
         (grad_all.astype(wide) * mixed_wide)[:, : LOCAL * HEAD].reshape(rows, LOCAL, HEAD), axis=2
     )
@@ -1922,28 +2156,15 @@
     stats = jnp.pad(stats, ((0, 0), (0, 0), (0, 4), (0, 0)))
     query_grad, dkv = attend_backward(queries, kv_all, grad_all, stats, bounds, tile, block)
 
-    def slabs(grad, extras):
-        grad = grad.astype(low_type).reshape(devices, s, -1)
-        extras = jnp.pad(extras.astype(low_type), ((0, 8 - extras.shape[0]), (0, 0)))
-        extras = jnp.broadcast_to(extras[None], (devices,) + extras.shape)
-        return jnp.concatenate([grad, extras], axis=1).reshape(2, 2, GROUPS, 2, s + 8, -1)
-
-    mix_extras = jnp.stack(
-        [
-            mix_bias_grad, early_grads[1], early_grads[2],
-            outer_bias_grad, final_grads[1], final_grads[2],
-        ]
-    )
-    pieces, outq, out1, out2, outm = last_kernel(
+    pieces, outq, outk, out1, outm = last_kernel(
         dkv.reshape(2, 2, 2, 2, 2, n, WIDE),
         query_grad.reshape(GROUPS, n, WIDE),
         toks,
         w_qkv,
-        slabs(grad1, inner_bias_grad[None]),
-        grad2.astype(low_type).reshape(GROUPS, 2, e, depth),
-        slabs(gradm, mix_extras),
-    )
-    results = final_kernel(early_grads[0], pieces, outq, out1, out2, outm, s, e)
+        sum1,
+        gradm,
+    )
+    results = final_kernel(hidden_grad, pieces, outq, outk, out1, out2, outm, s, e)
     return (output,) + tuple(
         result.reshape(-1) if result.shape[0] == 1 else result for result in results
     )

time: 291 us -> 250 us (0.86); the launches traced: 286 us -> 250 us
  matrix products: 19.6 us -> 0 us
  other arithmetic: 13.7 us -> 3.43 us
  local copies, waits for them, and re-layouts: 6.49 us -> 2.75 us
    dot_general x9 -> x0, matrix products: 19.6 us -> none  [the longest x1 7.14 us: on_device(): inner = jnp.dot(early_all, w1, preferred_element_type=wide) + i_bias]
    pallas_call x6 -> x1, Pallas kernels: 59.8 us -> 76.1 us  [middle_kernel(): pl.pallas_call(body, name='middle_kernel', out_shape=(jax.ShapeDtypeStruc...]
    pallas_call x1, Pallas kernels: 29.7 us -> 21 us  [attend_backward(): pl.pallas_call(body, name='attend_backward', grid=(LOCAL,), out_shape=(ja...]
    reduce_sum x12 -> x0, other arithmetic: 6.77 us -> none  [the longest x3 1.52 us: layer_norm(): return centered * lax.rsqrt(spread + eps_norm) * gain + shift]
    pallas_call x1, Pallas kernels: 20.7 us -> 14.6 us  [attend_forward(): pl.pallas_call(body, name='attend_forward', out_shape=(jax.ShapeDtypeStru...]
    pallas_call x1, Pallas kernels: 66.8 us -> 63.1 us  [last_kernel(): pl.pallas_call(body, name='last_kernel', out_shape=(jax.ShapeDtypeStruct(...]
where the time goes in v3:
time: 250 us
  Pallas kernels  243 us (97%)
  other arithmetic  3.43 us (1%)
  local copies, waits for them, and re-layouts  2.75 us (1%)
    pallas_call x1, Pallas kernels, middle_kernel(): pl.pallas_call(body, name='middle_kernel', out_shape=(jax.ShapeDtypeStruc...  76.1 us
    pallas_call x1, Pallas kernels, first_kernel(): pl.pallas_call(body, name='first_kernel', out_shape=(jax.ShapeDtypeStruct...  65.4 us
    pallas_call x1, Pallas kernels, last_kernel(): pl.pallas_call(body, name='last_kernel', out_shape=(jax.ShapeDtypeStruct(...  63.1 us
    pallas_call x1, Pallas kernels, attend_backward(): pl.pallas_call(body, name='attend_backward', grid=(LOCAL,), out_shape=(ja...  21 us
    pallas_call x1, Pallas kernels, attend_forward(): pl.pallas_call(body, name='attend_forward', out_shape=(jax.ShapeDtypeStru...  14.6 us

profile of v3, /device:TPU:0, one launch (start us, length us, event | category | flops | bytes accessed | tf_op | source)
XLA Modules:
  0.0 249.8 jit_solution(8316074941681057827)
XLA Ops:
  0.7 0.1 add_bitcast_fusion
  0.8 0.8 select_reduce_fusion
  1.6 0.1 fusion
  1.7 0.9 copy.42.low_ref
  2.5 0.9 copy.43.high_ref
  3.4 0.1 add_select_fusion
  3.5 0.7 pad_add_fusion.bounds_ref
  4.1 65.4 %first_kernel.1 = (bf16[4,128,768]{2,1,0:T(8,128)(2,1)}, bf16[4,128,384]{2,1,0:T(8,128)(2,1)}, bf16[4,4,2,24,896]{4,3,2,1,0:T(8,128)(2,1)}, f32[16,768]{1,0:T(8,...) custom-call(bf16[128,768]{1,0:T(8,128)(2,1)} %tok.1, ...), custom_call_target="tpu_custom_call" | custom-call | tf_op jit(solution)/shard_map/first_kernel/pallas_call | solution.py:1174
  69.5 14.6 %attend_forward.1 = (bf16[512,256]{1,0:T(8,128)(2,1)}, f32[512,256]{1,0:T(8,128)}, f32[512,128]{1,0:T(8,128)}) custom-call(s32[4,2]{1,0:T(4,128)} %pad_add_fusion.bounds_ref, bf16[512,384]{1,0:T(8,128)(2,1)} %bitcast.50, bf16[4096,384]{1,0:T(8,128)(2,1)} %bitcast.47, s32[512,1]{1,0:T(8,128)} %copy.42.low_ref, s32[512,1]{1,0:T(8,128)} %copy.43.high_ref), custom_call_target="tpu_custom_call" | custom-call | tf_op jit(solution)/shard_map/attend_forward/pallas_call | solution.py:759
  84.1 0.0 copy-start
  84.1 76.1 %middle_kernel.1 = (bf16[128,768]{1,0:T(8,128)(2,1)}, f32[128,768]{1,0:T(8,128)}, bf16[4,128,256]{2,1,0:T(8,128)(2,1)}, bf16[2,2,4,2,32,768]{5,4,3,2,1,0:T(8,128...) custom-call(bf16[4,128,256]{2,1,0:T(8,128)(2,1)} %bitcast.60, bf16[128,768]{1,0:T(8,128)(2,1)} %tok.1, ...), custom_call_target="tpu_custom_call" | custom-call | tf_op jit(solution)/shard_map/middle_kernel/pallas_call | solution.py:1796
  160.2 0.0 copy-start.1
  160.2 0.0 copy-done
  160.3 1.0 slice_multiply_fusion
  161.3 0.2 copy.45
  161.6 0.0 copy-done.1
  161.6 0.1 copy.48
  161.7 0.7 select_maximum_fusion.stat_ref
  162.4 21.0 %attend_backward.1 = (bf16[512,384]{1,0:T(8,128)(2,1)}, bf16[4096,384]{1,0:T(8,128)(2,1)}) custom-call(s32[4,2]{1,0:T(4,128)} %pad_add_fusion.bounds_ref, bf16[512,384]{1,0:T(8,128)(2,1)} %bitcast.51, bf16[4096,384]{1,0:T(8,128)(2,1)} %bitcast.48, bf16[512,256]{1,0:T(8,128)(2,1)} %bitcast.58, f32[4,3,8,128]{3,2,1,0:T(8,128)} %select_maximum_fusion.stat_ref), custom_call_target="tpu_custom_call" | custom-call | tf_op jit(solution)/shard_map/attend_backward/pallas_call | solution.py:829
  183.4 63.1 %last_kernel.1 = (bf16[4,128,768]{2,1,0:T(8,128)(2,1)}, bf16[4,32,256]{2,1,0:T(8,128)(2,1)}, bf16[4,32,384]{2,1,0:T(8,128)(2,1)}, bf16[4,32,768]{2,1,0:T(8,128)(2,1)}, f32[32,768]{1,0:T(8,128)}) custom-call(bf16[2,2,2,2,2,128,384]{6,5,4,3,2,1,0:T(8,128)(2,1)} %bitcast.49, bf16[4,128,384]{2,1,0:T(8,128)(2,1)} %bitcast.59, ...), custom_call_target="tpu_custom_call" | custom-call | tf_op jit(solution)/shard_map/last_kernel/pallas_call | solution.py:1446
  246.5 0.0 copy-start.2
  246.5 2.6 %final_kernel.1 = (bf16[128,768]{1,0:T(8,128)(2,1)}, f32[24,768]{1,0:T(8,128)}, f32[1,24]{1,0:T(1,128)}, f32[24,768]{1,0:T(8,128)}, f32[24,768]{1,0:T(8,128)}, /...) custom-call(f32[128,768]{1,0:T(8,128)} %get-tuple-element.65.hid, ...), custom_call_target="tpu_custom_call" | custom-call | tf_op jit(solution)/shard_map/final_kernel/pallas_call | solution.py:1531
  249.1 0.0 copy-done.2
  249.2 0.7 copy.50
  (8 shorter events, 0.1 us)
Async XLA Ops:
  84.1 76.1 %copy-start = (f32[512,256]{1,0:T(8,128)S(1)}, f32[512,256]{1,0:T(8,128)}, u32[]{:S(2)}) copy-start(f32[512,256]{1,0:T(8,128)} %get-tuple-element.68) | copy-start | bytes 1572868
  160.2 1.3 copy-start.1
  246.5 2.6 %copy-start.2 = (bf16[128,768]{1,0:T(8,128)(2,1)S(1)}, bf16[128,768]{1,0:T(8,128)(2,1)}, u32[]{:S(2)}) copy-start(bf16[128,768]{1,0:T(8,128)(2,1)} %get-tuple-element.120) | copy-start | bytes 589828

commit v4 on v3

--- a/solution.py
+++ b/solution.py
@@ -955,9 +955,9 @@
     return np.stack(rows + [np.zeros_like(column)] * 4).astype(np.int32)
 
 
-def first_kernel(tokens, wq, wk, wv, vectors, inner, outer, mix):
+def first_kernel(tokens, wq, wk, wv, vectors, inner, mix, e):
     n, depth = tokens.shape
-    s, e = wq.shape[0], outer.shape[0]
+    s = wq.shape[0]
     quarter = inner.shape[1] // 4
     cols = 2 * WIDE + LANES
     tables = jnp.asarray(first_tables(s, e, 2 * WIDE))
@@ -966,25 +966,23 @@
     def body(*refs):
         tok, wq_ref, wk_ref, wv_ref, tab = refs[:5]
         vecs = refs[5 : 5 + count]
-        w1f, w2f, wmf = refs[5 + count : 8 + count]
+        w1f, wmf = refs[5 + count : 7 + count]
         (
-            tok_out, q_out, wqkv_out, vec_out, kv_all, w1, w2, wm,
-            send, recv, local, tok_send, tok_recv, swap_send, swap_recv,
-            slab, toks, weights, kv_own, q_own, w1s, w2s, wms, vec, few,
-        ) = refs[8 + count :]
+            tok_out, q_out, wqkv_out, vec_out, kv_all, w1, wm,
+            send, recv, local, tok_send, tok_recv,
+            slab, toks, weights, kv_own, q_own, w1s, wms, vec, few,
+        ) = refs[7 + count :]
         me = Spot()
         copies = Copies(send, recv, local)
         square = me.square()
         line = [to for to, _ in me.line()]
         sources = [device for _, device in me.owners()]
-        swapped = [me.at(g=to, c=me.y, y=me.c) for to in [me.g] + line]
         barrier, expected = announce(
             [me.at(x=x, y=y) for x, y in square]
             + [me.at(g=to) for to in line]
-            + swapped[1:]
             + sources[1:]
             + [me.sibling()],
-            [(jnp.logical_not(me.selfish), sources[0]), (me.crossing, swapped[0])],
+            [(jnp.logical_not(me.selfish), sources[0])],
         )
         lane = lax.broadcasted_iota(jnp.int32, (s, LANES), 1)
         lower = lane < HEAD
@@ -1000,6 +998,7 @@
             slab[g, :, WIDE + h * LANES : WIDE + (h + 1) * LANES] = jnp.where(lower, q, 0.0).astype(
                 low_type
             )
+        wms[...] = wmf[...].astype(low_type)
         few[...] = jnp.zeros((s, LANES), wide)
         for index in range(count):
             few[index : index + 1, : vecs[index].shape[1]] = vecs[index][...]
@@ -1012,12 +1011,8 @@
         place = view.at[me.a, me.g, me.y]
         slab_first = [copies.push(slab.at[to], place, me.at(g=to)) for to in line]
         slab_own = copies.keep(slab.at[me.g], place)
-        tokens_go = Scatter(tok_send, tok_recv, me.selfish)
-        tokens_go.start([(tok, device) for _, device in me.readers()], toks.at[me.slot()], me.slot())
         for w in range(4):
             w1s[w] = w1f[:, w * quarter : (w + 1) * quarter].astype(low_type)
-        w2s[...] = w2f[...].astype(low_type)
-        wms[...] = wmf[...].astype(low_type)
         place = w1.at[me.x, me.c, me.g, me.y]
         w1_first = [
             copies.push(w1s.at[x * 2 + y], place, me.at(x=x, y=y)) for x, y in square
@@ -1029,6 +1024,11 @@
         slab_own.wait()
         for copy in slab_first:
             copy.wait_recv()
+        wm_first = [
+            copies.push(wms, wm.at[me.x, me.c, me.g, me.y], me.at(g=to)) for to in line
+        ]
+        tokens_go = Scatter(tok_send, tok_recv, me.selfish)
+        tokens_go.start([(tok, device) for _, device in me.readers()], toks.at[me.slot()], me.slot())
         block = view.at[me.a, :, me.y]
         slab_second = [copies.push(block, block, me.at(x=x, y=y)) for x, y in square]
         weight_arrivals.append(copies.push(block, block, me.sibling()))
@@ -1036,6 +1036,12 @@
             copy.wait_recv()
             block = view.at[x * 2 + me.c, :, y]
             weight_arrivals.append(copies.push(block, block, me.sibling()))
+        wm_own.wait()
+        for copy in wm_first:
+            copy.wait_recv()
+        block = wm.at[me.x, me.c, :, me.y]
+        wm_second = [copies.push(block, block, me.at(x=x, y=y)) for x, y in square]
+        arrivals.append(copies.push(block, block, me.sibling()))
         w1_own.wait()
         for copy in w1_first:
             copy.wait_recv()
@@ -1077,85 +1083,39 @@
             biases[1].append(jnp.where(lower, q, 0.0))
         bias = jnp.concatenate(biases[0] + biases[1], axis=1)
 
-        slots = [(u * 2 + v) for u in range(2) for v in range(2)]
-        for slot in slots:
-            tokens_go.arrived(slot, toks.at[slot])
-        block = w1.at[:, me.c, me.g, :]
-        w1_second = [copies.push(block, block, me.at(g=to)) for to in line]
-        wm_first = [
-            copies.push(wms, wm.at[me.x, me.c, me.g, me.y], me.at(g=to)) for to in line
-        ]
-        w2_place = w2.at[me.g, me.y]
-        w2_first = [
-            copies.push(w2s, w2_place, device) for device in swapped[1:]
-        ]
-        exchanged = pltpu.make_async_remote_copy(
-            src_ref=w2s,
-            dst_ref=w2_place,
-            send_sem=swap_send,
-            recv_sem=swap_recv,
-            device_id=swapped[0],
-            device_id_type=MESH,
-        )
-        stays = pltpu.make_async_copy(w2s, w2_place, swap_recv)
-
-        @pl.when(me.crossing)
-        def _():
-            exchanged.start()
-
-        @pl.when(jnp.logical_not(me.crossing))
-        def _():
-            stays.start()
-
         matrix = weights[:, :, :, :, : 2 * WIDE].reshape(depth, 2 * WIDE)
-        made = jnp.dot(
-            toks[...].reshape(GROUPS * n, depth), matrix, preferred_element_type=wide
-        )
-        made = (made + bias).astype(low_type).reshape(GROUPS, n, 2 * WIDE)
-        for slot in slots:
-            kv_own[slot // 2, slot % 2] = made[slot, :, :WIDE]
-            q_own[slot] = made[slot, :, WIDE:]
-        mine = kv_all.at[:, me.c, :, me.p, me.y]
-        kv_first = [copies.push(kv_own, mine, me.at(x=x, y=y)) for x, y in square]
-        arrivals.append(copies.push(kv_own, mine, me.sibling()))
+        kept, kv_first = [copies.keep(weights, wqkv_out), copies.keep(vec, vec_out)], []
+        for dv in range(2):
+            v = (me.half + dv) % 2
+            for u in range(2):
+                tokens_go.arrived(u * 2 + v, toks.at[u * 2 + v])
+            if dv:
+                block = w1.at[:, me.c, me.g, :]
+                w1_second = [copies.push(block, block, me.at(g=to)) for to in line]
+            both = jnp.concatenate([toks[v], toks[2 + v]], axis=0)
+            made = jnp.dot(both, matrix, preferred_element_type=wide)
+            made = (made + bias).astype(low_type)
+            for u in range(2):
+                kv_own[v, u] = made[u * n : (u + 1) * n, :WIDE]
+                q_own[u * 2 + v] = made[u * n : (u + 1) * n, WIDE:]
+            mine = kv_all.at[:, me.c, v, me.p, me.y]
+            kv_first.append(
+                [copies.push(kv_own.at[v], mine, me.at(x=x, y=y)) for x, y in square]
+            )
+            arrivals.append(copies.push(kv_own.at[v], mine, me.sibling()))
+            kept.append(copies.keep(kv_own.at[v], mine))
         block = w1.at[:, me.c, me.g, :]
         arrivals.append(copies.push(block, block, me.sibling()))
-        kept = [
-            copies.keep(kv_own, mine),
-            copies.keep(toks, tok_out),
-            copies.keep(q_own, q_out),
-            copies.keep(weights, wqkv_out),
-            copies.keep(vec, vec_out),
-        ]
-        wm_own.wait()
-        for copy in wm_first:
-            copy.wait_recv()
-        block = wm.at[me.x, me.c, :, me.y]
-        wm_second = [copies.push(block, block, me.at(x=x, y=y)) for x, y in square]
-        arrivals.append(copies.push(block, block, me.sibling()))
-
-        @pl.when(me.crossing)
-        def _():
-            exchanged.wait_recv()
-            exchanged.wait_send()
-
-        @pl.when(jnp.logical_not(me.crossing))
-        def _():
-            stays.wait()
-
-        block = w2.at[me.g, me.c]
-        arrivals.append(copies.push(block, block, me.sibling()))
-        for copy, (x, y) in zip(kv_first, square):
-            copy.wait_recv()
-            block = kv_all.at[:, me.c, :, (x + me.c) % 2, y]
-            arrivals.append(copies.push(block, block, me.sibling()))
+        kept += [copies.keep(toks, tok_out), copies.keep(q_own, q_out)]
+        for dv in range(2):
+            v = (me.half + dv) % 2
+            for copy, (x, y) in zip(kv_first[dv], square):
+                copy.wait_recv()
+                block = kv_all.at[:, me.c, v, (x + me.c) % 2, y]
+                arrivals.append(copies.push(block, block, me.sibling()))
         for copy, (x, y) in zip(wm_second, square):
             copy.wait_recv()
             block = wm.at[x, me.c, :, y]
-            arrivals.append(copies.push(block, block, me.sibling()))
-        for copy, (_, source) in zip(w2_first, me.line()):
-            copy.wait_recv()
-            block = w2.at[source, me.c]
             arrivals.append(copies.push(block, block, me.sibling()))
         for copy, (_, source) in zip(w1_second, me.line()):
             copy.wait_recv()
@@ -1181,20 +1141,18 @@
             jax.ShapeDtypeStruct((SMALL, 2 * WIDE), wide),
             jax.ShapeDtypeStruct((2, 2, 2, 2, 2, n, WIDE), low_type),
             jax.ShapeDtypeStruct((2, 2, GROUPS, 2, s, quarter), low_type),
-            jax.ShapeDtypeStruct((GROUPS, 2, e, depth), low_type),
             jax.ShapeDtypeStruct((2, 2, GROUPS, 2, s, depth), low_type),
         ),
-        in_specs=[pl.BlockSpec(memory_space=vmem)] * (8 + count),
-        out_specs=(pl.BlockSpec(memory_space=pl.ANY),) * 8,
+        in_specs=[pl.BlockSpec(memory_space=vmem)] * (7 + count),
+        out_specs=(pl.BlockSpec(memory_space=pl.ANY),) * 7,
         scratch_shapes=[
-            dma((total,)), dma((total,)), dma((8,)), dma((4,)), dma((4,)), dma, dma,
+            dma((total,)), dma((total,)), dma((12,)), dma((4,)), dma((4,)),
             vmem((GROUPS, s, cols), low_type),
             vmem((GROUPS, n, depth), low_type),
             vmem((4, GROUPS, 2, s, cols), low_type),
             vmem((2, 2, n, WIDE), low_type),
             vmem((GROUPS, n, WIDE), low_type),
             vmem((4, s, quarter), low_type),
-            vmem((e, depth), low_type),
             vmem((s, depth), low_type),
             vmem((SMALL, 2 * WIDE), wide),
             vmem((s, LANES), wide),
@@ -1202,7 +1160,7 @@
         compiler_params=pltpu.CompilerParams(
             collective_id=10, has_side_effects=True, vmem_limit_bytes=VMEM_LIMIT
         ),
-    )(tokens, wq, wk, wv, tables, *vectors, inner, outer, mix)
+    )(tokens, wq, wk, wv, tables, *vectors, inner, mix)
 
 
 def pass_back(ident, pieces):
@@ -1362,9 +1320,6 @@
         q_half.wait_recv()
         pair_sum(sq, gq)
         q_push = square_push(sq, pq)
-        wm_half.wait_recv()
-        pair_sum(sm, gm)
-        wm_push = square_push(sm, pm)
 
         move = Scatter(dx_send, dx_recv, me.selfish)
         for index, (slot, device) in enumerate(owners):
@@ -1403,17 +1358,20 @@
                     copies.push(f1.at[x, y], quarter, me.at(x=x, y=y)) for x, y in square
                 ]
                 kept.append(copies.keep(f1.at[me.x, me.y], quarter))
+        wm_half.wait_recv()
+        pair_sum(sm, gm)
+        wm_push = square_push(sm, pm)
         weight_grad(grads[:, :, :WIDE].reshape(GROUPS * n, WIDE), gk)
         half = copies.push(gk.at[:, other], sk, me.sibling())
+        half.wait_recv()
+        pair_sum(sk, gk)
+        push = square_push(sk, pp)
         for copy in wm_push:
             copy.wait_recv()
         square_sum(fm, sm, pm)
         wm_last = [
             copies.push(fm.at[to], tm.at[peer], me.at(g=to)) for peer, to in enumerate(line)
         ]
-        half.wait_recv()
-        pair_sum(sk, gk)
-        push = square_push(sk, pp)
         for copy in push:
             copy.wait_recv()
         square_sum(fk, sk, pp)
@@ -1578,13 +1536,14 @@
     quarter = inner.shape[1]
     rows = s + 8
     cut = depth // 2
+    hn = n // 2
 
     def body(
-        mixed_ref, tok, cot, wm_in, w1_in, w2_in, vec_ref,
+        mixed_ref, tok, cot, wm_in, w1_in, w2f, vec_ref,
         out, hidden_out, do_out, gm, s1, out2,
         send, recv, local, back_send, back_recv, on_send, on_recv, swap_send, swap_recv,
-        wm, w1, w2, came, mixed_tok, xs, acts, slopes, parts, sums, bgs, igs, parts2, sums2,
-        pieces, extra, norm_keep, g1, g2, s2, p2,
+        swap_send2, swap_recv2, wm, w1, w2p, w2s, came, mixed_tok, xs, acts, slopes, parts, sums, bgs, igs, parts2, sums2,
+        pieces, extra, attn, own1, own2, g1, g2, s2, p2,
     ):
         me = Spot()
         copies = Copies(send, recv, local)
@@ -1605,7 +1564,8 @@
                 (me.crossing, swapped[0]),
             ],
         )
-        loads = [copies.keep(wm_in, wm), copies.keep(w1_in, w1), copies.keep(w2_in, w2)]
+        loads = [copies.keep(wm_in, wm), copies.keep(w1_in, w1)]
+        w2s[...] = w2f[...].astype(low_type)
         pl.semaphore_wait(barrier, expected)
 
         back = Scatter(back_send, back_recv, me.selfish)
@@ -1614,6 +1574,26 @@
         loads[0].wait()
         for g in range(GROUPS):
             back.arrived(g, came.at[g])
+        w2_place = w2p.at[me.g, me.y]
+        w2_first = [copies.push(w2s, w2_place, device) for device in swapped[1:]]
+        w2_swap = pltpu.make_async_remote_copy(
+            src_ref=w2s,
+            dst_ref=w2_place,
+            send_sem=swap_send2,
+            recv_sem=swap_recv2,
+            device_id=swapped[0],
+            device_id_type=MESH,
+        )
+        w2_stays = pltpu.make_async_copy(w2s, w2_place, swap_recv2)
+
+        @pl.when(me.crossing)
+        def _():
+            w2_swap.start()
+
+        @pl.when(jnp.logical_not(me.crossing))
+        def _():
+            w2_stays.start()
+
         for half in range(2):
             a0 = came[2 * half, :, :LANES]
             b0 = came[2 * half, :, LANES:].astype(wide)
@@ -1629,63 +1609,109 @@
         def vector(index):
             return vec_ref[index : index + 1, :]
 
-        attn = jnp.dot(mixed_tok[...], wm[...], preferred_element_type=wide) + vector(2)
-        norm1, inverse1 = normed(tok[...].astype(wide) + attn)
+        mix = jnp.dot(mixed_tok[...], wm[...], preferred_element_type=wide) + vector(2)
+        norm1, inverse1 = normed(tok[...].astype(wide) + mix)
         early = norm1 * vector(3) + vector(4)
-        norm_keep[...] = norm1
         mine = me.x * 2 + me.y
-        xs[mine] = early.astype(low_type)
-        early_go = [copies.push(xs.at[mine], xs.at[mine], me.at(x=x, y=y)) for x, y in square]
+        halves = [slice(0, hn), slice(hn, n)]
+
+        def send_rows(ref, h):
+            place = ref.at[h, mine]
+            return [copies.push(place, place, me.at(x=x, y=y)) for x, y in square]
+
+        def send_back(ref, landing, h):
+            return [
+                copies.push(ref.at[h, x * 2 + y], landing.at[h, mine], me.at(x=x, y=y))
+                for x, y in square
+            ]
+
+        def arrive(started):
+            for copy in started:
+                copy.wait_recv()
+
+        def received(landing, h):
+            return [landing[h, x * 2 + y] for x, y in square]
+
+        early_go = []
+        for h, half in enumerate(halves):
+            xs[h, mine] = early[half].astype(low_type)
+            early_go.append(send_rows(xs, h))
         loads[1].wait()
-        loads[2].wait()
-
-        def forward(place):
-            inner = jnp.dot(xs[place], w1[...], preferred_element_type=wide) + vector(8)
+
+        def outer_weight():
+            return w2p[...].reshape(quarter, depth)
+
+        branch_go = []
+        for h in range(2):
+            arrive(early_go[h])
+            inner = jnp.dot(
+                xs[h].reshape(4 * hn, depth), w1[...], preferred_element_type=wide
+            ) + vector(8)
             act, slope = gelu_and_slope(inner)
-            acts[place] = act.astype(low_type)
-            slopes[place] = slope
-            return jnp.dot(acts[place], w2[...], preferred_element_type=wide)
-
-        own = forward(mine)
-        branch_go = []
-        for copy, (x, y) in zip(early_go, square):
-            copy.wait_recv()
-            place = x * 2 + y
-            parts[place] = forward(place).astype(low_type)
-            branch_go.append(copies.push(parts.at[place], sums.at[mine], me.at(x=x, y=y)))
-        for copy in branch_go:
-            copy.wait_recv()
-        branch = total_of(own, *[sums[x * 2 + y] for x, y in square]) + vector(5)
-        norm2, inverse2 = normed(early + branch)
-        out[...] = (norm2 * vector(6) + vector(7)).astype(low_type)
-        cot_wide = cot[...].astype(wide)
-        final_grad = normed_grad(cot_wide * vector(6), norm2, inverse2)
-        bgs[mine] = final_grad.astype(low_type)
-        grad_go = [copies.push(bgs.at[mine], bgs.at[mine], me.at(x=x, y=y)) for x, y in square]
+            act = act.astype(low_type)
+            acts[h] = act.reshape(4, hn, quarter)
+            slopes[h] = slope
+            if h == 0:
+
+                @pl.when(me.crossing)
+                def _():
+                    w2_swap.wait_recv()
+                    w2_swap.wait_send()
+
+                @pl.when(jnp.logical_not(me.crossing))
+                def _():
+                    w2_stays.wait()
+
+                block = w2p.at[me.g, me.c]
+                w2_last = [copies.push(block, block, me.sibling())]
+                for copy, (_, source) in zip(w2_first, me.line()):
+                    copy.wait_recv()
+                    block = w2p.at[source, me.c]
+                    w2_last.append(copies.push(block, block, me.sibling()))
+                arrive(w2_last)
+            made = jnp.dot(act, outer_weight(), preferred_element_type=wide).reshape(4, hn, depth)
+            own1[h] = made
+            parts[h] = made.astype(low_type)
+            branch_go.append(send_back(parts, sums, h))
+
+        grad_go, final_grads, norm_sums, cot_sums = [], [], [], []
+        for h, half in enumerate(halves):
+            arrive(branch_go[h])
+            branch = total_of(own1[h, mine], *received(sums, h)) + vector(5)
+            norm2, inverse2 = normed(early[half] + branch)
+            out[half, :] = (norm2 * vector(6) + vector(7)).astype(low_type)
+            cot_wide = cot[half, :].astype(wide)
+            final_grad = normed_grad(cot_wide * vector(6), norm2, inverse2)
+            bgs[h, mine] = final_grad.astype(low_type)
+            grad_go.append(send_rows(bgs, h))
+            final_grads.append(final_grad)
+            norm_sums.append(down_sum(cot_wide * norm2))
+            cot_sums.append(down_sum(cot_wide))
         extra[...] = jnp.zeros_like(extra)
-        extra[3:4, :] = down_sum(bgs[mine].astype(wide))
-        extra[4:5, :] = down_sum(cot_wide * norm2)
-        extra[5:6, :] = down_sum(cot_wide)
-
-        def backward(place):
-            grad = lax.dot_general(bgs[place], w2[...], NEXT, preferred_element_type=wide)
-            igs[place] = (grad * slopes[place]).astype(low_type)
-            return lax.dot_general(igs[place], w1[...], NEXT, preferred_element_type=wide)
-
-        own = backward(mine)
+        extra[3:4, :] = down_sum(bgs[0, mine].astype(wide)) + down_sum(bgs[1, mine].astype(wide))
+        extra[4:5, :] = norm_sums[0] + norm_sums[1]
+        extra[5:6, :] = cot_sums[0] + cot_sums[1]
+
         token_go = []
-        for copy, (x, y) in zip(grad_go, square):
-            copy.wait_recv()
-            place = x * 2 + y
-            parts2[place] = backward(place).astype(low_type)
-            token_go.append(copies.push(parts2.at[place], sums2.at[mine], me.at(x=x, y=y)))
+        for h in range(2):
+            arrive(grad_go[h])
+            grad = lax.dot_general(
+                bgs[h].reshape(4 * hn, depth), outer_weight(), NEXT, preferred_element_type=wide
+            )
+            grad = (grad * slopes[h]).astype(low_type)
+            igs[h] = grad.reshape(4, hn, quarter)
+            made = lax.dot_general(grad, w1[...], NEXT, preferred_element_type=wide)
+            made = made.reshape(4, hn, depth)
+            own2[h] = made
+            parts2[h] = made.astype(low_type)
+            token_go.append(send_back(parts2, sums2, h))
 
         other = 1 - me.c
         grads = bgs[...].reshape(4 * n, depth)
         for half in range(2):
             span = slice(half * cut, (half + 1) * cut)
             made = lax.dot_general(
-                acts[:, :, span].reshape(4 * n, cut), grads, DOWN, preferred_element_type=wide
+                acts[:, :, :, span].reshape(4 * n, cut), grads, DOWN, preferred_element_type=wide
             )
             g2[2 * half : 2 * half + 2] = made.astype(low_type).reshape(2, 2, e, depth)
         w2_half = copies.push(g2.at[:, other], s2, me.sibling())
@@ -1695,7 +1721,7 @@
         for half in range(2):
             span = slice(half * cut, (half + 1) * cut)
             made = lax.dot_general(
-                xs[:, :, span].reshape(4 * n, cut), grads, DOWN, preferred_element_type=wide
+                xs[:, :, :, span].reshape(4 * n, cut), grads, DOWN, preferred_element_type=wide
             ).astype(low_type)
             for index in range(16):
                 place = (half, index // 8, index // 2 % GROUPS, index % 2)
@@ -1737,16 +1763,20 @@
             s1[x, g, y] = s1[x, g, y] + g1[x, me.c, g, y]
 
         loop(16, add1)
-        for copy in token_go:
-            copy.wait_recv()
-        early_grad = total_of(final_grad, own, *[sums2[x * 2 + y] for x, y in square])
-        norm1 = norm_keep[...]
-        extra[1:2, :] = down_sum(early_grad * norm1)
-        extra[2:3, :] = down_sum(early_grad)
-        hidden = normed_grad(early_grad * vector(3), norm1, inverse1)
-        hidden_out[...] = hidden
-        attn_grad = hidden.astype(low_type)
-        extra[0:1, :] = down_sum(attn_grad.astype(wide))
+        norm_sums, grad_sums, attn_sums = [], [], []
+        for h, half in enumerate(halves):
+            arrive(token_go[h])
+            early_grad = total_of(final_grads[h], own2[h, mine], *received(sums2, h))
+            norm_sums.append(down_sum(early_grad * norm1[half]))
+            grad_sums.append(down_sum(early_grad))
+            hidden = normed_grad(early_grad * vector(3), norm1[half], inverse1[half])
+            hidden_out[half, :] = hidden
+            attn[half, :] = hidden.astype(low_type)
+            attn_sums.append(down_sum(hidden.astype(low_type).astype(wide)))
+        extra[0:1, :] = attn_sums[0] + attn_sums[1]
+        extra[1:2, :] = norm_sums[0] + norm_sums[1]
+        extra[2:3, :] = grad_sums[0] + grad_sums[1]
+        attn_grad = attn[...]
         back_grad = lax.dot_general(attn_grad, wm[...], NEXT, preferred_element_type=wide)
         for half in range(2):
             base = half * 3 * LANES
@@ -1791,8 +1821,10 @@
 
     vmem = pltpu.VMEM
     dma = pltpu.SemaphoreType.DMA
-    tall = vmem((4, n, depth), low_type)
-    space = [vmem] * 3 + [pl.ANY] * 3 + [vmem]
+    tall = vmem((2, 4, hn, depth), low_type)
+    full = vmem((2, 4, hn, depth), wide)
+    high = vmem((2, 4, hn, quarter), low_type)
+    space = [vmem] * 3 + [pl.ANY] * 2 + [vmem] * 2
     return pl.pallas_call(
         body,
         name="middle_kernel",
@@ -1809,21 +1841,20 @@
             pl.BlockSpec(memory_space=item) for item in (vmem, vmem, pl.ANY, vmem, vmem, vmem)
         ],
         scratch_shapes=[
-            dma((40,)), dma((40,)), dma((8,)), dma((4,)), dma((4,)), dma((4,)), dma((4,)), dma, dma,
+            dma((48,)), dma((48,)), dma((8,)), dma((4,)), dma((4,)), dma((4,)), dma((4,)), dma, dma, dma, dma,
             vmem((depth, depth), low_type),
             vmem((depth, quarter), low_type),
-            vmem((quarter, depth), low_type),
+            vmem((GROUPS, 2, e, depth), low_type),
+            vmem((e, depth), low_type),
             vmem((GROUPS, n, PACK), low_type),
             vmem((n, depth), low_type),
-            tall,
-            vmem((4, n, quarter), low_type),
-            vmem((4, n, quarter), wide),
-            tall, tall, tall,
-            vmem((4, n, quarter), low_type),
-            tall, tall,
+            tall, high,
+            vmem((2, 4 * hn, quarter), wide),
+            tall, tall, tall, high, tall, tall,
             vmem((GROUPS, n, PACK), low_type),
             vmem((8, depth), wide),
-            vmem((n, depth), wide),
+            vmem((n, depth), low_type),
+            full, full,
             vmem((2, 2, GROUPS, 2, rows, quarter), low_type),
             vmem((GROUPS, 2, e, depth), low_type),
             vmem((GROUPS, e, depth), low_type),
@@ -1833,6 +1864,223 @@
             collective_id=12, has_side_effects=True, vmem_limit_bytes=VMEM_LIMIT
         ),
     )(mixed, tokens, cotangent, mix, inner, outer, vec)
+
+
+def tile_base(me, slot, n):
+    u, v = slot // 2, slot % 2
+    return ((u * 2 + me.c) * 2 * GROUPS + (v * 2 + me.p) * 2 + me.y) * n
+
+
+def ends_of(lengths_ref):
+    ends = [lengths_ref[0]]
+    for index in range(1, lengths_ref.shape[0]):
+        ends.append(ends[-1] + lengths_ref[index])
+    return ends
+
+
+def document_of(place, ends):
+    first, last = place * 0, place * 0 + ends[-1]
+    for end in ends[:-1]:
+        before = end <= place
+        first = jnp.where(before, end, first)
+    for end in reversed(ends[:-1]):
+        last = jnp.where(end <= place, last, end)
+    return first, last
+
+
+def blocks_of(base, ends, n, block):
+    low, _ = document_of(base, ends)
+    _, high = document_of(base + n - 1, ends)
+    return low // block, (high + block - 1) // block
+
+
+def near_forward(lengths, queries, keys, n, block):
+    total_rows = queries.shape[0]
+    tokens = keys.shape[0]
+    chunks = [slice(index * LANES, (index + 1) * LANES) for index in range(block // LANES)]
+
+    def body(lengths_ref, q_ref, kv_ref, out_ref, keep_ref, lse_ref, table):
+        me = Spot()
+        ends = ends_of(lengths_ref)
+        lane = lax.broadcasted_iota(jnp.int32, (n, LANES), 1)
+        upper = lane >= HEAD
+        column = lax.broadcasted_iota(jnp.int32, (n, LANES), 0)
+
+        def one(slot, unused):
+            rows = pl.ds(pl.multiple_of(slot * n, n), n)
+            base = tile_base(me, slot, n)
+            low, high = blocks_of(base, ends, n, block)
+            first, last = document_of(column + base, ends)
+            heads = [
+                q_ref[rows, h * LANES : (h + 1) * LANES] * jnp.asarray(0.125, low_type)
+                for h in range(LOCAL)
+            ]
+
+            def score(j, tops):
+                begin = pl.multiple_of(j * block, block)
+                same = []
+                for chunk in chunks:
+                    place = lane + (begin + chunk.start)
+                    same.append((place >= first) & (place < last))
+                result = []
+                for h in range(LOCAL):
+                    kv = kv_ref[pl.ds(begin, block), h * LANES : (h + 1) * LANES]
+                    scores = lax.dot_general(heads[h], kv, NEXT, preferred_element_type=wide)
+                    top = tops[h]
+                    for chunk, mask in zip(chunks, same):
+                        part = jnp.where(mask, scores[:, chunk], mask_fill)
+                        table[h, j, :, chunk] = part
+                        top = jnp.maximum(top, part)
+                    result.append(top)
+                return tuple(result)
+
+            tops = lax.fori_loop(
+                low, high, score, (jnp.full((n, LANES), lowest_start, wide),) * LOCAL
+            )
+            tops = [jnp.max(top, axis=1, keepdims=True) for top in tops]
+            spread = [jnp.broadcast_to(top, (n, LANES)) for top in tops]
+
+            def weigh(j, carry):
+                begin = pl.multiple_of(j * block, block)
+                result = []
+                for h in range(LOCAL):
+                    total, mixed = carry[h]
+                    kv = kv_ref[pl.ds(begin, block), h * LANES : (h + 1) * LANES]
+                    parts = []
+                    for chunk in chunks:
+                        part = jnp.exp(table[h, j, :, chunk] - spread[h])
+                        total = total + part
+                        parts.append(part.astype(low_type))
+                    powers = jnp.concatenate(parts, axis=1)
+                    mixed = mixed + jnp.dot(powers, kv, preferred_element_type=wide)
+                    result.append((total, mixed))
+                return tuple(result)
+
+            zero = jnp.zeros((n, LANES), wide)
+            done = lax.fori_loop(low, high, weigh, ((zero, zero),) * LOCAL)
+            totals = [jnp.sum(total, axis=1, keepdims=True) for total, _ in done]
+            mixes = [mixed / total for total, (_, mixed) in zip(totals, done)]
+            turned = [pltpu.roll(mixed, HEAD, 1) for mixed in mixes]
+            front = jnp.where(upper, mixes[1], turned[0])
+            back = jnp.where(upper, 0.0, turned[2])
+            both = jnp.concatenate([front, back], axis=1)
+            keep_ref[rows, :] = both
+            out_ref[rows, :] = both.astype(low_type)
+            logs = [top + jnp.log(total) for top, total in zip(tops, totals)]
+            logs = jnp.where(lane == 0, logs[0], jnp.where(lane == 1, logs[1], logs[2]))
+            lse_ref[slot] = jnp.transpose(logs)[:8]
+            return unused
+
+        lax.fori_loop(0, GROUPS, one, 0)
+
+    vmem = pl.BlockSpec(memory_space=pltpu.VMEM)
+    return pl.pallas_call(
+        body,
+        name="near_forward",
+        out_shape=(
+            jax.ShapeDtypeStruct((total_rows, PACK), low_type),
+            jax.ShapeDtypeStruct((total_rows, PACK), wide),
+            jax.ShapeDtypeStruct((GROUPS, 8, n), wide),
+        ),
+        in_specs=[pl.BlockSpec(memory_space=pltpu.SMEM)] + [vmem] * 2,
+        out_specs=(vmem,) * 3,
+        scratch_shapes=[pltpu.VMEM((LOCAL, tokens // block, n, block), wide)],
+        compiler_params=pltpu.CompilerParams(vmem_limit_bytes=VMEM_LIMIT),
+    )(lengths, queries, keys)
+
+
+def near_backward(lengths, queries, keys, grads, mixed, lse, n, block):
+    total_rows = queries.shape[0]
+    tokens = keys.shape[0]
+
+    def body(lengths_ref, q_ref, kv_ref, do_ref, mixed_ref, lse_ref, dq_ref, dkv_ref, sums):
+        me = Spot()
+        ends = ends_of(lengths_ref)
+        zeros = jnp.zeros((block, LANES), wide)
+        spans = [slice(h * LANES, (h + 1) * LANES) for h in range(LOCAL)]
+
+        def clear(j, unused):
+            for span in spans:
+                sums[pl.ds(pl.multiple_of(j * block, block), block), span] = zeros
+            return unused
+
+        lax.fori_loop(0, tokens // block, clear, 0)
+        lane = lax.broadcasted_iota(jnp.int32, (n, LANES), 1)
+        upper = lane >= HEAD
+        along = lax.broadcasted_iota(jnp.int32, (1, n), 1)
+        down = lax.broadcasted_iota(jnp.int32, (block, n), 0)
+
+        def upper_halves(ref, rows):
+            front = ref[rows, :LANES].astype(wide)
+            back = ref[rows, LANES:].astype(wide)
+            parts = (pltpu.roll(front, HEAD, 1), front, pltpu.roll(back, HEAD, 1))
+            return [jnp.where(upper, part, 0.0) for part in parts]
+
+        def one(slot, unused):
+            rows = pl.ds(pl.multiple_of(slot * n, n), n)
+            base = tile_base(me, slot, n)
+            low, high = blocks_of(base, ends, n, block)
+            first, last = document_of(along + base, ends)
+            outs, inputs = upper_halves(mixed_ref, rows), upper_halves(do_ref, rows)
+            logs, deltas, operands = [], [], []
+            for h, span in enumerate(spans):
+                q = q_ref[rows, span] * jnp.asarray(0.125, low_type)
+                operands.append(jnp.concatenate([q, inputs[h].astype(low_type)], axis=0))
+                deltas.append(down_sum(jnp.transpose(inputs[h] * outs[h])))
+                logs.append(lse_ref[slot, h : h + 1, :])
+
+            def step(j, totals):
+                begin = pl.multiple_of(j * block, block)
+                part = pl.ds(begin, block)
+                place = down + begin
+                same = (place >= first) & (place < last)
+                kvs = [kv_ref[part, span] for span in spans]
+                made = [
+                    lax.dot_general(kv, both, NEXT, preferred_element_type=wide)
+                    for kv, both in zip(kvs, operands)
+                ]
+                result = []
+                for h, span in enumerate(spans):
+                    probs = jnp.exp(jnp.where(same, made[h][:, :n], mask_fill) - logs[h])
+                    score_grad = (probs * (made[h][:, n:] - deltas[h])).astype(low_type)
+                    pairs = jnp.concatenate([score_grad, probs.astype(low_type)], axis=1)
+                    sums[part, span] += jnp.dot(
+                        pairs, operands[h], preferred_element_type=wide
+                    )
+                    result.append(
+                        totals[h]
+                        + lax.dot_general(score_grad, kvs[h], DOWN, preferred_element_type=wide)
+                    )
+                return tuple(result)
+
+            totals = lax.fori_loop(low, high, step, (jnp.zeros((n, LANES), wide),) * LOCAL)
+            for total, span in zip(totals, spans):
+                dq_ref[rows, span] = jnp.where(upper, 0.0, total * 0.125).astype(low_type)
+            return unused
+
+        lax.fori_loop(0, GROUPS, one, 0)
+
+        def store(j, unused):
+            part = pl.ds(pl.multiple_of(j * block, block), block)
+            for span in spans:
+                dkv_ref[part, span] = sums[part, span].astype(low_type)
+            return unused
+
+        lax.fori_loop(0, tokens // block, store, 0)
+
+    vmem = pl.BlockSpec(memory_space=pltpu.VMEM)
+    return pl.pallas_call(
+        body,
+        name="near_backward",
+        out_shape=(
+            jax.ShapeDtypeStruct((total_rows, WIDE), low_type),
+            jax.ShapeDtypeStruct((tokens, WIDE), low_type),
+        ),
+        in_specs=[pl.BlockSpec(memory_space=pltpu.SMEM)] + [vmem] * 5,
+        out_specs=(vmem,) * 2,
+        scratch_shapes=[pltpu.VMEM((tokens, WIDE), wide)],
+        compiler_params=pltpu.CompilerParams(vmem_limit_bytes=VMEM_LIMIT),
+    )(lengths, queries, keys, grads, mixed, lse)
 
 
 def on_device_general(
@@ -2103,59 +2351,23 @@
         )
     ]
     vectors.append(inner_bias.reshape(1, -1))
-    toks, queries, w_qkv, vec, kv_all, w1, w2, wm = first_kernel(
+    toks, queries, w_qkv, vec, kv_all, w1, wm = first_kernel(
         tokens, query_weight, key_weight, value_weight, vectors,
-        inner_weight, outer_weight, mix_weight,
+        inner_weight, mix_weight, e,
     )
     queries = queries.reshape(rows, WIDE)
     kv_all = kv_all.reshape(total_tokens, WIDE)
     w_qkv = w_qkv.reshape(depth, -1)
     w1 = w1.reshape(depth, quarter)
-    w2 = w2.reshape(quarter, depth)
     wm = wm.reshape(depth, depth)
-    tile, block = 128, 1024
-    count = doc_lengths.shape[0]
-    upto = jnp.arange(count)[None, :] <= jnp.arange(count)[:, None]
-    ends = jnp.sum(jnp.where(upto, doc_lengths[None, :], 0), axis=1)
-    slot = jnp.arange(GROUPS)
-    owners = ((slot // 2 * 2 + me.c) * cycle + (slot % 2 * 2 + me.p) * 2 + me.y) * n
-    places = (owners[:, None] + jnp.arange(n)[None, :]).reshape(rows)
-    before = ends[None, :] <= places[:, None]
-    first = jnp.max(jnp.where(before, ends[None, :], 0), axis=1).astype(jnp.int32)
-    last = jnp.min(jnp.where(before, total_tokens, ends[None, :]), axis=1).astype(jnp.int32)
-    tiles = rows // tile
-    bounds = jnp.stack(
-        [
-            first.reshape(tiles, tile)[:, 0] // block,
-            (last.reshape(tiles, tile)[:, -1] + block - 1) // block,
-        ],
-        axis=1,
-    )
-    mixed, mixed_wide, lse = attend_forward(
-        queries, kv_all, bounds, first[:, None], last[:, None], tile, block
-    )
+    mixed, mixed_wide, lse = near_forward(doc_lengths, queries, kv_all, n, 512)
     output, hidden_grad, grad_all, gradm, sum1, out2 = middle_kernel(
-        mixed.reshape(GROUPS, n, PACK), tokens, cotangent, wm, w1, w2, vec, s, e
+        mixed.reshape(GROUPS, n, PACK), tokens, cotangent, wm, w1, outer_weight, vec, s, e
     )
     grad_all = grad_all.reshape(rows, PACK)
-    delta = jnp.sum(
-        (grad_all.astype(wide) * mixed_wide)[:, : LOCAL * HEAD].reshape(rows, LOCAL, HEAD), axis=2
-    )
-
-    def as_stat(values):
-        return jnp.transpose(values.reshape(tiles, tile, LOCAL), (0, 2, 1))
-
-    def same_stat(values):
-        return jnp.broadcast_to(
-            values.astype(wide).reshape(tiles, 1, tile), (tiles, LOCAL, tile)
-        )
-
-    stats = jnp.stack(
-        [same_stat(first), same_stat(last), as_stat(lse[:, :LOCAL]), as_stat(delta)], axis=2
-    )
-    stats = jnp.pad(stats, ((0, 0), (0, 0), (0, 4), (0, 0)))
-    query_grad, dkv = attend_backward(queries, kv_all, grad_all, stats, bounds, tile, block)
-
+    query_grad, dkv = near_backward(
+        doc_lengths, queries, kv_all, grad_all, mixed_wide, lse, n, 512
+    )
     pieces, outq, outk, out1, outm = last_kernel(
         dkv.reshape(2, 2, 2, 2, 2, n, WIDE),
         query_grad.reshape(GROUPS, n, WIDE),

time: 250 us -> 224 us (0.90); the launches traced: 250 us -> 220 us
  Pallas kernels: 243 us -> 219 us
  other arithmetic: 3.43 us -> 0 us
    pallas_call x2, Pallas kernels: 35.6 us -> 25.7 us  [the longest x1 14.3 us: near_backward(): pl.pallas_call(body, name='near_backward', out_shape=(jax.ShapeDtypeStruc...]
    pallas_call x1, Pallas kernels: 65.4 us -> 57.3 us  [first_kernel(): pl.pallas_call(body, name='first_kernel', out_shape=(jax.ShapeDtypeStruct...]
    pallas_call x1, Pallas kernels: 76.1 us -> 72.6 us  [middle_kernel(): pl.pallas_call(body, name='middle_kernel', out_shape=(jax.ShapeDtypeStruc...]
    pallas_call x1, Pallas kernels: 63.1 us -> 60.4 us  [last_kernel(): pl.pallas_call(body, name='last_kernel', out_shape=(jax.ShapeDtypeStruct(...]
where the time goes in v4:
time: 224 us; the launch traced here: 220 us
  Pallas kernels  219 us (98%)
    pallas_call x1, Pallas kernels, middle_kernel(): pl.pallas_call(body, name='middle_kernel', out_shape=(jax.ShapeDtypeStruc...  72.6 us
    pallas_call x1, Pallas kernels, last_kernel(): pl.pallas_call(body, name='last_kernel', out_shape=(jax.ShapeDtypeStruct(...  60.4 us
    pallas_call x1, Pallas kernels, first_kernel(): pl.pallas_call(body, name='first_kernel', out_shape=(jax.ShapeDtypeStruct...  57.3 us
    pallas_call x1, Pallas kernels, near_backward(): pl.pallas_call(body, name='near_backward', out_shape=(jax.ShapeDtypeStruc...  14.3 us
    pallas_call x1, Pallas kernels, near_forward(): pl.pallas_call(body, name='near_forward', out_shape=(jax.ShapeDtypeStruct...  11.4 us

profile of v4, /device:TPU:0, one launch (start us, length us, event | category | flops | bytes accessed | tf_op | source)
XLA Modules:
  0.0 220.0 jit_solution(6824459192252678433)
XLA Ops:
  0.7 57.3 %first_kernel.1 = (bf16[4,128,768]{2,1,0:T(8,128)(2,1)}, bf16[4,128,384]{2,1,0:T(8,128)(2,1)}, bf16[4,4,2,24,896]{4,3,2,1,0:T(8,128)(2,1)}, f32[16,768]{1,0:T(8,...) custom-call(bf16[128,768]{1,0:T(8,128)(2,1)} %tok.1, ...), custom_call_target="tpu_custom_call" | custom-call | tf_op jit(solution)/shard_map/first_kernel/pallas_call | solution.py:1134
  58.0 11.4 %near_forward.1 = (bf16[512,256]{1,0:T(8,128)(2,1)}, f32[512,256]{1,0:T(8,128)}, f32[4,8,128]{2,1,0:T(8,128)}) custom-call(s32[16]{0:T(128)} %lengths_ref.3, bf16[512,384]{1,0:T(8,128)(2,1)} %bitcast.30, bf16[4096,384]{1,0:T(8,128)(2,1)} %bitcast.27), custom_call_target="tpu_custom_call" | custom-call | tf_op jit(solution)/shard_map/near_forward/pallas_call | solution.py:1977
  69.4 72.6 %middle_kernel.1 = (bf16[128,768]{1,0:T(8,128)(2,1)}, f32[128,768]{1,0:T(8,128)}, bf16[4,128,256]{2,1,0:T(8,128)(2,1)}, bf16[2,2,4,2,32,768]{5,4,3,2,1,0:T(8,128...) custom-call(bf16[4,128,256]{2,1,0:T(8,128)(2,1)} %bitcast.37, bf16[128,768]{1,0:T(8,128)(2,1)} %tok.1, ...), custom_call_target="tpu_custom_call" | custom-call | tf_op jit(solution)/shard_map/middle_kernel/pallas_call | solution.py:1828
  142.0 14.3 %near_backward.1 = (bf16[512,384]{1,0:T(8,128)(2,1)}, bf16[4096,384]{1,0:T(8,128)(2,1)}) custom-call(s32[16]{0:T(128)} %lengths_ref.3, bf16[512,384]{1,0:T(8,128)(2,1)} %bitcast.31, bf16[4096,384]{1,0:T(8,128)(2,1)} %bitcast.28, bf16[512,256]{1,0:T(8,128)(2,1)} %bitcast.36, f32[512,256]{1,0:T(8,128)} %get-tuple-element.65.mixed_ref, ...), custom_call_target="tpu_custom_call" | custom-call | tf_op jit(solution)/shard_map/near_backward/pallas_call | solution.py:2072
  156.3 60.4 %last_kernel.1 = (bf16[4,128,768]{2,1,0:T(8,128)(2,1)}, bf16[4,32,256]{2,1,0:T(8,128)(2,1)}, bf16[4,32,384]{2,1,0:T(8,128)(2,1)}, bf16[4,32,768]{2,1,0:T(8,128)(2,1)}, f32[32,768]{1,0:T(8,128)}) custom-call(bf16[2,2,2,2,2,128,384]{6,5,4,3,2,1,0:T(8,128)(2,1)} %bitcast.29, bf16[4,128,384]{2,1,0:T(8,128)(2,1)} %bitcast.35, ...), custom_call_target="tpu_custom_call" | custom-call | tf_op jit(solution)/shard_map/last_kernel/pallas_call | solution.py:1404
  216.7 0.0 copy-start
  216.7 2.6 %final_kernel.1 = (bf16[128,768]{1,0:T(8,128)(2,1)}, f32[24,768]{1,0:T(8,128)}, f32[1,24]{1,0:T(1,128)}, f32[24,768]{1,0:T(8,128)}, f32[24,768]{1,0:T(8,128)}, /...) custom-call(f32[128,768]{1,0:T(8,128)} %get-tuple-element.63.hid, ...), custom_call_target="tpu_custom_call" | custom-call | tf_op jit(solution)/shard_map/final_kernel/pallas_call | solution.py:1489
  219.3 0.0 copy-done
  219.3 0.7 copy.37
Async XLA Ops:
  216.7 2.6 %copy-start = (bf16[128,768]{1,0:T(8,128)(2,1)S(1)}, bf16[128,768]{1,0:T(8,128)(2,1)}, u32[]{:S(2)}) copy-start(bf16[128,768]{1,0:T(8,128)(2,1)} %get-tuple-element.112) | copy-start | bytes 589828

commit v5 on v4

--- a/solution.py
+++ b/solution.py
@@ -22,6 +22,7 @@
 wide = jnp.float32
 MESH = pl.DeviceIdType.MESH
 VMEM_LIMIT = 62 * 1024 * 1024
+NEAR_LIMIT = 30 * 1024 * 1024
 
 
 def layer_norm(hidden, gain, shift):
@@ -964,14 +965,21 @@
     count = len(vectors)
 
     def body(*refs):
-        tok, wq_ref, wk_ref, wv_ref, tab = refs[:5]
-        vecs = refs[5 : 5 + count]
-        w1f, wmf = refs[5 + count : 7 + count]
+        tok = refs[0]
+        arguments = refs[1 : 7 + count]
         (
             tok_out, q_out, wqkv_out, vec_out, kv_all, w1, wm,
             send, recv, local, tok_send, tok_recv,
             slab, toks, weights, kv_own, q_own, w1s, wms, vec, few,
+            loaded, *places,
         ) = refs[7 + count :]
+        wq_ref, wk_ref, wv_ref, tab = places[:4]
+        vecs = places[4 : 4 + count]
+        w1f, wmf = places[4 + count :]
+        loads = []
+        for index, (argument, place) in enumerate(zip(arguments, places)):
+            loads.append(pltpu.make_async_copy(argument, place, loaded.at[index]))
+            loads[-1].start()
         me = Spot()
         copies = Copies(send, recv, local)
         square = me.square()
@@ -984,6 +992,8 @@
             + [me.sibling()],
             [(jnp.logical_not(me.selfish), sources[0])],
         )
+        for copy in loads:
+            copy.wait()
         lane = lax.broadcasted_iota(jnp.int32, (s, LANES), 1)
         lower = lane < HEAD
         for head in range(HEADS):
@@ -1143,7 +1153,7 @@
             jax.ShapeDtypeStruct((2, 2, GROUPS, 2, s, quarter), low_type),
             jax.ShapeDtypeStruct((2, 2, GROUPS, 2, s, depth), low_type),
         ),
-        in_specs=[pl.BlockSpec(memory_space=vmem)] * (7 + count),
+        in_specs=[pl.BlockSpec(memory_space=pltpu.HBM)] * (7 + count),
         out_specs=(pl.BlockSpec(memory_space=pl.ANY),) * 7,
         scratch_shapes=[
             dma((total,)), dma((total,)), dma((12,)), dma((4,)), dma((4,)),
@@ -1156,11 +1166,13 @@
             vmem((s, depth), low_type),
             vmem((SMALL, 2 * WIDE), wide),
             vmem((s, LANES), wide),
+            dma((6 + count,)),
+            *[vmem(item.shape, item.dtype) for item in (wq, wk, wv, tables, *vectors, inner, mix)],
         ],
         compiler_params=pltpu.CompilerParams(
-            collective_id=10, has_side_effects=True, vmem_limit_bytes=VMEM_LIMIT
+            collective_id=10, has_side_effects=True, vmem_limit_bytes=NEAR_LIMIT
         ),
-    )(tokens, wq, wk, wv, tables, *vectors, inner, mix)
+    )(*[pltpu.with_memory_space_constraint(item, pltpu.HBM) for item in (tokens, wq, wk, wv, tables, *vectors, inner, mix)])
 
 
 def pass_back(ident, pieces):
@@ -1428,7 +1440,7 @@
             vmem((3, rows, depth), low_type),
         ],
         compiler_params=pltpu.CompilerParams(
-            collective_id=11, has_side_effects=True, vmem_limit_bytes=VMEM_LIMIT
+            collective_id=11, has_side_effects=True, vmem_limit_bytes=NEAR_LIMIT
         ),
     )(dkv, dq, tokens, weights, sum1, gradm)
 
@@ -1498,7 +1510,7 @@
         ),
         in_specs=[pl.BlockSpec(memory_space=vmem)] * 7,
         out_specs=(pl.BlockSpec(memory_space=vmem),) * 16,
-        compiler_params=pltpu.CompilerParams(vmem_limit_bytes=VMEM_LIMIT),
+        compiler_params=pltpu.CompilerParams(vmem_limit_bytes=NEAR_LIMIT),
     )(hidden, pieces, outq, outk, out1, out2, outm)
 
 
@@ -1861,7 +1873,7 @@
             vmem((4, e, depth), low_type),
         ],
         compiler_params=pltpu.CompilerParams(
-            collective_id=12, has_side_effects=True, vmem_limit_bytes=VMEM_LIMIT
+            collective_id=12, has_side_effects=True, vmem_limit_bytes=NEAR_LIMIT
         ),
     )(mixed, tokens, cotangent, mix, inner, outer, vec)
 
@@ -1985,7 +1997,7 @@
         in_specs=[pl.BlockSpec(memory_space=pltpu.SMEM)] + [vmem] * 2,
         out_specs=(vmem,) * 3,
         scratch_shapes=[pltpu.VMEM((LOCAL, tokens // block, n, block), wide)],
-        compiler_params=pltpu.CompilerParams(vmem_limit_bytes=VMEM_LIMIT),
+        compiler_params=pltpu.CompilerParams(vmem_limit_bytes=NEAR_LIMIT),
     )(lengths, queries, keys)
 
 
@@ -2079,7 +2091,7 @@
         in_specs=[pl.BlockSpec(memory_space=pltpu.SMEM)] + [vmem] * 5,
         out_specs=(vmem,) * 2,
         scratch_shapes=[pltpu.VMEM((tokens, WIDE), wide)],
-        compiler_params=pltpu.CompilerParams(vmem_limit_bytes=VMEM_LIMIT),
+        compiler_params=pltpu.CompilerParams(vmem_limit_bytes=NEAR_LIMIT),
     )(lengths, queries, keys, grads, mixed, lse)
 
 

time: 224 us -> 208 us (0.929); the launches traced: 220 us -> 210 us
  Pallas kernels: 219 us -> 208 us
    pallas_call x1, Pallas kernels: 60.4 us -> 57.4 us  [last_kernel(): pl.pallas_call(body, name='last_kernel', out_shape=(jax.ShapeDtypeStruct(...]
where the time goes in v5:
time: 208 us; the launch traced here: 210 us
  Pallas kernels  208 us (100%)
    pallas_call x1, Pallas kernels, middle_kernel(): pl.pallas_call(body, name='middle_kernel', out_shape=(jax.ShapeDtypeStruc...  71 us
    pallas_call x1, Pallas kernels, last_kernel(): pl.pallas_call(body, name='last_kernel', out_shape=(jax.ShapeDtypeStruct(...  57.4 us
    pallas_call x1, Pallas kernels, first_kernel(): pl.pallas_call(body, name='first_kernel', out_shape=(jax.ShapeDtypeStruct...  56.1 us
    pallas_call x1, Pallas kernels, near_backward(): pl.pallas_call(body, name='near_backward', out_shape=(jax.ShapeDtypeStruc...  12.3 us
    pallas_call x1, Pallas kernels, near_forward(): pl.pallas_call(body, name='near_forward', out_shape=(jax.ShapeDtypeStruct...  10.2 us

profile of v5, /device:TPU:0, one launch (start us, length us, event | category | flops | bytes accessed | tf_op | source)
XLA Modules:
  0.0 210.2 jit_solution(18060297814753157282)
XLA Ops:
  0.7 56.1 %first_kernel.1 = (bf16[4,128,768]{2,1,0:T(8,128)(2,1)S(1)}, bf16[4,128,384]{2,1,0:T(8,128)(2,1)S(1)}, bf16[4,4,2,24,896]{4,3,2,1,0:T(8,128)(2,1)S(1)}, f32[16,7...) custom-call(bf16[128,768]{1,0:T(8,128)(2,1)} %tok.1, ...), custom_call_target="tpu_custom_call" | custom-call | tf_op jit(solution)/shard_map/first_kernel/pallas_call | solution.py:1144
  56.8 0.0 copy-start.3
  56.8 0.6 copy-done.3
  57.4 0.0 copy-start
  57.4 0.0 copy-start.1
  57.4 0.0 copy-start.2
  57.4 10.2 %near_forward.1 = (bf16[512,256]{1,0:T(8,128)(2,1)S(1)}, f32[512,256]{1,0:T(8,128)S(1)}, f32[4,8,128]{2,1,0:T(8,128)S(1)}) custom-call(s32[16]{0:T(128)S(1)} %copy-done.3, bf16[512,384]{1,0:T(8,128)(2,1)S(1)} %bitcast.30, bf16[4096,384]{1,0:T(8,128)(2,1)S(1)} %bitcast.27), custom_call_target="tpu_custom_call" | custom-call | tf_op jit(solution)/shard_map/near_forward/pallas_call | solution.py:1989
  67.6 0.0 copy-done
  67.6 0.0 copy-done.1
  67.6 0.0 copy-done.2
  67.6 0.0 copy-start.4
  67.6 71.0 %middle_kernel.1 = (bf16[128,768]{1,0:T(8,128)(2,1)S(1)}, f32[128,768]{1,0:T(8,128)S(1)}, bf16[4,128,256]{2,1,0:T(8,128)(2,1)S(1)}, bf16[2,2,4,2,32,768]{5,4,3,2...) custom-call(bf16[4,128,256]{2,1,0:T(8,128)(2,1)S(1)} %bitcast.37, ...), custom_call_target="tpu_custom_call" | custom-call | tf_op jit(solution)/shard_map/middle_kernel/pallas_call | solution.py:1840
  138.7 0.0 copy-done.4
  138.7 12.3 %near_backward.1 = (bf16[512,384]{1,0:T(8,128)(2,1)S(1)}, bf16[4096,384]{1,0:T(8,128)(2,1)S(1)}) custom-call(s32[16]{0:T(128)S(1)} %copy-done.4, bf16[512,384]{1,0:T(8,128)(2,1)S(1)} %bitcast.31, bf16[4096,384]{1,0:T(8,128)(2,1)S(1)} %bitcast.28, bf16[512,256]{1,0:T(8,128)(2,1)S(1)} %bitcast.36, f32[512,256]{1,0:T(8,128)S(1)} %get-tuple-element.65.mixed_ref, ...), custom_call_target="tpu_custom_call" | custom-call | tf_op jit(solution)/shard_map/near_backward/pallas_call | solution.py:2084
  151.0 57.4 %last_kernel.1 = (bf16[4,128,768]{2,1,0:T(8,128)(2,1)S(1)}, bf16[4,32,256]{2,1,0:T(8,128)(2,1)S(1)}, bf16[4,32,384]{2,1,0:T(8,128)(2,1)S(1)}, bf16[4,32,768]{2,1,0:T(8,128)(2,1)S(1)}, f32[32,768]{1,0:T(8,128)S(1)}) custom-call(bf16[2,2,2,2,2,128,384]{6,5,4,3,2,1,0:T(8,128)(2,1)S(1)} %bitcast.29, bf16[4,128,384]{2,1,0:T(8,128)(2,1)S(1)} %bitcast.35, ...), custom_call_target="tpu_custom_call" | custom-call | tf_op jit(solution)/shard_map/last_kernel/pallas_call | solution.py:1416
  208.4 1.1 final_kernel.1
  209.5 0.7 copy.37
Async XLA Ops:
  56.8 0.7 copy-start.3
  57.4 10.2 %copy-start = (bf16[128,768]{1,0:T(8,128)(2,1)S(1)}, bf16[128,768]{1,0:T(8,128)(2,1)}, u32[]{:S(2)}) copy-start(bf16[128,768]{1,0:T(8,128)(2,1)} %tok.1) | copy-start | bytes 589828
  57.4 10.2 %copy-start.1 = (f32[96,768]{1,0:T(8,128)S(1)}, f32[96,768]{1,0:T(8,128)}, u32[]{:S(2)}) copy-start(f32[96,768]{1,0:T(8,128)} %w2f.1) | copy-start | bytes 884740
  57.4 10.2 %copy-start.2 = (bf16[128,768]{1,0:T(8,128)(2,1)S(1)}, bf16[128,768]{1,0:T(8,128)(2,1)}, u32[]{:S(2)}) copy-start(bf16[128,768]{1,0:T(8,128)(2,1)} %cot.1) | copy-start | bytes 589828
  67.6 71.1 %copy-start.4 = (s32[16]{0:T(128)S(1)}, s32[16]{0:T(128)}, u32[]{:S(2)}) copy-start(s32[16]{0:T(128)} %lengths_ref.3) | copy-start | bytes 196

commit v6 on v5

--- a/solution.py
+++ b/solution.py
@@ -23,6 +23,7 @@
 MESH = pl.DeviceIdType.MESH
 VMEM_LIMIT = 62 * 1024 * 1024
 NEAR_LIMIT = 30 * 1024 * 1024
+TURN_LIMIT = 48 * 1024 * 1024
 
 
 def layer_norm(hidden, gain, shift):
@@ -1221,238 +1222,15 @@
     )(pieces)
 
 
-def last_kernel(dkv, dq, tokens, weights, sum1, gradm):
-    n = dq.shape[1]
-    depth = tokens.shape[-1]
-    s = depth // 32
-    rows = s + 8
-    cut = depth // 2
-
-    def body(
-        dkv_ref, dq_ref, tok, w_ref, s1, gm, dx_out, outq, outk, out1, outm,
-        send, recv, local, dx_send, dx_recv,
-        kst, pk, grads, queries, dxs, gq, sq, pq, fq, gk, sk, pp, fk, p1, f1, sm, pm, fm, tm,
-    ):
-        me = Spot()
-        copies = Copies(send, recv, local)
-        square = me.square()
-        line = [to for to, _ in me.line()]
-        owners = me.owners()
-        readers = [device for _, device in me.readers()]
-        barrier, expected = announce(
-            [me.at(x=x, y=y) for x, y in square]
-            + [me.at(g=to) for to in line]
-            + readers[1:]
-            + [me.sibling()],
-            [(jnp.logical_not(me.selfish), readers[0])],
-        )
-        pl.semaphore_wait(barrier, expected)
-        other = 1 - me.c
-        k_half = []
-        for dv in range(2):
-            v = (me.half + dv) % 2
-            k_half += [
-                copies.push(dkv_ref.at[u, other, v], kst.at[u, v], me.sibling()) for u in range(2)
-            ]
-
-        wm_half = copies.push(gm.at[:, other], sm, me.sibling())
-        w1_push = [
-            copies.push(s1.at[:, to, :], p1.at[slot], me.at(g=to)) for slot, to in enumerate(line)
-        ]
-
-        lower = lax.broadcasted_iota(jnp.int32, (n, LANES), 1) < HEAD
-        for slot in range(GROUPS):
-            second = pltpu.roll(dq_ref[slot, :, LANES : 2 * LANES].astype(wide), HEAD, 1)
-            front = jnp.where(lower, dq_ref[slot, :, :LANES].astype(wide), second)
-            queries[slot, :, :LANES] = front.astype(low_type)
-            queries[slot, :, LANES:] = dq_ref[slot, :, 2 * LANES :]
-            grads[slot, :, WIDE:] = dq_ref[slot]
-
-        def weight_grad(values, target):
-            width = values.shape[-1]
-            bias = jnp.sum(values.astype(wide), axis=0, keepdims=True)
-            bias = jnp.broadcast_to(bias, (8, width)).astype(low_type)
-            for half in range(2):
-                made = lax.dot_general(
-                    tok[:, :, half * cut : (half + 1) * cut].reshape(GROUPS * n, cut),
-                    values,
-                    DOWN,
-                    preferred_element_type=wide,
-                ).astype(low_type)
-                for index in range(16):
-                    place = (half, index // 8, index // 2 % GROUPS, index % 2)
-                    target[(*place, slice(None, s))] = made[index * s : (index + 1) * s]
-                    target[(*place, slice(s, None))] = bias
-
-        def keys_on(dv):
-            v = (me.half + dv) % 2
-            for u in range(2):
-                k_half[2 * dv + u].wait_recv()
-            pushed = []
-            for du in range(2):
-                for slot, (x, y) in enumerate(square):
-                    u, p = (x + du) % 2, (x + me.c) % 2
-                    kst[u, v, p, y] = kst[u, v, p, y] + dkv_ref[u, me.c, v, p, y]
-                    pushed.append(
-                        copies.push(
-                            kst.at[u, v, p, y], pk.at[2 * dv + du, slot], me.at(x=x, y=y)
-                        )
-                    )
-            return pushed
-
-        k_push = keys_on(0)
-        weight_grad(queries[...].reshape(GROUPS * n, PACK), gq)
-        q_half = copies.push(gq.at[:, other], sq, me.sibling())
-        k_push += keys_on(1)
-
-        def at8(index):
-            return index // 8, index // 2 % GROUPS, index % 2
-
-        def pair_sum(total, mine):
-            def add(index):
-                x, g, y = at8(index)
-                total[x, g, y] = total[x, g, y] + mine[x, me.c, g, y]
-
-            loop(16, add)
-
-        def square_push(total, landing):
-            return [
-                copies.push(total.at[x, :, y], landing.at[slot], me.at(x=x, y=y))
-                for slot, (x, y) in enumerate(square)
-            ]
-
-        def square_sum(result, total, landed):
-            def add(g):
-                result[g] = total_of(
-                    total[me.x, g, me.y], landed[0, g], landed[1, g], landed[2, g]
-                ).astype(low_type)
-
-            loop(GROUPS, add)
-
-        q_half.wait_recv()
-        pair_sum(sq, gq)
-        q_push = square_push(sq, pq)
-
-        move = Scatter(dx_send, dx_recv, me.selfish)
-        for index, (slot, device) in enumerate(owners):
-            for copy in k_push[3 * index : 3 * index + 3]:
-                copy.wait_recv()
-            u, v = slot // 2, slot % 2
-            grads[slot, :, :WIDE] = total_of(
-                kst[u, v, me.p, me.y],
-                dkv_ref[u, me.c, v, me.p, me.y],
-                *[pk[index, peer] for peer in range(3)],
-            ).astype(low_type)
-            dxs[slot] = lax.dot_general(
-                grads[slot], w_ref[:, : 2 * WIDE], NEXT, preferred_element_type=wide
-            ).astype(low_type)
-            move.send_one(dxs.at[slot], dx_out.at[me.g], me.g, device)
-            if index == 1:
-                for copy in q_push:
-                    copy.wait_recv()
-                square_sum(fq, sq, pq)
-                arrivals = [
-                    copies.push(fq.at[to], outq.at[me.g], me.at(g=to)) for to in line
-                ]
-                kept = [copies.keep(fq.at[me.g], outq.at[me.g])]
-                for copy in w1_push:
-                    copy.wait_recv()
-
-                def addw(index):
-                    x, y = index // 2, index % 2
-                    f1[x, y] = total_of(
-                        s1[x, me.g, y], *[p1[peer, x, y] for peer in range(3)]
-                    ).astype(low_type)
-
-                loop(4, addw)
-                quarter = out1.at[me.x * 2 + me.y]
-                arrivals += [
-                    copies.push(f1.at[x, y], quarter, me.at(x=x, y=y)) for x, y in square
-                ]
-                kept.append(copies.keep(f1.at[me.x, me.y], quarter))
-        wm_half.wait_recv()
-        pair_sum(sm, gm)
-        wm_push = square_push(sm, pm)
-        weight_grad(grads[:, :, :WIDE].reshape(GROUPS * n, WIDE), gk)
-        half = copies.push(gk.at[:, other], sk, me.sibling())
-        half.wait_recv()
-        pair_sum(sk, gk)
-        push = square_push(sk, pp)
-        for copy in wm_push:
-            copy.wait_recv()
-        square_sum(fm, sm, pm)
-        wm_last = [
-            copies.push(fm.at[to], tm.at[peer], me.at(g=to)) for peer, to in enumerate(line)
-        ]
-        for copy in push:
-            copy.wait_recv()
-        square_sum(fk, sk, pp)
-        arrivals += [copies.push(fk.at[to], outk.at[me.g], me.at(g=to)) for to in line]
-        kept.append(copies.keep(fk.at[me.g], outk.at[me.g]))
-        for copy in wm_last:
-            copy.wait_recv()
-        outm[...] = total_of(fm[me.g], *[tm[peer] for peer in range(3)])
-        for copy in arrivals:
-            copy.wait_recv()
-        for g in range(GROUPS):
-            move.arrived(g, dx_out.at[g])
-        for copy in kept:
-            copy.wait()
-        move.finish()
-        copies.finish()
-
-    vmem = pltpu.VMEM
-    dma = pltpu.SemaphoreType.DMA
-    total = 64
-
-    def stages(width):
-        return [
-            vmem((2, 2, GROUPS, 2, rows, width), low_type),
-            vmem((2, GROUPS, 2, rows, width), low_type),
-            vmem((3, GROUPS, rows, width), low_type),
-            vmem((GROUPS, rows, width), low_type),
-        ]
-
-    return pl.pallas_call(
-        body,
-        name="last_kernel",
-        out_shape=(
-            jax.ShapeDtypeStruct((GROUPS, n, depth), low_type),
-            jax.ShapeDtypeStruct((GROUPS, rows, PACK), low_type),
-            jax.ShapeDtypeStruct((GROUPS, rows, WIDE), low_type),
-            jax.ShapeDtypeStruct((4, rows, depth), low_type),
-            jax.ShapeDtypeStruct((rows, depth), wide),
-        ),
-        in_specs=[pl.BlockSpec(memory_space=vmem)] * 6,
-        out_specs=[pl.BlockSpec(memory_space=pl.ANY)] * 4 + [pl.BlockSpec(memory_space=vmem)],
-        scratch_shapes=[
-            dma((total,)), dma((total,)), dma((4,)), dma((4,)), dma((4,)),
-            vmem((2, 2, 2, 2, n, WIDE), low_type),
-            vmem((4, 3, n, WIDE), low_type),
-            vmem((GROUPS, n, 2 * WIDE), low_type),
-            vmem((GROUPS, n, PACK), low_type),
-            vmem((GROUPS, n, depth), low_type),
-            *stages(PACK),
-            *stages(WIDE),
-            vmem((3, 2, 2, rows, depth), low_type),
-            vmem((2, 2, rows, depth), low_type),
-            *stages(depth)[1:],
-            vmem((3, rows, depth), low_type),
-        ],
-        compiler_params=pltpu.CompilerParams(
-            collective_id=11, has_side_effects=True, vmem_limit_bytes=NEAR_LIMIT
-        ),
-    )(dkv, dq, tokens, weights, sum1, gradm)
-
-
-def final_kernel(hidden, pieces, outq, outk, out1, out2, outm, s, e):
+def final_kernel(hidden, pieces, outqk, out1, out2, outm, s, e):
     n, depth = hidden.shape
     quarter = out1.shape[-1]
 
-    def body(hid, dx, q_in, k_in, i_in, o_in, m_in, xg, qw, qb, kw, vw, vb, mw, mb, eg, es, iw, ib, ow, ob, fg, fs):
+    def body(hid, dx, qk_in, i_in, o_in, m_in, xg, qw, qb, kw, vw, vb, mw, mb, eg, es, iw, ib, ow, ob, fg, fs):
         device = lax.axis_index("au") * lax.axis_size("row") + lax.axis_index("row")
         xg[...] = total_of(hid[...], dx[0], dx[1], dx[2], dx[3]).astype(low_type)
-        rows = q_in.shape[1]
+        rows = qk_in.shape[1]
+        q_in, k_in = qk_in.at[:, :, WIDE:], qk_in.at[:, :, :WIDE]
         lower = lax.broadcasted_iota(jnp.int32, (rows, LANES), 1) < HEAD
 
         def part(head):
@@ -1508,10 +1286,10 @@
             shape(s, 4 * quarter), shape(1, e), shape(e, depth),
             shape(1, s), shape(1, s), shape(1, s),
         ),
-        in_specs=[pl.BlockSpec(memory_space=vmem)] * 7,
+        in_specs=[pl.BlockSpec(memory_space=vmem)] * 6,
         out_specs=(pl.BlockSpec(memory_space=vmem),) * 16,
         compiler_params=pltpu.CompilerParams(vmem_limit_bytes=NEAR_LIMIT),
-    )(hidden, pieces, outq, outk, out1, out2, outm)
+    )(hidden, pieces, outqk, out1, out2, outm)
 
 
 def gelu_and_slope(value):
@@ -1552,10 +1330,10 @@
 
     def body(
         mixed_ref, tok, cot, wm_in, w1_in, w2f, vec_ref,
-        out, hidden_out, do_out, gm, s1, out2,
-        send, recv, local, back_send, back_recv, on_send, on_recv, swap_send, swap_recv,
+        out, hidden_out, do_out, sm, s1, s2,
+        send, recv, local, back_send, back_recv, on_send, on_recv,
         swap_send2, swap_recv2, wm, w1, w2p, w2s, came, mixed_tok, xs, acts, slopes, parts, sums, bgs, igs, parts2, sums2,
-        pieces, extra, attn, own1, own2, g1, g2, s2, p2,
+        pieces, extra, attn, own1, own2, g1, g2, gm,
     ):
         me = Spot()
         copies = Copies(send, recv, local)
@@ -1746,28 +1524,6 @@
             s2[g] = s2[g] + g2[g, me.c]
 
         loop(GROUPS, add2)
-        w2_push = [
-            copies.push(s2.at[to], p2.at[index + 1], swapped[index + 1])
-            for index, to in enumerate(line)
-        ]
-        exchanged = pltpu.make_async_remote_copy(
-            src_ref=s2.at[me.g],
-            dst_ref=p2.at[0],
-            send_sem=swap_send,
-            recv_sem=swap_recv,
-            device_id=swapped[0],
-            device_id_type=MESH,
-        )
-        stays = pltpu.make_async_copy(s2.at[me.g], p2.at[0], swap_recv)
-
-        @pl.when(me.crossing)
-        def _():
-            exchanged.start()
-
-        @pl.when(jnp.logical_not(me.crossing))
-        def _():
-            stays.start()
-
         w1_half.wait_recv()
 
         def add1(index):
@@ -1813,18 +1569,14 @@
                 place = (half, index // 8, index // 2 % GROUPS, index % 2)
                 gm[(*place, slice(None, s))] = made[index * s : (index + 1) * s]
                 gm[(*place, slice(s, None))] = extra[...].astype(low_type)
-        @pl.when(me.crossing)
-        def _():
-            exchanged.wait_recv()
-            exchanged.wait_send()
-
-        @pl.when(jnp.logical_not(me.crossing))
-        def _():
-            stays.wait()
-
-        for copy in w2_push:
-            copy.wait_recv()
-        out2[...] = total_of(*[p2[index] for index in range(4)])
+        wm_half = copies.push(gm.at[:, other], sm, me.sibling())
+        wm_half.wait_recv()
+
+        def addm(index):
+            x, g, y = index // 8, index // 2 % GROUPS, index % 2
+            sm[x, g, y] = sm[x, g, y] + gm[x, me.c, g, y]
+
+        loop(16, addm)
         for index in range(GROUPS):
             onward.arrived(index, do_out.at[index])
         back.finish()
@@ -1844,16 +1596,16 @@
             jax.ShapeDtypeStruct((n, depth), low_type),
             jax.ShapeDtypeStruct((n, depth), wide),
             jax.ShapeDtypeStruct((GROUPS, n, PACK), low_type),
-            jax.ShapeDtypeStruct((2, 2, GROUPS, 2, rows, depth), low_type),
+            jax.ShapeDtypeStruct((2, GROUPS, 2, rows, depth), low_type),
             jax.ShapeDtypeStruct((2, GROUPS, 2, rows, quarter), low_type),
-            jax.ShapeDtypeStruct((e, depth), wide),
+            jax.ShapeDtypeStruct((GROUPS, e, depth), low_type),
         ),
         in_specs=[pl.BlockSpec(memory_space=item) for item in space],
         out_specs=[
             pl.BlockSpec(memory_space=item) for item in (vmem, vmem, pl.ANY, vmem, vmem, vmem)
         ],
         scratch_shapes=[
-            dma((48,)), dma((48,)), dma((8,)), dma((4,)), dma((4,)), dma((4,)), dma((4,)), dma, dma, dma, dma,
+            dma((48,)), dma((48,)), dma((8,)), dma((4,)), dma((4,)), dma((4,)), dma((4,)), dma, dma,
             vmem((depth, depth), low_type),
             vmem((depth, quarter), low_type),
             vmem((GROUPS, 2, e, depth), low_type),
@@ -1869,8 +1621,7 @@
             full, full,
             vmem((2, 2, GROUPS, 2, rows, quarter), low_type),
             vmem((GROUPS, 2, e, depth), low_type),
-            vmem((GROUPS, e, depth), low_type),
-            vmem((4, e, depth), low_type),
+            vmem((2, 2, GROUPS, 2, rows, depth), low_type),
         ],
         compiler_params=pltpu.CompilerParams(
             collective_id=12, has_side_effects=True, vmem_limit_bytes=NEAR_LIMIT
@@ -2001,98 +1752,348 @@
     )(lengths, queries, keys)
 
 
-def near_backward(lengths, queries, keys, grads, mixed, lse, n, block):
-    total_rows = queries.shape[0]
-    tokens = keys.shape[0]
-
-    def body(lengths_ref, q_ref, kv_ref, do_ref, mixed_ref, lse_ref, dq_ref, dkv_ref, sums):
+def turn_kernel(lengths, queries, keys, grads_in, mixed, lse, tokens, weights, sum1, sum2, summ):
+    n = tokens.shape[1]
+    depth = tokens.shape[-1]
+    s = depth // 32
+    rows = s + 8
+    cut = depth // 2
+    tall = sum2.shape[1]
+    block = GROUPS * n
+    width = WIDE + PACK
+    spans = [slice(h * LANES, (h + 1) * LANES) for h in range(LOCAL)]
+
+    def body(
+        lengths_ref, q_ref, kv_ref, do_ref, mixed_ref, lse_ref, tok, w_ref, s1, s2, sm,
+        dx_out, outqk, out1, out2, outm,
+        send, recv, local, dx_send, dx_recv, swap_send, swap_recv, ks, kr, ps, pr,
+        both, kbuf, kin, pk, dqs, grads, narrow, dxs, gk, sk, pp, fk, p1, f1, pm, fm, tm, p2,
+    ):
         me = Spot()
+        copies = Copies(send, recv, local)
+        square = me.square()
+        line = [to for to, _ in me.line()]
+        readers = [device for _, device in me.readers()]
+        swapped = [me.at(g=to, c=me.y, y=me.c) for to in [me.g] + line]
+        barrier, expected = announce(
+            [me.at(x=x, y=y) for x, y in square]
+            + [me.at(g=to) for to in line]
+            + readers[1:]
+            + swapped[1:]
+            + [me.sibling()],
+            [(jnp.logical_not(me.selfish), readers[0]), (me.crossing, swapped[0])],
+        )
         ends = ends_of(lengths_ref)
-        zeros = jnp.zeros((block, LANES), wide)
-        spans = [slice(h * LANES, (h + 1) * LANES) for h in range(LOCAL)]
-
-        def clear(j, unused):
-            for span in spans:
-                sums[pl.ds(pl.multiple_of(j * block, block), block), span] = zeros
-            return unused
-
-        lax.fori_loop(0, tokens // block, clear, 0)
         lane = lax.broadcasted_iota(jnp.int32, (n, LANES), 1)
         upper = lane >= HEAD
         along = lax.broadcasted_iota(jnp.int32, (1, n), 1)
         down = lax.broadcasted_iota(jnp.int32, (block, n), 0)
 
-        def upper_halves(ref, rows):
-            front = ref[rows, :LANES].astype(wide)
-            back = ref[rows, LANES:].astype(wide)
+        def upper_halves(ref, part):
+            front = ref[part, :LANES].astype(wide)
+            back = ref[part, LANES:].astype(wide)
             parts = (pltpu.roll(front, HEAD, 1), front, pltpu.roll(back, HEAD, 1))
-            return [jnp.where(upper, part, 0.0) for part in parts]
-
-        def one(slot, unused):
-            rows = pl.ds(pl.multiple_of(slot * n, n), n)
-            base = tile_base(me, slot, n)
-            low, high = blocks_of(base, ends, n, block)
-            first, last = document_of(along + base, ends)
-            outs, inputs = upper_halves(mixed_ref, rows), upper_halves(do_ref, rows)
-            logs, deltas, operands = [], [], []
+            return [jnp.where(upper, item, 0.0) for item in parts]
+
+        firsts, lasts, logs, deltas = [], [], [], []
+        for slot in range(GROUPS):
+            part = slice(slot * n, (slot + 1) * n)
+            first, last = document_of(along + tile_base(me, slot, n), ends)
+            firsts.append(first)
+            lasts.append(last)
+            outs, inputs = upper_halves(mixed_ref, part), upper_halves(do_ref, part)
             for h, span in enumerate(spans):
-                q = q_ref[rows, span] * jnp.asarray(0.125, low_type)
-                operands.append(jnp.concatenate([q, inputs[h].astype(low_type)], axis=0))
-                deltas.append(down_sum(jnp.transpose(inputs[h] * outs[h])))
-                logs.append(lse_ref[slot, h : h + 1, :])
-
-            def step(j, totals):
-                begin = pl.multiple_of(j * block, block)
-                part = pl.ds(begin, block)
-                place = down + begin
-                same = (place >= first) & (place < last)
-                kvs = [kv_ref[part, span] for span in spans]
-                made = [
-                    lax.dot_general(kv, both, NEXT, preferred_element_type=wide)
-                    for kv, both in zip(kvs, operands)
-                ]
-                result = []
-                for h, span in enumerate(spans):
-                    probs = jnp.exp(jnp.where(same, made[h][:, :n], mask_fill) - logs[h])
-                    score_grad = (probs * (made[h][:, n:] - deltas[h])).astype(low_type)
-                    pairs = jnp.concatenate([score_grad, probs.astype(low_type)], axis=1)
-                    sums[part, span] += jnp.dot(
-                        pairs, operands[h], preferred_element_type=wide
+                base = slot * 2 * n
+                both[h, base : base + n] = q_ref[part, span] * jnp.asarray(0.125, low_type)
+                both[h, base + n : base + 2 * n] = inputs[h].astype(low_type)
+            deltas.append([down_sum(jnp.transpose(i * o)) for i, o in zip(inputs, outs)])
+            logs.append([lse_ref[slot, h : h + 1, :] for h in range(LOCAL)])
+        dqs[...] = jnp.zeros_like(dqs)
+        pl.semaphore_wait(barrier, expected)
+
+        wm_push = [
+            copies.push(sm.at[x, :, y], pm.at[peer], me.at(x=x, y=y))
+            for peer, (x, y) in enumerate(square)
+        ]
+        w1_push = [
+            copies.push(s1.at[:, to, :], p1.at[slot], me.at(g=to)) for slot, to in enumerate(line)
+        ]
+        w2_push = [
+            copies.push(s2.at[to], p2.at[index + 1], swapped[index + 1])
+            for index, to in enumerate(line)
+        ]
+        exchanged = pltpu.make_async_remote_copy(
+            src_ref=s2.at[me.g],
+            dst_ref=p2.at[0],
+            send_sem=swap_send,
+            recv_sem=swap_recv,
+            device_id=swapped[0],
+            device_id_type=MESH,
+        )
+        stays = pltpu.make_async_copy(s2.at[me.g], p2.at[0], swap_recv)
+
+        @pl.when(me.crossing)
+        def _():
+            exchanged.start()
+
+        @pl.when(jnp.logical_not(me.crossing))
+        def _():
+            stays.start()
+
+        other = 1 - me.c
+
+        def attend(u, c, v, target):
+            begin = pl.multiple_of(((u * 2 + c) * 2 + v) * block, block)
+            place = down + begin
+            same = [(place >= first) & (place < last) for first, last in zip(firsts, lasts)]
+            for h, span in enumerate(spans):
+                kv = kv_ref[pl.ds(begin, block), span]
+                made = lax.dot_general(kv, both[h], NEXT, preferred_element_type=wide)
+                pairs = []
+                for slot in range(GROUPS):
+                    base = slot * 2 * n
+                    scores = jnp.where(same[slot], made[:, base : base + n], mask_fill)
+                    probs = jnp.exp(scores - logs[slot][h])
+                    dots = made[:, base + n : base + 2 * n]
+                    score_grad = (probs * (dots - deltas[slot][h])).astype(low_type)
+                    pairs += [score_grad, probs.astype(low_type)]
+                    dqs[slot, :, span] += lax.dot_general(
+                        score_grad, kv, DOWN, preferred_element_type=wide
                     )
-                    result.append(
-                        totals[h]
-                        + lax.dot_general(score_grad, kvs[h], DOWN, preferred_element_type=wide)
-                    )
-                return tuple(result)
-
-            totals = lax.fori_loop(low, high, step, (jnp.zeros((n, LANES), wide),) * LOCAL)
-            for total, span in zip(totals, spans):
-                dq_ref[rows, span] = jnp.where(upper, 0.0, total * 0.125).astype(low_type)
-            return unused
-
-        lax.fori_loop(0, GROUPS, one, 0)
-
-        def store(j, unused):
-            part = pl.ds(pl.multiple_of(j * block, block), block)
-            for span in spans:
-                dkv_ref[part, span] = sums[part, span].astype(low_type)
-            return unused
-
-        lax.fori_loop(0, tokens // block, store, 0)
-
-    vmem = pl.BlockSpec(memory_space=pltpu.VMEM)
+                made = jnp.dot(
+                    jnp.concatenate(pairs, axis=1), both[h], preferred_element_type=wide
+                )
+                target[:, :, :, span] = made.astype(low_type).reshape(2, 2, n, LANES)
+
+        def to_sibling(turn):
+            return pltpu.make_async_remote_copy(
+                src_ref=kbuf.at[0, turn],
+                dst_ref=kin.at[turn],
+                send_sem=ks.at[turn],
+                recv_sem=kr.at[turn],
+                device_id=me.sibling(),
+                device_id_type=MESH,
+            )
+
+        def to_peer(turn, peer):
+            x, y = square[peer]
+            return pltpu.make_async_remote_copy(
+                src_ref=kbuf.at[1, turn, (x + me.c) % 2, y],
+                dst_ref=pk.at[turn, peer],
+                send_sem=ps.at[turn * 3 + peer],
+                recv_sem=pr.at[turn * 3 + peer],
+                device_id=me.at(x=x, y=y),
+                device_id_type=MESH,
+            )
+
+        def key_turn(turn):
+            u, v = turn % 2, (me.half + turn // 2) % 2
+
+            def of_core(index):
+                attend(u, jnp.where(index == 0, other, me.c), v, kbuf.at[index, turn])
+
+                @pl.when(index == 0)
+                def _():
+                    to_sibling(turn).start()
+
+            loop(2, of_core)
+            to_sibling(turn).wait_recv()
+            for p in range(2):
+                for y in range(2):
+                    kbuf[1, turn, p, y] = kbuf[1, turn, p, y] + kin[turn, p, y]
+            for peer in range(3):
+                to_peer(turn, peer).start()
+
+        loop(4, key_turn)
+
+        def square_push(total, landing):
+            return [
+                copies.push(total.at[x, :, y], landing.at[slot], me.at(x=x, y=y))
+                for slot, (x, y) in enumerate(square)
+            ]
+
+        def square_sum(result, total, landed):
+            def add(g):
+                result[g] = total_of(
+                    total[me.x, g, me.y], landed[0, g], landed[1, g], landed[2, g]
+                ).astype(low_type)
+
+            loop(GROUPS, add)
+
+        moves = []
+        for turn in range(4):
+            u, dv = turn % 2, turn // 2
+            v = (me.half + dv) % 2
+            slot = u * 2 + v
+            wides = [dqs[slot, :, span] * 0.125 for span in spans]
+            for h, span in enumerate(spans):
+                grads[slot, :, WIDE + span.start : WIDE + span.stop] = jnp.where(
+                    upper, 0.0, wides[h]
+                ).astype(low_type)
+            narrow[slot, :, WIDE : WIDE + LANES] = jnp.where(
+                upper, pltpu.roll(wides[1], HEAD, 1), wides[0]
+            ).astype(low_type)
+            narrow[slot, :, WIDE + LANES :] = jnp.where(upper, 0.0, wides[2]).astype(low_type)
+            for peer in range(3):
+                to_peer(turn, peer).wait_recv()
+            here = total_of(
+                kbuf[1, turn, me.p, me.y], *[pk[turn, peer] for peer in range(3)]
+            ).astype(low_type)
+            grads[slot, :, :WIDE] = here
+            narrow[slot, :, :WIDE] = here
+            dxs[slot] = lax.dot_general(
+                grads[slot], w_ref[:, : 2 * WIDE], NEXT, preferred_element_type=wide
+            ).astype(low_type)
+            copy = pltpu.make_async_remote_copy(
+                src_ref=dxs.at[slot],
+                dst_ref=dx_out.at[me.g],
+                send_sem=dx_send.at[turn],
+                recv_sem=dx_recv.at[me.g],
+                device_id=me.at(x=u, g=2 * v + me.p),
+                device_id_type=MESH,
+            )
+            if dv:
+                copy.start()
+                moves.append((copy, None))
+                continue
+            stay = pltpu.make_async_copy(dxs.at[slot], dx_out.at[me.g], dx_recv.at[me.g])
+            at_home = me.selfish & (me.x == u)
+            away = jnp.logical_not(at_home)
+            moves.append((copy, away))
+
+            @pl.when(at_home)
+            def _(stay=stay):
+                stay.start()
+
+            @pl.when(away)
+            def _(copy=copy):
+                copy.start()
+
+        values = narrow[...].reshape(GROUPS * n, width)
+        bias = jnp.broadcast_to(down_sum(values.astype(wide)), (8, width)).astype(low_type)
+        for half in range(2):
+            made = lax.dot_general(
+                tok[:, :, half * cut : (half + 1) * cut].reshape(GROUPS * n, cut),
+                values,
+                DOWN,
+                preferred_element_type=wide,
+            ).astype(low_type)
+            for index in range(16):
+                place = (half, index // 8, index // 2 % GROUPS, index % 2)
+                gk[(*place, slice(None, s))] = made[index * s : (index + 1) * s]
+                gk[(*place, slice(s, None))] = bias
+        g_half = copies.push(gk.at[:, other], sk, me.sibling())
+
+        for copy in wm_push:
+            copy.wait_recv()
+        square_sum(fm, sm, pm)
+        wm_last = [
+            copies.push(fm.at[to], tm.at[peer], me.at(g=to)) for peer, to in enumerate(line)
+        ]
+        for copy in w1_push:
+            copy.wait_recv()
+
+        def addw(index):
+            x, y = index // 2, index % 2
+            f1[x, y] = total_of(s1[x, me.g, y], *[p1[peer, x, y] for peer in range(3)]).astype(
+                low_type
+            )
+
+        loop(4, addw)
+        quarter = out1.at[me.x * 2 + me.y]
+        g_half.wait_recv()
+
+        def pair_sum(index):
+            x, g, y = index // 8, index // 2 % GROUPS, index % 2
+            sk[x, g, y] = sk[x, g, y] + gk[x, me.c, g, y]
+
+        loop(16, pair_sum)
+        push = square_push(sk, pp)
+        arrivals = [copies.push(f1.at[x, y], quarter, me.at(x=x, y=y)) for x, y in square]
+        kept = [copies.keep(f1.at[me.x, me.y], quarter)]
+
+        @pl.when(me.crossing)
+        def _():
+            exchanged.wait_recv()
+            exchanged.wait_send()
+
+        @pl.when(jnp.logical_not(me.crossing))
+        def _():
+            stays.wait()
+
+        for copy in w2_push:
+            copy.wait_recv()
+        out2[...] = total_of(*[p2[index] for index in range(4)])
+        for copy in push:
+            copy.wait_recv()
+        square_sum(fk, sk, pp)
+        arrivals += [copies.push(fk.at[to], outqk.at[me.g], me.at(g=to)) for to in line]
+        kept.append(copies.keep(fk.at[me.g], outqk.at[me.g]))
+        for copy in wm_last:
+            copy.wait_recv()
+        outm[...] = total_of(fm[me.g], *[tm[peer] for peer in range(3)])
+        for copy in arrivals:
+            copy.wait_recv()
+        for g in range(GROUPS):
+            pltpu.make_async_copy(dx_out.at[g], dx_out.at[g], dx_recv.at[g]).wait()
+        for copy in kept:
+            copy.wait()
+        for copy, away in moves:
+            if away is None:
+                copy.wait_send()
+                continue
+
+            @pl.when(away)
+            def _(copy=copy):
+                copy.wait_send()
+
+        for turn in range(4):
+            to_sibling(turn).wait_send()
+            for peer in range(3):
+                to_peer(turn, peer).wait_send()
+        copies.finish()
+
+    vmem = pltpu.VMEM
+    dma = pltpu.SemaphoreType.DMA
+    total = 40
     return pl.pallas_call(
         body,
-        name="near_backward",
+        name="turn_kernel",
         out_shape=(
-            jax.ShapeDtypeStruct((total_rows, WIDE), low_type),
-            jax.ShapeDtypeStruct((tokens, WIDE), low_type),
+            jax.ShapeDtypeStruct((GROUPS, n, depth), low_type),
+            jax.ShapeDtypeStruct((GROUPS, rows, width), low_type),
+            jax.ShapeDtypeStruct((4, rows, depth), low_type),
+            jax.ShapeDtypeStruct((tall, depth), wide),
+            jax.ShapeDtypeStruct((rows, depth), wide),
         ),
-        in_specs=[pl.BlockSpec(memory_space=pltpu.SMEM)] + [vmem] * 5,
-        out_specs=(vmem,) * 2,
-        scratch_shapes=[pltpu.VMEM((tokens, WIDE), wide)],
-        compiler_params=pltpu.CompilerParams(vmem_limit_bytes=NEAR_LIMIT),
-    )(lengths, queries, keys, grads, mixed, lse)
+        in_specs=[pl.BlockSpec(memory_space=pltpu.SMEM)] + [pl.BlockSpec(memory_space=vmem)] * 10,
+        out_specs=[pl.BlockSpec(memory_space=pl.ANY)] * 3 + [pl.BlockSpec(memory_space=vmem)] * 2,
+        scratch_shapes=[
+            dma((total,)), dma((total,)), dma((4,)), dma((4,)), dma((4,)), dma, dma,
+            dma((4,)), dma((4,)), dma((12,)), dma((12,)),
+            vmem((LOCAL, 2 * block, LANES), low_type),
+            vmem((2, 4, 2, 2, n, WIDE), low_type),
+            vmem((4, 2, 2, n, WIDE), low_type),
+            vmem((4, 3, n, WIDE), low_type),
+            vmem((GROUPS, n, WIDE), wide),
+            vmem((GROUPS, n, 2 * WIDE), low_type),
+            vmem((GROUPS, n, width), low_type),
+            vmem((GROUPS, n, depth), low_type),
+            vmem((2, 2, GROUPS, 2, rows, width), low_type),
+            vmem((2, GROUPS, 2, rows, width), low_type),
+            vmem((3, GROUPS, rows, width), low_type),
+            vmem((GROUPS, rows, width), low_type),
+            vmem((3, 2, 2, rows, depth), low_type),
+            vmem((2, 2, rows, depth), low_type),
+            vmem((3, GROUPS, rows, depth), low_type),
+            vmem((GROUPS, rows, depth), low_type),
+            vmem((3, rows, depth), low_type),
+            vmem((4, tall, depth), low_type),
+        ],
+        compiler_params=pltpu.CompilerParams(
+            collective_id=11, has_side_effects=True, vmem_limit_bytes=TURN_LIMIT
+        ),
+    )(lengths, queries, keys, grads_in, mixed, lse, tokens, weights, sum1, sum2, summ)
 
 
 def on_device_general(
@@ -2373,22 +2374,14 @@
     w1 = w1.reshape(depth, quarter)
     wm = wm.reshape(depth, depth)
     mixed, mixed_wide, lse = near_forward(doc_lengths, queries, kv_all, n, 512)
-    output, hidden_grad, grad_all, gradm, sum1, out2 = middle_kernel(
+    output, hidden_grad, grad_all, summ, sum1, sum2 = middle_kernel(
         mixed.reshape(GROUPS, n, PACK), tokens, cotangent, wm, w1, outer_weight, vec, s, e
     )
     grad_all = grad_all.reshape(rows, PACK)
-    query_grad, dkv = near_backward(
-        doc_lengths, queries, kv_all, grad_all, mixed_wide, lse, n, 512
+    pieces, outqk, out1, out2, outm = turn_kernel(
+        doc_lengths, queries, kv_all, grad_all, mixed_wide, lse, toks, w_qkv, sum1, sum2, summ
     )
-    pieces, outq, outk, out1, outm = last_kernel(
-        dkv.reshape(2, 2, 2, 2, 2, n, WIDE),
-        query_grad.reshape(GROUPS, n, WIDE),
-        toks,
-        w_qkv,
-        sum1,
-        gradm,
-    )
-    results = final_kernel(hidden_grad, pieces, outq, outk, out1, out2, outm, s, e)
+    results = final_kernel(hidden_grad, pieces, outqk, out1, out2, outm, s, e)
     return (output,) + tuple(
         result.reshape(-1) if result.shape[0] == 1 else result for result in results
     )

time: 208 us -> 196 us (0.942); the launches traced: 210 us -> 195 us
  Pallas kernels: 208 us -> 192 us
    pallas_call x1, Pallas kernels: 71 us -> 61.1 us  [middle_kernel(): pl.pallas_call(body, name='middle_kernel', out_shape=(jax.ShapeDtypeStruc...]
    pallas_call x2 -> x1, Pallas kernels: 69.7 us -> 64.6 us  [turn_kernel(): pl.pallas_call(body, name='turn_kernel', out_shape=(jax.ShapeDtypeStruct(...]
where the time goes in v6:
time: 196 us; the launch traced here: 195 us
  Pallas kernels  192 us (98%)
  local copies, waits for them, and re-layouts  2.42 us (1%)
    pallas_call x1, Pallas kernels, turn_kernel(): pl.pallas_call(body, name='turn_kernel', out_shape=(jax.ShapeDtypeStruct(...  64.6 us
    pallas_call x1, Pallas kernels, middle_kernel(): pl.pallas_call(body, name='middle_kernel', out_shape=(jax.ShapeDtypeStruc...  61.1 us
    pallas_call x1, Pallas kernels, first_kernel(): pl.pallas_call(body, name='first_kernel', out_shape=(jax.ShapeDtypeStruct...  56.1 us
    pallas_call x1, Pallas kernels, near_forward(): pl.pallas_call(body, name='near_forward', out_shape=(jax.ShapeDtypeStruct...  9.11 us

profile of v6, /device:TPU:0, one launch (start us, length us, event | category | flops | bytes accessed | tf_op | source)
XLA Modules:
  0.0 195.1 jit_solution(9844115166533771656)
XLA Ops:
  0.7 56.1 %first_kernel.1 = (bf16[4,128,768]{2,1,0:T(8,128)(2,1)S(1)}, bf16[4,128,384]{2,1,0:T(8,128)(2,1)S(1)}, bf16[4,4,2,24,896]{4,3,2,1,0:T(8,128)(2,1)S(1)}, f32[16,7...) custom-call(bf16[128,768]{1,0:T(8,128)(2,1)} %tok.1, ...), custom_call_target="tpu_custom_call" | custom-call | tf_op jit(solution)/shard_map/first_kernel/pallas_call | solution.py:1145
  56.8 0.0 copy-start.1
  56.8 1.1 copy-done.1
  57.8 0.0 copy-start
  57.8 0.0 copy-start.5
  57.8 0.7 copy-done.5
  58.5 0.0 copy-start.2
  58.5 0.0 copy-start.3
  58.5 0.0 copy-start.4
  58.5 9.1 %near_forward.1 = (bf16[512,256]{1,0:T(8,128)(2,1)S(1)}, f32[512,256]{1,0:T(8,128)S(1)}, f32[4,8,128]{2,1,0:T(8,128)S(1)}) custom-call(s32[16]{0:T(128)S(1)} %copy-done.5, bf16[512,384]{1,0:T(8,128)(2,1)S(1)} %bitcast.27, bf16[4096,384]{1,0:T(8,128)(2,1)S(1)} %bitcast.25), custom_call_target="tpu_custom_call" | custom-call | tf_op jit(solution)/shard_map/near_forward/pallas_call | solution.py:1740
  67.6 0.0 copy-done
  67.6 0.0 copy-done.2
  67.6 0.0 copy-done.3
  67.6 0.0 copy-done.4
  67.6 0.0 copy-start.6
  67.7 61.1 %middle_kernel.1 = (bf16[128,768]{1,0:T(8,128)(2,1)S(1)}, f32[128,768]{1,0:T(8,128)S(1)}, bf16[4,128,256]{2,1,0:T(8,128)(2,1)S(1)}, bf16[2,4,2,32,768]{4,3,2,1,0...) custom-call(bf16[4,128,256]{2,1,0:T(8,128)(2,1)S(1)} %bitcast.33, ...), custom_call_target="tpu_custom_call" | custom-call | tf_op jit(solution)/shard_map/middle_kernel/pallas_call | solution.py:1592
  128.7 0.0 copy-done.6
  128.7 64.6 %turn_kernel.1 = (bf16[4,128,768]{2,1,0:T(8,128)(2,1)S(1)}, bf16[4,32,640]{2,1,0:T(8,128)(2,1)S(1)}, bf16[4,32,768]{2,1,0:T(8,128)(2,1)S(1)}, f32[96,768]{1,0:T(8,128)S(1)}, f32[32,768]{1,0:T(8,128)S(1)}) custom-call(s32[16]{0:T(128)S(1)} %copy-done.6, bf16[512,384]{1,0:T(8,128)(2,1)S(1)} %bitcast.28, bf16[4096,384]{1,0:T(8,128)(2,1)} %bitcast.26, ...), custom_call_target="tpu_custom_call" | custom-call | tf_op jit(solution)/shard_map/turn_kernel/pallas_call | solution.py:2059
  193.3 1.1 final_kernel.1
  194.5 0.7 copy.37
Async XLA Ops:
  56.8 1.1 copy-start.1
  57.8 9.8 %copy-start = (bf16[2,2,2,2,2,128,384]{6,5,4,3,2,1,0:T(8,128)(2,1)}, bf16[2,2,2,2,2,128,384]{6,5,4,3,2,1,0:T(8,128)(2,1)S(1)}, u32[]{:S(2)}) copy-start(bf16[2,2,2,2,2,128,384]{6,5,4,3,2,1,0:T(8,128)(2,1)S(1)} %get-tuple-element.55) | copy-start | bytes 9437188
  57.8 0.7 copy-start.5
  58.5 9.1 %copy-start.2 = (bf16[128,768]{1,0:T(8,128)(2,1)S(1)}, bf16[128,768]{1,0:T(8,128)(2,1)}, u32[]{:S(2)}) copy-start(bf16[128,768]{1,0:T(8,128)(2,1)} %tok.1) | copy-start | bytes 589828
  58.5 9.1 %copy-start.3 = (f32[96,768]{1,0:T(8,128)S(1)}, f32[96,768]{1,0:T(8,128)}, u32[]{:S(2)}) copy-start(f32[96,768]{1,0:T(8,128)} %w2f.1) | copy-start | bytes 884740
  58.5 9.1 %copy-start.4 = (bf16[128,768]{1,0:T(8,128)(2,1)S(1)}, bf16[128,768]{1,0:T(8,128)(2,1)}, u32[]{:S(2)}) copy-start(bf16[128,768]{1,0:T(8,128)(2,1)} %cot.1) | copy-start | bytes 589828
  67.6 61.1 %copy-start.6 = (s32[16]{0:T(128)S(1)}, s32[16]{0:T(128)}, u32[]{:S(2)}) copy-start(s32[16]{0:T(128)} %lengths_ref.3) | copy-start | bytes 196

commit v7 on v6

--- a/solution.py
+++ b/solution.py
@@ -957,7 +957,7 @@
     return np.stack(rows + [np.zeros_like(column)] * 4).astype(np.int32)
 
 
-def first_kernel(tokens, wq, wk, wv, vectors, inner, mix, e):
+def first_kernel(lengths, tokens, wq, wk, wv, vectors, inner, mix, e):
     n, depth = tokens.shape
     s = wq.shape[0]
     quarter = inner.shape[1] // 4
@@ -966,18 +966,19 @@
     count = len(vectors)
 
     def body(*refs):
-        tok = refs[0]
-        arguments = refs[1 : 7 + count]
+        lengths_in, tok = refs[:2]
+        arguments = refs[2 : 8 + count]
         (
-            tok_out, q_out, wqkv_out, vec_out, kv_all, w1, wm,
+            tok_out, q_out, wqkv_out, vec_out, kv_out, w1, wm, mixed_out, mixed_wide, lse_out,
             send, recv, local, tok_send, tok_recv,
-            slab, toks, weights, kv_own, q_own, w1s, wms, vec, few,
-            loaded, *places,
-        ) = refs[7 + count :]
+            slab, toks, weights, kv_own, q_own, w1s, wms, vec, few, kv_all, scaled, sums,
+            loaded, lengths_ref, lengths_sem, *places,
+        ) = refs[8 + count :]
         wq_ref, wk_ref, wv_ref, tab = places[:4]
         vecs = places[4 : 4 + count]
         w1f, wmf = places[4 + count :]
-        loads = []
+        loads = [pltpu.make_async_copy(lengths_in, lengths_ref, lengths_sem)]
+        loads[0].start()
         for index, (argument, place) in enumerate(zip(arguments, places)):
             loads.append(pltpu.make_async_copy(argument, place, loaded.at[index]))
             loads[-1].start()
@@ -1096,6 +1097,7 @@
 
         matrix = weights[:, :, :, :, : 2 * WIDE].reshape(depth, 2 * WIDE)
         kept, kv_first = [copies.keep(weights, wqkv_out), copies.keep(vec, vec_out)], []
+        kv_sibling, kv_kept = [], []
         for dv in range(2):
             v = (me.half + dv) % 2
             for u in range(2):
@@ -1113,25 +1115,91 @@
             kv_first.append(
                 [copies.push(kv_own.at[v], mine, me.at(x=x, y=y)) for x, y in square]
             )
-            arrivals.append(copies.push(kv_own.at[v], mine, me.sibling()))
-            kept.append(copies.keep(kv_own.at[v], mine))
+            kv_sibling.append(copies.push(kv_own.at[v], mine, me.sibling()))
+            kv_kept.append(copies.keep(kv_own.at[v], mine))
         block = w1.at[:, me.c, me.g, :]
         arrivals.append(copies.push(block, block, me.sibling()))
         kept += [copies.keep(toks, tok_out), copies.keep(q_own, q_out)]
+        for copy, (x, y) in zip(wm_second, square):
+            copy.wait_recv()
+            block = wm.at[x, me.c, :, y]
+            arrivals.append(copies.push(block, block, me.sibling()))
+
+        ends = ends_of(lengths_ref)
+        rows = GROUPS * n
+        spans = [slice(h * LANES, (h + 1) * LANES) for h in range(LOCAL)]
+        along = lax.broadcasted_iota(jnp.int32, (1, n), 1)
+        ranges = [document_of(along + tile_base(me, slot, n), ends) for slot in range(GROUPS)]
+        first = jnp.concatenate([low for low, _ in ranges], axis=1)
+        last = jnp.concatenate([high for _, high in ranges], axis=1)
+        down = lax.broadcasted_iota(jnp.int32, (rows, rows), 0)
+        for slot in range(GROUPS):
+            for h, span in enumerate(spans):
+                scaled[h, slot * n : (slot + 1) * n] = q_own[slot, :, span] * jnp.asarray(
+                    0.125, low_type
+                )
+        sums[...] = jnp.zeros_like(sums)
+
+        def attend(u, c, v, carry):
+            begin = ((u * 2 + c) * 2 + v) * rows
+            place = down + begin
+            same = (place >= first) & (place < last)
+            result = []
+            for h, span in enumerate(spans):
+                top, total = carry[h]
+                kv = kv_all[u, c, v, :, :, :, span].reshape(rows, LANES)
+                scores = lax.dot_general(kv, scaled[h], NEXT, preferred_element_type=wide)
+                scores = jnp.where(same, scores, mask_fill)
+                new_top = jnp.maximum(top, jnp.max(scores, axis=0, keepdims=True))
+                factor = jnp.exp(top - new_top)
+                powers = jnp.exp(scores - new_top)
+                total = total * factor + jnp.sum(powers, axis=0, keepdims=True)
+                sums[h] = sums[h] * factor + lax.dot_general(
+                    kv, powers.astype(low_type), DOWN, preferred_element_type=wide
+                )
+                result.append((new_top, total))
+            return tuple(result)
+
+        state = tuple(
+            (jnp.full((1, rows), lowest_start, wide), jnp.zeros((1, rows), wide))
+            for _ in range(LOCAL)
+        )
         for dv in range(2):
             v = (me.half + dv) % 2
+            forwards = [kv_sibling[dv]]
             for copy, (x, y) in zip(kv_first[dv], square):
                 copy.wait_recv()
                 block = kv_all.at[:, me.c, v, (x + me.c) % 2, y]
-                arrivals.append(copies.push(block, block, me.sibling()))
-        for copy, (x, y) in zip(wm_second, square):
-            copy.wait_recv()
-            block = wm.at[x, me.c, :, y]
-            arrivals.append(copies.push(block, block, me.sibling()))
+                forwards.append(copies.push(block, block, me.sibling()))
+            kv_kept[dv].wait()
+            state = lax.fori_loop(
+                0, 2, lambda u, carry, v=v: attend(u, me.c, v, carry), state
+            )
+            for copy in forwards:
+                copy.wait_recv()
+            state = lax.fori_loop(
+                0, 2, lambda u, carry, v=v: attend(u, 1 - me.c, v, carry), state
+            )
+        kept.append(copies.keep(kv_all, kv_out))
         for copy, (_, source) in zip(w1_second, me.line()):
             copy.wait_recv()
             block = w1.at[:, me.c, source, :]
             arrivals.append(copies.push(block, block, me.sibling()))
+        lane = lax.broadcasted_iota(jnp.int32, (n, LANES), 1)
+        upper = lane >= HEAD
+        for slot in range(GROUPS):
+            part = slice(slot * n, (slot + 1) * n)
+            mixes = []
+            for h in range(LOCAL):
+                top, total = state[h]
+                mixes.append(jnp.transpose(sums[h, :, part] / total[:, part]))
+                lse_out[slot, h : h + 1, :] = top[:, part] + jnp.log(total[:, part])
+            turned = [pltpu.roll(mixes[h], HEAD, 1) for h in (0, 2)]
+            both = jnp.concatenate(
+                [jnp.where(upper, mixes[1], turned[0]), jnp.where(upper, 0.0, turned[1])], axis=1
+            )
+            mixed_wide[part, :] = both
+            mixed_out[slot] = both.astype(low_type)
         for copy in arrivals:
             copy.wait_recv()
         for copy in kept:
@@ -1148,14 +1216,18 @@
         out_shape=(
             jax.ShapeDtypeStruct((GROUPS, n, depth), low_type),
             jax.ShapeDtypeStruct((GROUPS, n, WIDE), low_type),
-            jax.ShapeDtypeStruct((4, GROUPS, 2, s, cols), low_type),
+            pltpu.HBM((4, GROUPS, 2, s, cols), low_type),
             jax.ShapeDtypeStruct((SMALL, 2 * WIDE), wide),
-            jax.ShapeDtypeStruct((2, 2, 2, 2, 2, n, WIDE), low_type),
+            pltpu.HBM((2, 2, 2, 2, 2, n, WIDE), low_type),
             jax.ShapeDtypeStruct((2, 2, GROUPS, 2, s, quarter), low_type),
             jax.ShapeDtypeStruct((2, 2, GROUPS, 2, s, depth), low_type),
+            jax.ShapeDtypeStruct((GROUPS, n, PACK), low_type),
+            jax.ShapeDtypeStruct((GROUPS * n, PACK), wide),
+            jax.ShapeDtypeStruct((GROUPS, 8, n), wide),
         ),
-        in_specs=[pl.BlockSpec(memory_space=pltpu.HBM)] * (7 + count),
-        out_specs=(pl.BlockSpec(memory_space=pl.ANY),) * 7,
+        in_specs=[pl.BlockSpec(memory_space=pltpu.HBM)] * (8 + count),
+        out_specs=(pl.BlockSpec(memory_space=pl.ANY),) * 7
+        + (pl.BlockSpec(memory_space=vmem),) * 3,
         scratch_shapes=[
             dma((total,)), dma((total,)), dma((12,)), dma((4,)), dma((4,)),
             vmem((GROUPS, s, cols), low_type),
@@ -1167,13 +1239,18 @@
             vmem((s, depth), low_type),
             vmem((SMALL, 2 * WIDE), wide),
             vmem((s, LANES), wide),
+            vmem((2, 2, 2, 2, 2, n, WIDE), low_type),
+            vmem((LOCAL, GROUPS * n, LANES), low_type),
+            vmem((LOCAL, LANES, GROUPS * n), wide),
             dma((6 + count,)),
+            pltpu.SMEM(lengths.shape, jnp.int32),
+            dma,
             *[vmem(item.shape, item.dtype) for item in (wq, wk, wv, tables, *vectors, inner, mix)],
         ],
         compiler_params=pltpu.CompilerParams(
             collective_id=10, has_side_effects=True, vmem_limit_bytes=NEAR_LIMIT
         ),
-    )(*[pltpu.with_memory_space_constraint(item, pltpu.HBM) for item in (tokens, wq, wk, wv, tables, *vectors, inner, mix)])
+    )(*[pltpu.with_memory_space_constraint(item, pltpu.HBM) for item in (lengths, tokens, wq, wk, wv, tables, *vectors, inner, mix)])
 
 
 def pass_back(ident, pieces):
@@ -1329,10 +1406,10 @@
     hn = n // 2
 
     def body(
-        mixed_ref, tok, cot, wm_in, w1_in, w2f, vec_ref,
+        mixed_ref, tok_in, cot_in, wm_in, w1_in, w2f_in, vec_in,
         out, hidden_out, do_out, sm, s1, s2,
         send, recv, local, back_send, back_recv, on_send, on_recv,
-        swap_send2, swap_recv2, wm, w1, w2p, w2s, came, mixed_tok, xs, acts, slopes, parts, sums, bgs, igs, parts2, sums2,
+        swap_send2, swap_recv2, tok, cot, w2f, vec_ref, wm, w1, w2p, w2s, came, mixed_tok, xs, acts, slopes, parts, sums, bgs, igs, parts2, sums2,
         pieces, extra, attn, own1, own2, g1, g2, gm,
     ):
         me = Spot()
@@ -1355,13 +1432,19 @@
             ],
         )
         loads = [copies.keep(wm_in, wm), copies.keep(w1_in, w1)]
-        w2s[...] = w2f[...].astype(low_type)
+        small_loads = [
+            copies.keep(source, target)
+            for source, target in ((tok_in, tok), (vec_in, vec_ref), (w2f_in, w2f), (cot_in, cot))
+        ]
         pl.semaphore_wait(barrier, expected)
 
         back = Scatter(back_send, back_recv, me.selfish)
         back.start([(mixed_ref.at[slot], device) for slot, device in owners], came.at[me.g], me.g)
         lower = lax.broadcasted_iota(jnp.int32, (n, LANES), 1) < HEAD
         loads[0].wait()
+        for copy in small_loads:
+            copy.wait()
+        w2s[...] = w2f[...].astype(low_type)
         for g in range(GROUPS):
             back.arrived(g, came.at[g])
         w2_place = w2p.at[me.g, me.y]
@@ -1588,7 +1671,9 @@
     tall = vmem((2, 4, hn, depth), low_type)
     full = vmem((2, 4, hn, depth), wide)
     high = vmem((2, 4, hn, quarter), low_type)
-    space = [vmem] * 3 + [pl.ANY] * 2 + [vmem] * 2
+    tokens, cotangent, outer = [
+        pltpu.with_memory_space_constraint(item, pltpu.HBM) for item in (tokens, cotangent, outer)
+    ]
     return pl.pallas_call(
         body,
         name="middle_kernel",
@@ -1600,12 +1685,19 @@
             jax.ShapeDtypeStruct((2, GROUPS, 2, rows, quarter), low_type),
             jax.ShapeDtypeStruct((GROUPS, e, depth), low_type),
         ),
-        in_specs=[pl.BlockSpec(memory_space=item) for item in space],
+        in_specs=[
+            pl.BlockSpec(memory_space=item)
+            for item in (pl.ANY, pltpu.HBM, pltpu.HBM, pl.ANY, pl.ANY, pltpu.HBM, pl.ANY)
+        ],
         out_specs=[
             pl.BlockSpec(memory_space=item) for item in (vmem, vmem, pl.ANY, vmem, vmem, vmem)
         ],
         scratch_shapes=[
             dma((48,)), dma((48,)), dma((8,)), dma((4,)), dma((4,)), dma((4,)), dma((4,)), dma, dma,
+            vmem((n, depth), low_type),
+            vmem((n, depth), low_type),
+            vmem((e, depth), wide),
+            vmem(vec.shape, wide),
             vmem((depth, depth), low_type),
             vmem((depth, quarter), low_type),
             vmem((GROUPS, 2, e, depth), low_type),
@@ -1649,107 +1741,6 @@
     for end in reversed(ends[:-1]):
         last = jnp.where(end <= place, last, end)
     return first, last
-
-
-def blocks_of(base, ends, n, block):
-    low, _ = document_of(base, ends)
-    _, high = document_of(base + n - 1, ends)
-    return low // block, (high + block - 1) // block
-
-
-def near_forward(lengths, queries, keys, n, block):
-    total_rows = queries.shape[0]
-    tokens = keys.shape[0]
-    chunks = [slice(index * LANES, (index + 1) * LANES) for index in range(block // LANES)]
-
-    def body(lengths_ref, q_ref, kv_ref, out_ref, keep_ref, lse_ref, table):
-        me = Spot()
-        ends = ends_of(lengths_ref)
-        lane = lax.broadcasted_iota(jnp.int32, (n, LANES), 1)
-        upper = lane >= HEAD
-        column = lax.broadcasted_iota(jnp.int32, (n, LANES), 0)
-
-        def one(slot, unused):
-            rows = pl.ds(pl.multiple_of(slot * n, n), n)
-            base = tile_base(me, slot, n)
-            low, high = blocks_of(base, ends, n, block)
-            first, last = document_of(column + base, ends)
-            heads = [
-                q_ref[rows, h * LANES : (h + 1) * LANES] * jnp.asarray(0.125, low_type)
-                for h in range(LOCAL)
-            ]
-
-            def score(j, tops):
-                begin = pl.multiple_of(j * block, block)
-                same = []
-                for chunk in chunks:
-                    place = lane + (begin + chunk.start)
-                    same.append((place >= first) & (place < last))
-                result = []
-                for h in range(LOCAL):
-                    kv = kv_ref[pl.ds(begin, block), h * LANES : (h + 1) * LANES]
-                    scores = lax.dot_general(heads[h], kv, NEXT, preferred_element_type=wide)
-                    top = tops[h]
-                    for chunk, mask in zip(chunks, same):
-                        part = jnp.where(mask, scores[:, chunk], mask_fill)
-                        table[h, j, :, chunk] = part
-                        top = jnp.maximum(top, part)
-                    result.append(top)
-                return tuple(result)
-
-            tops = lax.fori_loop(
-                low, high, score, (jnp.full((n, LANES), lowest_start, wide),) * LOCAL
-            )
-            tops = [jnp.max(top, axis=1, keepdims=True) for top in tops]
-            spread = [jnp.broadcast_to(top, (n, LANES)) for top in tops]
-
-            def weigh(j, carry):
-                begin = pl.multiple_of(j * block, block)
-                result = []
-                for h in range(LOCAL):
-                    total, mixed = carry[h]
-                    kv = kv_ref[pl.ds(begin, block), h * LANES : (h + 1) * LANES]
-                    parts = []
-                    for chunk in chunks:
-                        part = jnp.exp(table[h, j, :, chunk] - spread[h])
-                        total = total + part
-                        parts.append(part.astype(low_type))
-                    powers = jnp.concatenate(parts, axis=1)
-                    mixed = mixed + jnp.dot(powers, kv, preferred_element_type=wide)
-                    result.append((total, mixed))
-                return tuple(result)
-
-            zero = jnp.zeros((n, LANES), wide)
-            done = lax.fori_loop(low, high, weigh, ((zero, zero),) * LOCAL)
-            totals = [jnp.sum(total, axis=1, keepdims=True) for total, _ in done]
-            mixes = [mixed / total for total, (_, mixed) in zip(totals, done)]
-            turned = [pltpu.roll(mixed, HEAD, 1) for mixed in mixes]
-            front = jnp.where(upper, mixes[1], turned[0])
-            back = jnp.where(upper, 0.0, turned[2])
-            both = jnp.concatenate([front, back], axis=1)
-            keep_ref[rows, :] = both
-            out_ref[rows, :] = both.astype(low_type)
-            logs = [top + jnp.log(total) for top, total in zip(tops, totals)]
-            logs = jnp.where(lane == 0, logs[0], jnp.where(lane == 1, logs[1], logs[2]))
-            lse_ref[slot] = jnp.transpose(logs)[:8]
-            return unused
-
-        lax.fori_loop(0, GROUPS, one, 0)
-
-    vmem = pl.BlockSpec(memory_space=pltpu.VMEM)
-    return pl.pallas_call(
-        body,
-        name="near_forward",
-        out_shape=(
-            jax.ShapeDtypeStruct((total_rows, PACK), low_type),
-            jax.ShapeDtypeStruct((total_rows, PACK), wide),
-            jax.ShapeDtypeStruct((GROUPS, 8, n), wide),
-        ),
-        in_specs=[pl.BlockSpec(memory_space=pltpu.SMEM)] + [vmem] * 2,
-        out_specs=(vmem,) * 3,
-        scratch_shapes=[pltpu.VMEM((LOCAL, tokens // block, n, block), wide)],
-        compiler_params=pltpu.CompilerParams(vmem_limit_bytes=NEAR_LIMIT),
-    )(lengths, queries, keys)
 
 
 def turn_kernel(lengths, queries, keys, grads_in, mixed, lse, tokens, weights, sum1, sum2, summ):
@@ -2364,8 +2355,8 @@
         )
     ]
     vectors.append(inner_bias.reshape(1, -1))
-    toks, queries, w_qkv, vec, kv_all, w1, wm = first_kernel(
-        tokens, query_weight, key_weight, value_weight, vectors,
+    toks, queries, w_qkv, vec, kv_all, w1, wm, mixed, mixed_wide, lse = first_kernel(
+        doc_lengths, tokens, query_weight, key_weight, value_weight, vectors,
         inner_weight, mix_weight, e,
     )
     queries = queries.reshape(rows, WIDE)
@@ -2373,7 +2364,6 @@
     w_qkv = w_qkv.reshape(depth, -1)
     w1 = w1.reshape(depth, quarter)
     wm = wm.reshape(depth, depth)
-    mixed, mixed_wide, lse = near_forward(doc_lengths, queries, kv_all, n, 512)
     output, hidden_grad, grad_all, summ, sum1, sum2 = middle_kernel(
         mixed.reshape(GROUPS, n, PACK), tokens, cotangent, wm, w1, outer_weight, vec, s, e
     )

time: 196 us -> 190 us (0.969)
  Pallas kernels: 192 us -> 187 us
    pallas_call x1 -> x0, Pallas kernels: 9.11 us -> none  [near_forward(): pl.pallas_call(body, name='near_forward', out_shape=(jax.ShapeDtypeStruct...]
    pallas_call x1, Pallas kernels: 56.1 us -> 62.6 us  [first_kernel(): pl.pallas_call(body, name='first_kernel', out_shape=(jax.ShapeDtypeStruct...]
    pallas_call x1, Pallas kernels: 64.6 us -> 62.2 us  [turn_kernel(): pl.pallas_call(body, name='turn_kernel', out_shape=(jax.ShapeDtypeStruct(...]
where the time goes in v7:
time: 190 us; the launch traced here: 189 us
  Pallas kernels  187 us (98%)
    pallas_call x1, Pallas kernels, first_kernel(): pl.pallas_call(body, name='first_kernel', out_shape=(jax.ShapeDtypeStruct...  62.6 us
    pallas_call x1, Pallas kernels, turn_kernel(): pl.pallas_call(body, name='turn_kernel', out_shape=(jax.ShapeDtypeStruct(...  62.2 us
    pallas_call x1, Pallas kernels, middle_kernel(): pl.pallas_call(body, name='middle_kernel', out_shape=(jax.ShapeDtypeStruc...  61.2 us

profile of v7, /device:TPU:0, one launch (start us, length us, event | category | flops | bytes accessed | tf_op | source)
XLA Modules:
  0.0 188.5 jit_solution(4676074314324797497)
XLA Ops:
  0.7 62.6 %first_kernel.1 = (bf16[4,128,768]{2,1,0:T(8,128)(2,1)S(1)}, bf16[4,128,384]{2,1,0:T(8,128)(2,1)S(1)}, bf16[4,4,2,24,896]{4,3,2,1,0:T(8,128)(2,1)}, f32[16,768]{...) custom-call(s32[16]{0:T(128)} %lengths_ref.1, ...), custom_call_target="tpu_custom_call" | custom-call | tf_op jit(solution)/shard_map/first_kernel/pallas_call | solution.py:1213
  63.2 0.0 copy-start
  63.3 61.2 %middle_kernel.1 = (bf16[128,768]{1,0:T(8,128)(2,1)S(1)}, f32[128,768]{1,0:T(8,128)S(1)}, bf16[4,128,256]{2,1,0:T(8,128)(2,1)S(1)}, bf16[2,4,2,32,768]{4,3,2,1,0...) custom-call(bf16[4,128,256]{2,1,0:T(8,128)(2,1)S(1)} %get-tuple-element.54.mixed_ref, ...), custom_call_target="tpu_custom_call" | custom-call | tf_op jit(solution)/shard_map/middle_kernel/pallas_call | solution.py:1677
  124.5 0.0 copy-done
  124.5 62.2 %turn_kernel.1 = (bf16[4,128,768]{2,1,0:T(8,128)(2,1)S(1)}, bf16[4,32,640]{2,1,0:T(8,128)(2,1)S(1)}, bf16[4,32,768]{2,1,0:T(8,128)(2,1)S(1)}, f32[96,768]{1,0:T(8,128)S(1)}, f32[32,768]{1,0:T(8,128)S(1)}) custom-call(s32[16]{0:T(128)S(1)} %copy-done, bf16[512,384]{1,0:T(8,128)(2,1)S(1)} %bitcast.26, bf16[4096,384]{1,0:T(8,128)(2,1)} %bitcast.28, ...), custom_call_target="tpu_custom_call" | custom-call | tf_op jit(solution)/shard_map/turn_kernel/pallas_call | solution.py:2050
  186.7 1.1 final_kernel.1
  187.9 0.7 copy.37
Async XLA Ops:
  63.2 61.3 %copy-start = (s32[16]{0:T(128)S(1)}, s32[16]{0:T(128)}, u32[]{:S(2)}) copy-start(s32[16]{0:T(128)} %lengths_ref.1) | copy-start | bytes 196

commit v8 on v7

--- a/solution.py
+++ b/solution.py
@@ -1036,9 +1036,6 @@
         slab_own.wait()
         for copy in slab_first:
             copy.wait_recv()
-        wm_first = [
-            copies.push(wms, wm.at[me.x, me.c, me.g, me.y], me.at(g=to)) for to in line
-        ]
         tokens_go = Scatter(tok_send, tok_recv, me.selfish)
         tokens_go.start([(tok, device) for _, device in me.readers()], toks.at[me.slot()], me.slot())
         block = view.at[me.a, :, me.y]
@@ -1048,12 +1045,6 @@
             copy.wait_recv()
             block = view.at[x * 2 + me.c, :, y]
             weight_arrivals.append(copies.push(block, block, me.sibling()))
-        wm_own.wait()
-        for copy in wm_first:
-            copy.wait_recv()
-        block = wm.at[me.x, me.c, :, me.y]
-        wm_second = [copies.push(block, block, me.at(x=x, y=y)) for x, y in square]
-        arrivals.append(copies.push(block, block, me.sibling()))
         w1_own.wait()
         for copy in w1_first:
             copy.wait_recv()
@@ -1104,6 +1095,9 @@
                 tokens_go.arrived(u * 2 + v, toks.at[u * 2 + v])
             if dv:
                 block = w1.at[:, me.c, me.g, :]
+                wm_first = [
+                    copies.push(wms, wm.at[me.x, me.c, me.g, me.y], me.at(g=to)) for to in line
+                ]
                 w1_second = [copies.push(block, block, me.at(g=to)) for to in line]
             both = jnp.concatenate([toks[v], toks[2 + v]], axis=0)
             made = jnp.dot(both, matrix, preferred_element_type=wide)
@@ -1120,10 +1114,6 @@
         block = w1.at[:, me.c, me.g, :]
         arrivals.append(copies.push(block, block, me.sibling()))
         kept += [copies.keep(toks, tok_out), copies.keep(q_own, q_out)]
-        for copy, (x, y) in zip(wm_second, square):
-            copy.wait_recv()
-            block = wm.at[x, me.c, :, y]
-            arrivals.append(copies.push(block, block, me.sibling()))
 
         ends = ends_of(lengths_ref)
         rows = GROUPS * n
@@ -1172,6 +1162,13 @@
                 block = kv_all.at[:, me.c, v, (x + me.c) % 2, y]
                 forwards.append(copies.push(block, block, me.sibling()))
             kv_kept[dv].wait()
+            if dv:
+                wm_own.wait()
+                for copy in wm_first:
+                    copy.wait_recv()
+                block = wm.at[me.x, me.c, :, me.y]
+                wm_second = [copies.push(block, block, me.at(x=x, y=y)) for x, y in square]
+                arrivals.append(copies.push(block, block, me.sibling()))
             state = lax.fori_loop(
                 0, 2, lambda u, carry, v=v: attend(u, me.c, v, carry), state
             )
@@ -1181,6 +1178,10 @@
                 0, 2, lambda u, carry, v=v: attend(u, 1 - me.c, v, carry), state
             )
         kept.append(copies.keep(kv_all, kv_out))
+        for copy, (x, y) in zip(wm_second, square):
+            copy.wait_recv()
+            block = wm.at[x, me.c, :, y]
+            arrivals.append(copies.push(block, block, me.sibling()))
         for copy, (_, source) in zip(w1_second, me.line()):
             copy.wait_recv()
             block = w1.at[:, me.c, source, :]
@@ -1299,12 +1300,13 @@
     )(pieces)
 
 
-def final_kernel(hidden, pieces, outqk, out1, out2, outm, s, e):
+def final_kernel(output, hidden, pieces, outqk, out1, out2, outm, s, e):
     n, depth = hidden.shape
     quarter = out1.shape[-1]
 
-    def body(hid, dx, qk_in, i_in, o_in, m_in, xg, qw, qb, kw, vw, vb, mw, mb, eg, es, iw, ib, ow, ob, fg, fs):
+    def body(y_in, hid, dx, qk_in, i_in, o_in, m_in, yo, xg, qw, qb, kw, vw, vb, mw, mb, eg, es, iw, ib, ow, ob, fg, fs):
         device = lax.axis_index("au") * lax.axis_size("row") + lax.axis_index("row")
+        yo[...] = y_in[...]
         xg[...] = total_of(hid[...], dx[0], dx[1], dx[2], dx[3]).astype(low_type)
         rows = qk_in.shape[1]
         q_in, k_in = qk_in.at[:, :, WIDE:], qk_in.at[:, :, :WIDE]
@@ -1358,15 +1360,16 @@
         name="final_kernel",
         out_shape=(
             jax.ShapeDtypeStruct((n, depth), low_type),
+            jax.ShapeDtypeStruct((n, depth), low_type),
             shape(s, depth), shape(1, s), shape(s, depth), shape(s, depth), shape(1, s),
             shape(s, depth), shape(1, s), shape(1, s), shape(1, s),
             shape(s, 4 * quarter), shape(1, e), shape(e, depth),
             shape(1, s), shape(1, s), shape(1, s),
         ),
-        in_specs=[pl.BlockSpec(memory_space=vmem)] * 6,
-        out_specs=(pl.BlockSpec(memory_space=vmem),) * 16,
+        in_specs=[pl.BlockSpec(memory_space=vmem)] * 7,
+        out_specs=(pl.BlockSpec(memory_space=vmem),) * 17,
         compiler_params=pltpu.CompilerParams(vmem_limit_bytes=NEAR_LIMIT),
-    )(hidden, pieces, outqk, out1, out2, outm)
+    )(output, hidden, pieces, outqk, out1, out2, outm)
 
 
 def gelu_and_slope(value):
@@ -1758,7 +1761,7 @@
         lengths_ref, q_ref, kv_ref, do_ref, mixed_ref, lse_ref, tok, w_ref, s1, s2, sm,
         dx_out, outqk, out1, out2, outm,
         send, recv, local, dx_send, dx_recv, swap_send, swap_recv, ks, kr, ps, pr,
-        both, kbuf, kin, pk, dqs, grads, narrow, dxs, gk, sk, pp, fk, p1, f1, pm, fm, tm, p2,
+        both, kbuf, kin, pk, dqs, grads, narrow, dxs, gk, sk, pp, fk, p1, f1, pm, fm, tm, p2, early,
     ):
         me = Spot()
         copies = Copies(send, recv, local)
@@ -1911,8 +1914,21 @@
 
             loop(GROUPS, add)
 
+        def weight_grad(slots, half):
+            span = slice(half * cut, (half + 1) * cut)
+            return lax.dot_general(
+                jnp.concatenate([tok[slot, :, span] for slot in slots], axis=0),
+                jnp.concatenate([narrow[slot] for slot in slots], axis=0),
+                DOWN,
+                preferred_element_type=wide,
+            )
+
         moves = []
+        slots = [turn % 2 * 2 + (me.half + turn // 2) % 2 for turn in range(4)]
         for turn in range(4):
+            if turn == 3:
+                for half in range(2):
+                    early[half] = weight_grad(slots[:3], half)
             u, dv = turn % 2, turn // 2
             v = (me.half + dv) % 2
             slot = u * 2 + v
@@ -1960,15 +1976,10 @@
             def _(copy=copy):
                 copy.start()
 
-        values = narrow[...].reshape(GROUPS * n, width)
-        bias = jnp.broadcast_to(down_sum(values.astype(wide)), (8, width)).astype(low_type)
+        bias = down_sum(total_of(*[down_sum(narrow[slot].astype(wide)) for slot in range(GROUPS)]))
+        bias = jnp.broadcast_to(bias, (8, width)).astype(low_type)
         for half in range(2):
-            made = lax.dot_general(
-                tok[:, :, half * cut : (half + 1) * cut].reshape(GROUPS * n, cut),
-                values,
-                DOWN,
-                preferred_element_type=wide,
-            ).astype(low_type)
+            made = (early[half] + weight_grad(slots[3:], half)).astype(low_type)
             for index in range(16):
                 place = (half, index // 8, index // 2 % GROUPS, index % 2)
                 gk[(*place, slice(None, s))] = made[index * s : (index + 1) * s]
@@ -2080,6 +2091,7 @@
             vmem((GROUPS, rows, depth), low_type),
             vmem((3, rows, depth), low_type),
             vmem((4, tall, depth), low_type),
+            vmem((2, cut, width), wide),
         ],
         compiler_params=pltpu.CompilerParams(
             collective_id=11, has_side_effects=True, vmem_limit_bytes=TURN_LIMIT
@@ -2371,8 +2383,8 @@
     pieces, outqk, out1, out2, outm = turn_kernel(
         doc_lengths, queries, kv_all, grad_all, mixed_wide, lse, toks, w_qkv, sum1, sum2, summ
     )
-    results = final_kernel(hidden_grad, pieces, outqk, out1, out2, outm, s, e)
-    return (output,) + tuple(
+    results = final_kernel(output, hidden_grad, pieces, outqk, out1, out2, outm, s, e)
+    return tuple(
         result.reshape(-1) if result.shape[0] == 1 else result for result in results
     )
 

time: 190 us -> 188 us (0.989)
    pallas_call x1, Pallas kernels: 62.6 us -> 59.5 us  [first_kernel(): pl.pallas_call(body, name='first_kernel', out_shape=(jax.ShapeDtypeStruct...]
    pallas_call x1, Pallas kernels: 61.2 us -> 63.8 us  [middle_kernel(): pl.pallas_call(body, name='middle_kernel', out_shape=(jax.ShapeDtypeStruc...]
where the time goes in v8:
time: 188 us; the launch traced here: 187 us
  Pallas kernels  186 us (99%)
    pallas_call x1, Pallas kernels, middle_kernel(): pl.pallas_call(body, name='middle_kernel', out_shape=(jax.ShapeDtypeStruc...  63.8 us
    pallas_call x1, Pallas kernels, turn_kernel(): pl.pallas_call(body, name='turn_kernel', out_shape=(jax.ShapeDtypeStruct(...  61.7 us
    pallas_call x1, Pallas kernels, first_kernel(): pl.pallas_call(body, name='first_kernel', out_shape=(jax.ShapeDtypeStruct...  59.5 us

profile of v8, /device:TPU:0, one launch (start us, length us, event | category | flops | bytes accessed | tf_op | source)
XLA Modules:
  0.0 187.1 jit_solution(10299409559151345372)
XLA Ops:
  0.7 59.5 %first_kernel.1 = (bf16[4,128,768]{2,1,0:T(8,128)(2,1)S(1)}, bf16[4,128,384]{2,1,0:T(8,128)(2,1)S(1)}, bf16[4,4,2,24,896]{4,3,2,1,0:T(8,128)(2,1)}, f32[16,768]{...) custom-call(s32[16]{0:T(128)} %lengths_ref.1, ...), custom_call_target="tpu_custom_call" | custom-call | tf_op jit(solution)/shard_map/first_kernel/pallas_call | solution.py:1214
  60.2 0.0 copy-start
  60.2 63.8 %middle_kernel.1 = (bf16[128,768]{1,0:T(8,128)(2,1)S(1)}, f32[128,768]{1,0:T(8,128)S(1)}, bf16[4,128,256]{2,1,0:T(8,128)(2,1)S(1)}, bf16[2,4,2,32,768]{4,3,2,1,0...) custom-call(bf16[4,128,256]{2,1,0:T(8,128)(2,1)S(1)} %get-tuple-element.55.mixed_ref, ...), custom_call_target="tpu_custom_call" | custom-call | tf_op jit(solution)/shard_map/middle_kernel/pallas_call | solution.py:1680
  124.0 0.0 copy-done
  124.0 61.7 %turn_kernel.1 = (bf16[4,128,768]{2,1,0:T(8,128)(2,1)S(1)}, bf16[4,32,640]{2,1,0:T(8,128)(2,1)S(1)}, bf16[4,32,768]{2,1,0:T(8,128)(2,1)S(1)}, f32[96,768]{1,0:T(8,128)S(1)}, f32[32,768]{1,0:T(8,128)S(1)}) custom-call(s32[16]{0:T(128)S(1)} %copy-done, bf16[512,384]{1,0:T(8,128)(2,1)S(1)} %bitcast.26, bf16[4096,384]{1,0:T(8,128)(2,1)} %bitcast.28, ...), custom_call_target="tpu_custom_call" | custom-call | tf_op jit(solution)/shard_map/turn_kernel/pallas_call | solution.py:2061
  185.7 1.2 final_kernel.1
Async XLA Ops:
  60.2 63.8 %copy-start = (s32[16]{0:T(128)S(1)}, s32[16]{0:T(128)}, u32[]{:S(2)}) copy-start(s32[16]{0:T(128)} %lengths_ref.1) | copy-start | bytes 196

commit v9 on v8

--- a/solution.py
+++ b/solution.py
@@ -961,7 +961,8 @@
     n, depth = tokens.shape
     s = wq.shape[0]
     quarter = inner.shape[1] // 4
-    cols = 2 * WIDE + LANES
+    width = WIDE + PACK
+    cols = width + LANES
     tables = jnp.asarray(first_tables(s, e, 2 * WIDE))
     count = len(vectors)
 
@@ -1000,23 +1001,32 @@
         lower = lane < HEAD
         for head in range(HEADS):
             pair = slice(head // 2 * LANES, head // 2 * LANES + LANES)
-            q, k, v = wq_ref[:, pair], wk_ref[:, pair], wv_ref[:, pair]
+            k, v = wk_ref[:, pair], wv_ref[:, pair]
             if head % 2:
-                q, k = pltpu.roll(q, HEAD, 1), pltpu.roll(k, HEAD, 1)
+                k = pltpu.roll(k, HEAD, 1)
             else:
                 v = pltpu.roll(v, HEAD, 1)
             g, h = head // LOCAL, head % LOCAL
             slab[g, :, h * LANES : (h + 1) * LANES] = jnp.where(lower, k, v).astype(low_type)
-            slab[g, :, WIDE + h * LANES : WIDE + (h + 1) * LANES] = jnp.where(lower, q, 0.0).astype(
-                low_type
-            )
+        for half in range(2):
+            b0, b1, b2 = [
+                wq_ref[:, (3 * half + index) * LANES : (3 * half + index + 1) * LANES]
+                for index in range(3)
+            ]
+            r1, r2 = pltpu.roll(b1, HEAD, 1), pltpu.roll(b2, HEAD, 1)
+            tiles = [(b0, b1), (jnp.where(lower, r1, r2), r2)]
+            for odd, (front, back) in enumerate(tiles):
+                slab[2 * half + odd, :, WIDE : WIDE + LANES] = front.astype(low_type)
+                slab[2 * half + odd, :, WIDE + LANES : width] = jnp.where(lower, back, 0.0).astype(
+                    low_type
+                )
         wms[...] = wmf[...].astype(low_type)
         few[...] = jnp.zeros((s, LANES), wide)
         for index in range(count):
             few[index : index + 1, : vecs[index].shape[1]] = vecs[index][...]
         small = few[...]
         for g in range(GROUPS):
-            slab[g, :, 2 * WIDE :] = small.astype(low_type)
+            slab[g, :, width:] = small.astype(low_type)
         pl.semaphore_wait(barrier, expected)
 
         view = weights
@@ -1064,29 +1074,27 @@
             return jnp.sum(found.reshape(count // SMALL, SMALL, 2 * WIDE), axis=0)
 
         every = spread(
-            view[:, :, :, :SMALL, 2 * WIDE :].reshape(32, SMALL, LANES), table[0:1], table[1:2]
+            view[:, :, :, :SMALL, width:].reshape(32, SMALL, LANES), table[0:1], table[1:2]
         )
         w_me = me.x * 2 + me.y
         inner_bias = spread(
-            view[w_me, :, :, :SMALL, 2 * WIDE :].reshape(8, SMALL, LANES), table[2:3], table[3:4]
+            view[w_me, :, :, :SMALL, width:].reshape(8, SMALL, LANES), table[2:3], table[3:4]
         )
         rows16 = lax.broadcasted_iota(jnp.int32, (SMALL, 2 * WIDE), 0)
         vec[...] = jnp.where(rows16 == 8, inner_bias, every)
         turned = pltpu.roll(every, 2 * WIDE - me.g * LOCAL * HEAD, 1)
         lower = lax.broadcasted_iota(jnp.int32, (1, LANES), 1) < HEAD
-        biases = [[], []]
+        biases = []
         for h in range(LOCAL):
-            pair = slice(h // 2 * LANES, h // 2 * LANES + LANES)
-            q, v = turned[0:1, pair], turned[1:2, pair]
-            if h % 2:
-                q = pltpu.roll(q, HEAD, 1)
-            else:
-                v = pltpu.roll(v, HEAD, 1)
-            biases[0].append(jnp.where(lower, 0.0, v))
-            biases[1].append(jnp.where(lower, q, 0.0))
-        bias = jnp.concatenate(biases[0] + biases[1], axis=1)
-
-        matrix = weights[:, :, :, :, : 2 * WIDE].reshape(depth, 2 * WIDE)
+            v = turned[1:2, h // 2 * LANES : h // 2 * LANES + LANES]
+            v = v if h % 2 else pltpu.roll(v, HEAD, 1)
+            biases.append(jnp.where(lower, 0.0, v))
+        biases.append(turned[0:1, :LANES])
+        biases.append(jnp.where(lower, turned[0:1, LANES : 2 * LANES], 0.0))
+        bias = jnp.concatenate(biases, axis=1)
+        lower_rows = lax.broadcasted_iota(jnp.int32, (n, LANES), 1) < HEAD
+
+        matrix = weights[:, :, :, :, :width].reshape(depth, width)
         kept, kv_first = [copies.keep(weights, wqkv_out), copies.keep(vec, vec_out)], []
         kv_sibling, kv_kept = [], []
         for dv in range(2):
@@ -1101,10 +1109,15 @@
                 w1_second = [copies.push(block, block, me.at(g=to)) for to in line]
             both = jnp.concatenate([toks[v], toks[2 + v]], axis=0)
             made = jnp.dot(both, matrix, preferred_element_type=wide)
-            made = (made + bias).astype(low_type)
+            made = made + bias
             for u in range(2):
-                kv_own[v, u] = made[u * n : (u + 1) * n, :WIDE]
-                q_own[u * 2 + v] = made[u * n : (u + 1) * n, WIDE:]
+                mine = made[u * n : (u + 1) * n]
+                kv_own[v, u] = mine[:, :WIDE].astype(low_type)
+                front, back = mine[:, WIDE : WIDE + LANES], mine[:, WIDE + LANES :]
+                for h, part in enumerate((front, pltpu.roll(front, HEAD, 1), back)):
+                    q_own[u * 2 + v, :, h * LANES : (h + 1) * LANES] = jnp.where(
+                        lower_rows, part, 0.0
+                    ).astype(low_type)
             mine = kv_all.at[:, me.c, v, me.p, me.y]
             kv_first.append(
                 [copies.push(kv_own.at[v], mine, me.at(x=x, y=y)) for x, y in square]
@@ -1512,6 +1525,12 @@
         for h, half in enumerate(halves):
             xs[h, mine] = early[half].astype(low_type)
             early_go.append(send_rows(xs, h))
+            if h == 0:
+                for copy in early_go[0]:
+                    copy.wait_send()
+                copies.started = [
+                    item for item in copies.started if all(item is not copy for copy in early_go[0])
+                ]
         loads[1].wait()
 
         def outer_weight():
@@ -1761,7 +1780,7 @@
         lengths_ref, q_ref, kv_ref, do_ref, mixed_ref, lse_ref, tok, w_ref, s1, s2, sm,
         dx_out, outqk, out1, out2, outm,
         send, recv, local, dx_send, dx_recv, swap_send, swap_recv, ks, kr, ps, pr,
-        both, kbuf, kin, pk, dqs, grads, narrow, dxs, gk, sk, pp, fk, p1, f1, pm, fm, tm, p2, early,
+        both, kbuf, kin, pk, dqs, narrow, dxs, gk, sk, pp, fk, p1, f1, pm, fm, tm, p2, early,
     ):
         me = Spot()
         copies = Copies(send, recv, local)
@@ -1933,10 +1952,6 @@
             v = (me.half + dv) % 2
             slot = u * 2 + v
             wides = [dqs[slot, :, span] * 0.125 for span in spans]
-            for h, span in enumerate(spans):
-                grads[slot, :, WIDE + span.start : WIDE + span.stop] = jnp.where(
-                    upper, 0.0, wides[h]
-                ).astype(low_type)
             narrow[slot, :, WIDE : WIDE + LANES] = jnp.where(
                 upper, pltpu.roll(wides[1], HEAD, 1), wides[0]
             ).astype(low_type)
@@ -1946,10 +1961,9 @@
             here = total_of(
                 kbuf[1, turn, me.p, me.y], *[pk[turn, peer] for peer in range(3)]
             ).astype(low_type)
-            grads[slot, :, :WIDE] = here
             narrow[slot, :, :WIDE] = here
             dxs[slot] = lax.dot_general(
-                grads[slot], w_ref[:, : 2 * WIDE], NEXT, preferred_element_type=wide
+                narrow[slot], w_ref[:, :width], NEXT, preferred_element_type=wide
             ).astype(low_type)
             copy = pltpu.make_async_remote_copy(
                 src_ref=dxs.at[slot],
@@ -2078,7 +2092,6 @@
             vmem((4, 2, 2, n, WIDE), low_type),
             vmem((4, 3, n, WIDE), low_type),
             vmem((GROUPS, n, WIDE), wide),
-            vmem((GROUPS, n, 2 * WIDE), low_type),
             vmem((GROUPS, n, width), low_type),
             vmem((GROUPS, n, depth), low_type),
             vmem((2, 2, GROUPS, 2, rows, width), low_type),

time: 188 us -> 185 us (0.984)
  Pallas kernels: 186 us -> 184 us
    pallas_call x1, Pallas kernels: 63.8 us -> 61 us  [middle_kernel(): pl.pallas_call(body, name='middle_kernel', out_shape=(jax.ShapeDtypeStruc...]
    pallas_call x1, Pallas kernels: 61.7 us -> 64.1 us  [turn_kernel(): pl.pallas_call(body, name='turn_kernel', out_shape=(jax.ShapeDtypeStruct(...]
where the time goes in v9:
time: 185 us
  Pallas kernels  184 us (99%)
    pallas_call x1, Pallas kernels, turn_kernel(): pl.pallas_call(body, name='turn_kernel', out_shape=(jax.ShapeDtypeStruct(...  64.1 us
    pallas_call x1, Pallas kernels, middle_kernel(): pl.pallas_call(body, name='middle_kernel', out_shape=(jax.ShapeDtypeStruc...  61 us
    pallas_call x1, Pallas kernels, first_kernel(): pl.pallas_call(body, name='first_kernel', out_shape=(jax.ShapeDtypeStruct...  58 us

profile of v9, /device:TPU:0, one launch (start us, length us, event | category | flops | bytes accessed | tf_op | source)
XLA Modules:
  0.0 185.2 jit_solution(6023992096619604220)
XLA Ops:
  0.7 58.0 %first_kernel.1 = (bf16[4,128,768]{2,1,0:T(8,128)(2,1)S(1)}, bf16[4,128,384]{2,1,0:T(8,128)(2,1)S(1)}, bf16[4,4,2,24,768]{4,3,2,1,0:T(8,128)(2,1)}, f32[16,768]{...) custom-call(s32[16]{0:T(128)} %lengths_ref.1, ...), custom_call_target="tpu_custom_call" | custom-call | tf_op jit(solution)/shard_map/first_kernel/pallas_call | solution.py:1227
  58.7 0.0 copy-start
  58.7 61.0 %middle_kernel.1 = (bf16[128,768]{1,0:T(8,128)(2,1)S(1)}, f32[128,768]{1,0:T(8,128)S(1)}, bf16[4,128,256]{2,1,0:T(8,128)(2,1)S(1)}, bf16[2,4,2,32,768]{4,3,2,1,0...) custom-call(bf16[4,128,256]{2,1,0:T(8,128)(2,1)S(1)} %get-tuple-element.55.mixed_ref, ...), custom_call_target="tpu_custom_call" | custom-call | tf_op jit(solution)/shard_map/middle_kernel/pallas_call | solution.py:1699
  119.7 0.0 copy-done
  119.7 64.1 %turn_kernel.1 = (bf16[4,128,768]{2,1,0:T(8,128)(2,1)S(1)}, bf16[4,32,640]{2,1,0:T(8,128)(2,1)S(1)}, bf16[4,32,768]{2,1,0:T(8,128)(2,1)S(1)}, f32[96,768]{1,0:T(8,128)S(1)}, f32[32,768]{1,0:T(8,128)S(1)}) custom-call(s32[16]{0:T(128)S(1)} %copy-done, bf16[512,384]{1,0:T(8,128)(2,1)S(1)} %bitcast.26, bf16[4096,384]{1,0:T(8,128)(2,1)} %bitcast.28, ...), custom_call_target="tpu_custom_call" | custom-call | tf_op jit(solution)/shard_map/turn_kernel/pallas_call | solution.py:2075
  183.8 1.2 final_kernel.1
Async XLA Ops:
  58.7 61.0 %copy-start = (s32[16]{0:T(128)S(1)}, s32[16]{0:T(128)}, u32[]{:S(2)}) copy-start(s32[16]{0:T(128)} %lengths_ref.1) | copy-start | bytes 196

commit v10 on v9

--- a/solution.py
+++ b/solution.py
@@ -862,7 +862,7 @@
         self.crossing = self.c != self.y
 
     def square(self):
-        return [(to[0], to[2]) for to, _ in self.plane()]
+        return [(to[0], to[2]) for to, _ in reversed(self.plane())]
 
     def readers(self):
         result = []

time: 185 us -> 185 us (level)
  no operation moved by 1% of the time
where the time goes in v10:
time: 185 us; the launch traced here: 184 us
  Pallas kernels  184 us (99%)
    pallas_call x1, Pallas kernels, turn_kernel(): pl.pallas_call(body, name='turn_kernel', out_shape=(jax.ShapeDtypeStruct(...  63.4 us
    pallas_call x1, Pallas kernels, middle_kernel(): pl.pallas_call(body, name='middle_kernel', out_shape=(jax.ShapeDtypeStruc...  61.5 us
    pallas_call x1, Pallas kernels, first_kernel(): pl.pallas_call(body, name='first_kernel', out_shape=(jax.ShapeDtypeStruct...  57.4 us

profile of v10, /device:TPU:0, one launch (start us, length us, event | category | flops | bytes accessed | tf_op | source)
XLA Modules:
  0.0 184.4 jit_solution(18189493920454236060)
XLA Ops:
  0.7 57.4 %first_kernel.1 = (bf16[4,128,768]{2,1,0:T(8,128)(2,1)S(1)}, bf16[4,128,384]{2,1,0:T(8,128)(2,1)S(1)}, bf16[4,4,2,24,768]{4,3,2,1,0:T(8,128)(2,1)}, f32[16,768]{...) custom-call(s32[16]{0:T(128)} %lengths_ref.1, ...), custom_call_target="tpu_custom_call" | custom-call | tf_op jit(solution)/shard_map/first_kernel/pallas_call | solution.py:1227
  58.0 0.0 copy-start
  58.0 61.5 %middle_kernel.1 = (bf16[128,768]{1,0:T(8,128)(2,1)S(1)}, f32[128,768]{1,0:T(8,128)S(1)}, bf16[4,128,256]{2,1,0:T(8,128)(2,1)S(1)}, bf16[2,4,2,32,768]{4,3,2,1,0...) custom-call(bf16[4,128,256]{2,1,0:T(8,128)(2,1)S(1)} %get-tuple-element.55.mixed_ref, ...), custom_call_target="tpu_custom_call" | custom-call | tf_op jit(solution)/shard_map/middle_kernel/pallas_call | solution.py:1699
  119.6 0.0 copy-done
  119.6 63.4 %turn_kernel.1 = (bf16[4,128,768]{2,1,0:T(8,128)(2,1)S(1)}, bf16[4,32,640]{2,1,0:T(8,128)(2,1)S(1)}, bf16[4,32,768]{2,1,0:T(8,128)(2,1)S(1)}, f32[96,768]{1,0:T(8,128)S(1)}, f32[32,768]{1,0:T(8,128)S(1)}) custom-call(s32[16]{0:T(128)S(1)} %copy-done, bf16[512,384]{1,0:T(8,128)(2,1)S(1)} %bitcast.26, bf16[4096,384]{1,0:T(8,128)(2,1)} %bitcast.28, ...), custom_call_target="tpu_custom_call" | custom-call | tf_op jit(solution)/shard_map/turn_kernel/pallas_call | solution.py:2075
  183.0 1.2 final_kernel.1
Async XLA Ops:
  58.0 61.5 %copy-start = (s32[16]{0:T(128)S(1)}, s32[16]{0:T(128)}, u32[]{:S(2)}) copy-start(s32[16]{0:T(128)} %lengths_ref.1) | copy-start | bytes 196

commit v11 on v10

--- a/solution.py
+++ b/solution.py
@@ -22,8 +22,8 @@
 wide = jnp.float32
 MESH = pl.DeviceIdType.MESH
 VMEM_LIMIT = 62 * 1024 * 1024
-NEAR_LIMIT = 30 * 1024 * 1024
-TURN_LIMIT = 48 * 1024 * 1024
+NEAR_LIMIT = 36 * 1024 * 1024
+TURN_LIMIT = 40 * 1024 * 1024
 
 
 def layer_norm(hidden, gain, shift):
@@ -1948,6 +1948,22 @@
             if turn == 3:
                 for half in range(2):
                     early[half] = weight_grad(slots[:3], half)
+                for copy in wm_push:
+                    copy.wait_recv()
+                square_sum(fm, sm, pm)
+                wm_last = [
+                    copies.push(fm.at[to], tm.at[peer], me.at(g=to)) for peer, to in enumerate(line)
+                ]
+                for copy in w1_push:
+                    copy.wait_recv()
+
+                def addw(index):
+                    x, y = index // 2, index % 2
+                    f1[x, y] = total_of(s1[x, me.g, y], *[p1[peer, x, y] for peer in range(3)]).astype(
+                        low_type
+                    )
+
+                loop(4, addw)
             u, dv = turn % 2, turn // 2
             v = (me.half + dv) % 2
             slot = u * 2 + v
@@ -2000,22 +2016,6 @@
                 gk[(*place, slice(s, None))] = bias
         g_half = copies.push(gk.at[:, other], sk, me.sibling())
 
-        for copy in wm_push:
-            copy.wait_recv()
-        square_sum(fm, sm, pm)
-        wm_last = [
-            copies.push(fm.at[to], tm.at[peer], me.at(g=to)) for peer, to in enumerate(line)
-        ]
-        for copy in w1_push:
-            copy.wait_recv()
-
-        def addw(index):
-            x, y = index // 2, index % 2
-            f1[x, y] = total_of(s1[x, me.g, y], *[p1[peer, x, y] for peer in range(3)]).astype(
-                low_type
-            )
-
-        loop(4, addw)
         quarter = out1.at[me.x * 2 + me.y]
         g_half.wait_recv()
 

time: 185 us -> 184 us (level)
  Pallas kernels: 184 us -> 182 us
    pallas_call x1, Pallas kernels: 63.4 us -> 61.5 us  [turn_kernel(): pl.pallas_call(body, name='turn_kernel', out_shape=(jax.ShapeDtypeStruct(...]
where the time goes in v11:
time: 184 us
  Pallas kernels  182 us (99%)
    pallas_call x1, Pallas kernels, turn_kernel(): pl.pallas_call(body, name='turn_kernel', out_shape=(jax.ShapeDtypeStruct(...  61.5 us
    pallas_call x1, Pallas kernels, middle_kernel(): pl.pallas_call(body, name='middle_kernel', out_shape=(jax.ShapeDtypeStruc...  61.5 us
    pallas_call x1, Pallas kernels, first_kernel(): pl.pallas_call(body, name='first_kernel', out_shape=(jax.ShapeDtypeStruct...  57.4 us

profile of v11, /device:TPU:0, one launch (start us, length us, event | category | flops | bytes accessed | tf_op | source)
XLA Modules:
  0.0 183.9 jit_solution(13291933157384140464)
XLA Ops:
  0.7 57.4 %first_kernel.1 = (bf16[4,128,768]{2,1,0:T(8,128)(2,1)S(1)}, bf16[4,128,384]{2,1,0:T(8,128)(2,1)S(1)}, bf16[4,4,2,24,768]{4,3,2,1,0:T(8,128)(2,1)}, f32[16,768]{...) custom-call(s32[16]{0:T(128)} %lengths_ref.1, ...), custom_call_target="tpu_custom_call" | custom-call | tf_op jit(solution)/shard_map/first_kernel/pallas_call | solution.py:1227
  58.0 0.0 copy-start
  58.0 0.0 copy-start.2
  58.1 61.5 %middle_kernel.1 = (bf16[128,768]{1,0:T(8,128)(2,1)S(1)}, f32[128,768]{1,0:T(8,128)S(1)}, bf16[4,128,256]{2,1,0:T(8,128)(2,1)S(1)}, bf16[2,4,2,32,768]{4,3,2,1,0...) custom-call(bf16[4,128,256]{2,1,0:T(8,128)(2,1)S(1)} %get-tuple-element.55.mixed_ref, ...), custom_call_target="tpu_custom_call" | custom-call | tf_op jit(solution)/shard_map/middle_kernel/pallas_call | solution.py:1699
  119.6 0.0 copy-done
  119.6 0.0 copy-done.2
  119.6 0.0 copy-start.1
  119.6 1.3 copy-done.1
  120.9 61.5 %turn_kernel.1 = (bf16[4,128,768]{2,1,0:T(8,128)(2,1)S(1)}, bf16[4,32,640]{2,1,0:T(8,128)(2,1)S(1)}, bf16[4,32,768]{2,1,0:T(8,128)(2,1)S(1)}, f32[96,768]{1,0:T(8,128)S(1)}, f32[32,768]{1,0:T(8,128)S(1)}) custom-call(s32[16]{0:T(128)S(1)} %copy-done.2, bf16[512,384]{1,0:T(8,128)(2,1)S(1)} %bitcast.28, bf16[4096,384]{1,0:T(8,128)(2,1)S(1)} %bitcast.24, ...), custom_call_target="tpu_custom_call" | custom-call | tf_op jit(solution)/shard_map/turn_kernel/pallas_call | solution.py:2075
  182.4 1.2 final_kernel.1
Async XLA Ops:
  58.0 61.6 %copy-start = (bf16[2,2,2,2,2,128,384]{6,5,4,3,2,1,0:T(8,128)(2,1)S(1)}, bf16[2,2,2,2,2,128,384]{6,5,4,3,2,1,0:T(8,128)(2,1)}, u32[]{:S(2)}) copy-start(bf16[2,2,2,2,2,128,384]{6,5,4,3,2,1,0:T(8,128)(2,1)} %get-tuple-element.62) | copy-start | bytes 9437188
  58.0 61.6 %copy-start.2 = (s32[16]{0:T(128)S(1)}, s32[16]{0:T(128)}, u32[]{:S(2)}) copy-start(s32[16]{0:T(128)} %lengths_ref.1) | copy-start | bytes 196
  119.6 1.3 copy-start.1
